TPU v7x, 256 devices: a whole 4x4x8 slice. The times are simulated.
256 devices in a mesh: seq: 32 (over x, y, core), head: 8 (over z).
Axes of the slice: x: 4, y: 4, z: 8, core: 2. Of those that a mesh axis runs over, the one named last changes fastest.
Arguments:
- queries: bfloat16 [32768, 64, 128], P(('seq', 'head')), may hold values from -8 to 8
- keys: bfloat16 [32768, 8, 128], P(('seq', 'head')), may hold values from -8 to 8
- values: bfloat16 [32768, 8, 128], P(('seq', 'head')), may hold values from -6 to 6
- ancestors: int32 [256, 8], P('seq'), may hold values from 0 to 255, as said below
- lengths: int32 [256], replicated, may hold values from 2 to 128
Outputs:
- attended: bfloat16 [32768, 64, 128], P(('seq', 'head'))
Inputs may be any that keep to these rules, and one draw needn't show every extreme that they name: The 8 ancestors of a block are distinct blocks held on other indices of seq; the blocks of one index of seq name, all together, exactly 2 distinct blocks of each of 6 other indices and no other block.
All inputs are finite; a program needn't handle non-finite values.
Results may differ from a plain program's by a relative error of at most 0.0049.
Values may be sent and summed in bfloat16 or wider, within the bound.
No kernel may reach another device: no remote copies, remote signals or barrier semaphores. Data moves between devices by JAX's collectives and lax.ppermute only.
A program may use at most 64 MiB of HBM per device.

v0:
```python
import functools
import math

import jax
import jax.numpy as jnp
from jax import lax
from jax.experimental import pallas as pl
from jax.experimental.pallas import tpu as pltpu
from jax.sharding import PartitionSpec as P


BS = 128
POOL = 12
HALF = POOL // 2
TILE = 8
NEG = -1e30


def pool_of(ancestors):
    flat = ancestors.reshape(-1)
    n = flat.shape[0]
    order = jnp.arange(n, dtype=jnp.int32)
    same = flat[:, None] == flat[None, :]
    repeat = jnp.any(same & (order[None, :] < order[:, None]), axis=1)
    first = ~repeat
    rank = jnp.sum((first[None, :] & (flat[None, :] < flat[:, None])).astype(jnp.int32), axis=1)
    slots = jnp.arange(BS, dtype=jnp.int32)
    hit = first[:, None] & (rank[:, None] == slots[None, :])
    pool = jnp.sum(jnp.where(hit, flat[:, None], 0), axis=0)
    return pool, rank.reshape(ancestors.shape)


def pick_kernel(pools, held, low, high):
    def one(s, carry):
        for i in range(HALF):
            low[s, i] = held[pools[s, i]]
            high[s, i] = held[pools[s, HALF + i]]
        return carry

    lax.fori_loop(0, pools.shape[0], one, 0, unroll=4)


def pick(pools, held):
    groups = pools.shape[0]
    part = jax.ShapeDtypeStruct((groups, HALF, TILE, BS), held.dtype)
    whole = pl.BlockSpec(memory_space=pltpu.VMEM)
    return pl.pallas_call(
        pick_kernel,
        out_shape=(part, part),
        grid_spec=pltpu.PrefetchScalarGridSpec(
            num_scalar_prefetch=1, grid=(1,),
            in_specs=[pl.BlockSpec(held.shape, lambda i, _: (0, 0, 0))],
            out_specs=[pl.BlockSpec(part.shape, lambda i, _: (0, 0, 0, 0))] * 2,
        ),
        name="pick",
    )(pools, held)


def attend_kernel(scale, meta, q, own, low, high, _, out, keys, vals, acc):
    far = 8
    row = lax.broadcasted_iota(jnp.int32, (BS, BS), 0)

    def put(j, k, v, length):
        k = k.astype(jnp.float32).reshape(BS, BS)
        v = v.astype(jnp.float32).reshape(BS, BS)
        valid = row < length
        at = slice(j * BS, (j + 1) * BS)
        keys[at, :] = jnp.where(valid, k, k[0:1, :]).astype(jnp.bfloat16)
        vals[at, 0:BS] = jnp.where(valid, v, 0.0).astype(jnp.bfloat16)
        vals[at, BS:] = jnp.where(valid, 1.0, 0.0).astype(jnp.bfloat16)

    put(0, own[0:16, 0], own[16:32, 0], meta[17])
    for j in range(far):
        place, length = meta[1 + j], meta[9 + j]

        @pl.when(place < HALF)
        def _():
            put(j + 1, low[0:16, place], low[16:32, place], length)

        @pl.when(place >= HALF)
        def _():
            put(j + 1, high[0:16, place - HALF], high[16:32, place - HALF], length)

    tokens = 32
    rows = tokens * 8
    token = lax.broadcasted_iota(jnp.int32, (rows, BS), 0) // 8
    offset = lax.broadcasted_iota(jnp.int32, (rows, BS), 1)
    for i in range(BS // tokens):
        at = slice(i * tokens, (i + 1) * tokens)
        qt = q[at].astype(jnp.float32).reshape(rows, BS).astype(jnp.bfloat16)
        s = lax.dot_general(qt, keys[...], (((1,), (1,)), ((), ())), preferred_element_type=jnp.float32)
        s_own = jnp.where(offset <= token + i * tokens, s[:, 0:BS], NEG)
        s_far = s[:, BS:]
        m = jnp.maximum(jnp.max(s_own, axis=1, keepdims=True), jnp.max(s_far, axis=1, keepdims=True))
        p_own = jnp.exp2((s_own - m) * scale).astype(jnp.bfloat16)
        p_far = jnp.exp2((s_far - m) * scale).astype(jnp.bfloat16)
        o = jnp.dot(p_own, vals[0:BS, :], preferred_element_type=jnp.float32)
        o = o + jnp.dot(p_far, vals[BS:, :], preferred_element_type=jnp.float32)
        r = o[:, 0:BS] / o[:, BS:]
        out[at] = r.reshape(tokens, 8, BS).astype(out.dtype)


def attend(meta, q, own, low, high, prev):
    scale = math.log2(math.e) / math.sqrt(BS)
    shape = jax.ShapeDtypeStruct(q.shape, q.dtype)
    body = functools.partial(attend_kernel, scale)
    part = pl.BlockSpec(low.shape, lambda i, m: (0, 0, 0, 0))
    heads = pl.BlockSpec((BS, 8, BS), lambda i, m: (0, m[0], 0))
    flops = 2 * 2 * 1024 * 1152 * 128
    return pl.pallas_call(
        body,
        out_shape=shape,
        grid_spec=pltpu.PrefetchScalarGridSpec(
            num_scalar_prefetch=1, grid=(1,),
            in_specs=[
                heads,
                pl.BlockSpec((32, 1, TILE, BS), lambda i, m: (0, m[0], 0, 0)),
                part, part,
                pl.BlockSpec(memory_space=pl.ANY),
            ],
            out_specs=heads,
            scratch_shapes=[
                pltpu.VMEM((9 * BS, BS), jnp.bfloat16),
                pltpu.VMEM((9 * BS, 2 * BS), jnp.bfloat16),
                pltpu.VMEM((8, BS), jnp.float32),
            ],
        ),
        input_output_aliases={5: 0},
        cost_estimate=pl.CostEstimate(flops=flops, bytes_accessed=2 << 20, transcendentals=1024 * 1152),
        name="attend",
    )(meta, q, own, low, high, prev)


def blank_kernel(out):
    pass


def blank(like):
    return pl.pallas_call(
        blank_kernel,
        out_shape=jax.ShapeDtypeStruct(like.shape, like.dtype),
        out_specs=pl.BlockSpec(memory_space=pl.ANY),
        name="blank",
    )()


def local(n_head, queries, keys, values, ancestors, lengths):
    return attention(n_head, queries, keys, values, ancestors, lengths)


def attention(n_head, queries, keys, values, ancestors, lengths):
    n_seq = 32
    place, level = lax.axis_index("seq"), lax.axis_index("head")
    pool, rank = pool_of(ancestors)
    pools = lax.all_to_all(jnp.broadcast_to(pool[None, None], (n_seq, 1, BS)), "seq", 0, 0, tiled=True)
    pools = jnp.minimum(pools.reshape(n_seq, BS), n_seq * n_head - 1)

    named = lax.dynamic_slice_in_dim(ancestors, level, 1)[0]
    ranks = lax.dynamic_slice_in_dim(rank, level, 1)[0]
    far_len = jnp.take(lengths, named)
    own_len = lax.dynamic_slice_in_dim(lengths, place * n_head + level, 1)

    def meta_of(g):
        return jnp.concatenate([g.astype(jnp.int32).reshape(1), ranks, far_len, own_len])

    own = jnp.concatenate([keys, values], axis=0).reshape(32, TILE, n_head, BS).transpose(0, 2, 1, 3)
    held = lax.all_to_all(own.reshape(n_seq * n_head, TILE, BS), ("seq", "head"), 0, 0, tiled=True)
    low, high = pick(pools, held)
    low = lax.all_to_all(low, "seq", 0, 0, tiled=True)
    high = lax.all_to_all(high, "seq", 0, 0, tiled=True)

    up = [(i, (i + 1) % n_head) for i in range(n_head)]
    down = [(i, (i - 1) % n_head) for i in range(n_head)]
    out = blank(queries)
    out = attend(meta_of(level), queries, own, low, high, out)
    low_up = low_down = low
    high_up = high_down = high
    for step in range(1, n_head // 2 + 1):
        last = step == n_head // 2
        low_up = lax.ppermute(low_up, "head", up)
        high_down = lax.ppermute(high_down, "head", down)
        if last:
            out = attend(meta_of(lax.rem(level + step, n_head)), queries, own, low_up, high_down, out)
            break
        high_up = lax.ppermute(high_up, "head", up)
        low_down = lax.ppermute(low_down, "head", down)
        out = attend(meta_of(lax.rem(level + n_head - step, n_head)), queries, own, low_up, high_up, out)
        out = attend(meta_of(lax.rem(level + step, n_head)), queries, own, low_down, high_down, out)
    return out


def solution(mesh):
    placed = (
        P(("seq", "head"), None, None),
        P(("seq", "head"), None, None),
        P(("seq", "head"), None, None),
        P("seq", None),
        P(),
    )
    body = functools.partial(local, mesh.shape["head"])
    return jax.shard_map(
        body, mesh=mesh, in_specs=placed, out_specs=P(("seq", "head"), None, None), check_vma=False
    )
```

profile of v0, /device:TPU:1, one launch (start us, length us, event | category | flops | bytes accessed | tf_op | source)
XLA Modules:
  0.0 166.7 jit_solution(7486768348908640324)
XLA Ops:
  0.0 0.8 eq.28
  0.8 0.2 fusion.1
  1.0 0.2 convert_reduce_fusion
  1.1 0.1 select_reduce_fusion
  1.3 0.6 broadcast_in_dim.17
  1.9 8.6 %all-to-all-start = ((s32[32,1,128]{2,1,0:T(1,128)}), s32[32,1,128]{2,1,0:T(1,128)S(1)}, u32[]{:S(2)}, u32[]{:S(2)}) async-start(s32[32,1,128]{2,1,0:T(1,128)} %broadcast_in_dim.17), calls=%async_computation | async-start | bytes 32768 | tf_op jit(solution)/shard_map/all_to_all | solution.py:155
  10.5 1.1 pad_maximum_fusion
  11.6 0.0 copy-start
  11.6 0.9 copy.21
  12.5 4.9 %all-to-all-done = s32[32,1,128]{2,1,0:T(1,128)S(1)} async-done(((s32[32,1,128]{2,1,0:T(1,128)}), s32[32,1,128]{2,1,0:T(1,128)S(1)}, u32[]{:S(2)}, u32[]{:S(2)}) %all-to-all-start) | async-done | bytes 16416 | tf_op jit(solution)/shard_map/all_to_all | solution.py:155
  17.4 11.0 %all-to-all-start.1 = ((bf16[256,8,128]{2,1,0:T(8,128)(2,1)}), bf16[256,8,128]{2,1,0:T(8,128)(2,1)S(1)}, u32[]{:S(2)}, u32[]{:S(2)}) async-start(bf16[256,8,128]{2,1,0:T(8,128)(2,1)} %bitcast.9), calls=%async_computation.1 | async-start | bytes 1048576 | tf_op jit(solution)/shard_map/all_to_all | solution.py:167
  28.4 0.6 minimum_bitcast_fusion.pools
  29.0 20.5 %all-to-all-done.1.held = bf16[256,8,128]{2,1,0:T(8,128)(2,1)S(1)} async-done(((bf16[256,8,128]{2,1,0:T(8,128)(2,1)}), bf16[256,8,128]{2,1,0:T(8,128)(2,1)S(1)}, u32[]{:S(2)}, u32[]{:S(2)}) %all-to-all-start.1) | async-done | bytes 524320 | tf_op jit(solution)/shard_map/all_to_all | solution.py:167
  49.5 0.8 copy-done.1
  50.3 3.3 %pick.1 = (bf16[32,6,8,128]{3,2,1,0:T(8,128)(2,1)}, bf16[32,6,8,128]{3,2,1,0:T(8,128)(2,1)}) custom-call(s32[32,128]{1,0:T(8,128)} %minimum_bitcast_fusion.pools, bf16[256,8,128]{2,1,0:T(8,128)(2,1)} %copy-done.1), custom_call_target="tpu_custom_call" | custom-call | tf_op jit(solution)/shard_map/pick/pallas_call | solution.py:47
  53.5 14.7 %all_to_all.20.low = bf16[32,6,8,128]{3,2,1,0:T(8,128)(2,1)S(1)} all-to-all(bf16[32,6,8,128]{3,2,1,0:T(8,128)(2,1)} %get-tuple-element.7), channel_id=1, replica_groups=mesh['seq'=32,'head'=8] {'seq'}, dimensions={0} | all-to-all | bytes 786432 | tf_op jit(solution)/shard_map/all_to_all | solution.py:169
  68.2 3.7 %all-to-all-start.3 = ((bf16[32,6,8,128]{3,2,1,0:T(8,128)(2,1)}), bf16[32,6,8,128]{3,2,1,0:T(8,128)(2,1)S(1)}, u32[]{:S(2)}, u32[]{:S(2)}) async-start(bf16[32,6,8,128]{3,2,1,0:T(8,128)(2,1)} %get-tuple-element.8), calls=%async_computation.3 | async-start | bytes 786432 | tf_op jit(solution)/shard_map/all_to_all | solution.py:170
  71.9 0.8 collective-permute-start
  72.7 9.4 %all-to-all-done.3.high = bf16[32,6,8,128]{3,2,1,0:T(8,128)(2,1)S(1)} async-done(((bf16[32,6,8,128]{3,2,1,0:T(8,128)(2,1)}), bf16[32,6,8,128]{3,2,1,0:T(8,128)(2,1)S(1)}, u32[]{:S(2)}, u32[]{:S(2)}) %all-to-all-start.3) | async-done | bytes 393248 | tf_op jit(solution)/shard_map/all_to_all | solution.py:170
  82.1 0.0 collective-permute-start.4
  82.1 1.5 collective-permute-start.11
  83.6 1.2 collective-permute-start.8
  84.8 0.7 fusion.3
  85.5 0.0 collective-permute-done.low
  85.5 0.3 collective-permute-start.1
  85.8 7.0 %collective-permute-done.4.high = bf16[32,6,8,128]{3,2,1,0:T(8,128)(2,1)S(1)} collective-permute-done((bf16[32,6,8,128]{3,2,1,0:T(8,128)(2,1)S(1)}, bf16[32,6,8,128]{3,2,1,0:T(8,128)(2,1)S(1)}, u32[]{:S(2)}, u32[]{:S(2)}) %collective-permute-start.4) | collective-permute-done | bytes 393248 | tf_op jit(solution)/shard_map/ppermute | solution.py:181
  92.8 1.5 collective-permute-start.5
  94.3 0.1 reshape.83
  94.4 0.0 copy-done
  94.4 0.6 gather_fusion
  95.1 0.6 dynamic_slice.11
  95.7 0.7 and_select_fusion
  96.4 0.0 collective-permute-done.11.high
  96.4 0.1 collective-permute-start.12
  96.5 4.8 %collective-permute-done.8.low = bf16[32,6,8,128]{3,2,1,0:T(8,128)(2,1)S(1)} collective-permute-done((bf16[32,6,8,128]{3,2,1,0:T(8,128)(2,1)S(1)}, bf16[32,6,8,128]{3,2,1,0:T(8,128)(2,1)S(1)}, u32[]{:S(2)}, u32[]{:S(2)}) %collective-permute-start.8) | collective-permute-done | bytes 393248 | tf_op jit(solution)/shard_map/ppermute | solution.py:186
  101.3 1.5 collective-permute-start.9
  102.8 0.0 collective-permute-done.1.low
  102.8 0.1 collective-permute-start.2
  102.9 6.9 %collective-permute-done.5.high = bf16[32,6,8,128]{3,2,1,0:T(8,128)(2,1)S(1)} collective-permute-done((bf16[32,6,8,128]{3,2,1,0:T(8,128)(2,1)S(1)}, bf16[32,6,8,128]{3,2,1,0:T(8,128)(2,1)S(1)}, u32[]{:S(2)}, u32[]{:S(2)}) %collective-permute-start.5) | collective-permute-done | bytes 393248 | tf_op jit(solution)/shard_map/ppermute | solution.py:181
  109.8 1.4 collective-permute-start.6
  111.2 1.3 add_add_fusion.7
  112.5 1.3 add_add_fusion.6
  113.8 1.2 add_add_fusion.5
  115.0 0.0 collective-permute-done.12.high
  115.0 0.1 collective-permute-start.13
  115.1 3.1 %collective-permute-done.9.low = bf16[32,6,8,128]{3,2,1,0:T(8,128)(2,1)S(1)} collective-permute-done((bf16[32,6,8,128]{3,2,1,0:T(8,128)(2,1)S(1)}, bf16[32,6,8,128]{3,2,1,0:T(8,128)(2,1)S(1)}, u32[]{:S(2)}, u32[]{:S(2)}) %collective-permute-start.9) | collective-permute-done | bytes 393248 | tf_op jit(solution)/shard_map/ppermute | solution.py:186
  118.2 1.4 collective-permute-start.10
  119.6 1.3 add_add_fusion.4
  120.9 0.0 collective-permute-done.2.low
  120.9 0.1 collective-permute-start.3
  121.0 5.7 %collective-permute-done.6.high = bf16[32,6,8,128]{3,2,1,0:T(8,128)(2,1)} collective-permute-done((bf16[32,6,8,128]{3,2,1,0:T(8,128)(2,1)S(1)}, bf16[32,6,8,128]{3,2,1,0:T(8,128)(2,1)}, u32[]{:S(2)}, u32[]{:S(2)}) %collective-permute-start.6) | collective-permute-done | bytes 393248 | tf_op jit(solution)/shard_map/ppermute | solution.py:181
  126.6 1.5 collective-permute-start.7
  128.1 4.8 %attend.8._ = bf16[128,64,128]{2,1,0:T(8,128)(2,1)} custom-call(s32[18]{0:T(128)} %get-tuple-element.11.meta, bf16[128,64,128]{2,1,0:T(8,128)(2,1)} %q.15, bf16[32,8,8,128]{3,2,1,0:T(8,128)(2,1)} %bitcast.23.clone.2.own, bf16[32,6,8,128]{3,2,1,0:T(8,128)(2,1)} %copy-done.2, bf16[32,6,8,128]{3,2,1,0:T(8,128)(2,1)} %copy-done.3, ...), custom_call_target="tpu_custom_call", output_to_operand_aliasing={{}: (5, {})} | custom-call | flops 603979776 | bytes 2097152 | tf_op jit(solution)/shard_map/attend/pallas_call | solution.py:110
  133.0 4.8 %attend.9._ = bf16[128,64,128]{2,1,0:T(8,128)(2,1)} custom-call(s32[18]{0:T(128)} %get-tuple-element.13.meta, bf16[128,64,128]{2,1,0:T(8,128)(2,1)} %q.15, bf16[32,8,8,128]{3,2,1,0:T(8,128)(2,1)} %bitcast.23.clone.2.own, bf16[32,6,8,128]{3,2,1,0:T(8,128)(2,1)} %copy-done.4, bf16[32,6,8,128]{3,2,1,0:T(8,128)(2,1)} %copy-done.7, ...), custom_call_target="tpu_custom_call", output_to_operand_aliasing={{}: (5, {})} | custom-call | flops 603979776 | bytes 2097152 | tf_op jit(solution)/shard_map/attend/pallas_call | solution.py:110
  137.8 4.8 %attend.10._ = bf16[128,64,128]{2,1,0:T(8,128)(2,1)} custom-call(s32[18]{0:T(128)} %get-tuple-element.15.meta, bf16[128,64,128]{2,1,0:T(8,128)(2,1)} %q.15, bf16[32,8,8,128]{3,2,1,0:T(8,128)(2,1)} %bitcast.23.clone.2.own, bf16[32,6,8,128]{3,2,1,0:T(8,128)(2,1)} %copy-done.6, bf16[32,6,8,128]{3,2,1,0:T(8,128)(2,1)} %copy-done.5, ...), custom_call_target="tpu_custom_call", output_to_operand_aliasing={{}: (5, {})} | custom-call | flops 603979776 | bytes 2097152 | tf_op jit(solution)/shard_map/attend/pallas_call | solution.py:110
  142.6 4.8 %attend.11._ = bf16[128,64,128]{2,1,0:T(8,128)(2,1)} custom-call(s32[18]{0:T(128)} %get-tuple-element.17.meta, bf16[128,64,128]{2,1,0:T(8,128)(2,1)} %q.15, bf16[32,8,8,128]{3,2,1,0:T(8,128)(2,1)} %bitcast.23.clone.2.own, bf16[32,6,8,128]{3,2,1,0:T(8,128)(2,1)} %copy-done.8, ...), custom_call_target="tpu_custom_call", output_to_operand_aliasing={{}: (5, {})} | custom-call | flops 603979776 | bytes 2097152 | tf_op jit(solution)/shard_map/attend/pallas_call | solution.py:110
  147.3 5.0 %attend.12._ = bf16[128,64,128]{2,1,0:T(8,128)(2,1)} custom-call(s32[18]{0:T(128)} %get-tuple-element.16.meta, bf16[128,64,128]{2,1,0:T(8,128)(2,1)} %q.15, bf16[32,8,8,128]{3,2,1,0:T(8,128)(2,1)} %bitcast.23.clone.2.own, bf16[32,6,8,128]{3,2,1,0:T(8,128)(2,1)} %copy-done.10, bf16[32,6,8,128]{3,2,1,0:T(8,128)(2,1)} %copy-done.9, ...), custom_call_target="tpu_custom_call", output_to_operand_aliasing={{}: (5, {})} | custom-call | flops 603979776 | bytes 2097152 | tf_op jit(solution)/shard_map/attend/pallas_call | solution.py:110
  152.3 0.0 collective-permute-done.13.high
  152.4 4.8 %attend.13._ = bf16[128,64,128]{2,1,0:T(8,128)(2,1)} custom-call(s32[18]{0:T(128)} %get-tuple-element.14.meta, bf16[128,64,128]{2,1,0:T(8,128)(2,1)} %q.15, bf16[32,8,8,128]{3,2,1,0:T(8,128)(2,1)} %bitcast.23.clone.2.own, bf16[32,6,8,128]{3,2,1,0:T(8,128)(2,1)} %collective-permute-done.2.low, ...), custom_call_target="tpu_custom_call", output_to_operand_aliasing={{}: (5, {})} | custom-call | flops 603979776 | bytes 2097152 | tf_op jit(solution)/shard_map/attend/pallas_call | solution.py:110
  157.1 0.0 collective-permute-done.10.low
  157.1 4.8 %attend.14._ = bf16[128,64,128]{2,1,0:T(8,128)(2,1)} custom-call(s32[18]{0:T(128)} %get-tuple-element.12.meta, bf16[128,64,128]{2,1,0:T(8,128)(2,1)} %q.15, bf16[32,8,8,128]{3,2,1,0:T(8,128)(2,1)} %bitcast.23.clone.2.own, bf16[32,6,8,128]{3,2,1,0:T(8,128)(2,1)} %collective-permute-done.10.low, ...), custom_call_target="tpu_custom_call", output_to_operand_aliasing={{}: (5, {})} | custom-call | flops 603979776 | bytes 2097152 | tf_op jit(solution)/shard_map/attend/pallas_call | solution.py:110
  161.9 0.0 collective-permute-done.3.low
  161.9 0.0 collective-permute-done.7.high
  161.9 4.8 %attend.15 = bf16[128,64,128]{2,1,0:T(8,128)(2,1)} custom-call(s32[18]{0:T(128)} %get-tuple-element.18.meta, bf16[128,64,128]{2,1,0:T(8,128)(2,1)} %q.15, bf16[32,8,8,128]{3,2,1,0:T(8,128)(2,1)} %bitcast.23.clone.2.own, bf16[32,6,8,128]{3,2,1,0:T(8,128)(2,1)} %collective-permute-done.3.low, ...), custom_call_target="tpu_custom_call", output_to_operand_aliasing={{}: (5, {})} | custom-call | flops 603979776 | bytes 2097152 | tf_op jit(solution)/shard_map/attend/pallas_call | solution.py:110
  (23 shorter events, 0.1 us)
Async XLA Ops:
  1.9 15.5 %all-to-all-start = ((s32[32,1,128]{2,1,0:T(1,128)}), s32[32,1,128]{2,1,0:T(1,128)S(1)}, u32[]{:S(2)}, u32[]{:S(2)}) async-start(s32[32,1,128]{2,1,0:T(1,128)} %broadcast_in_dim.17), calls=%async_computation | async-start | bytes 32768 | tf_op jit(solution)/shard_map/all_to_all | solution.py:155
  11.6 82.9 %copy-start = (s32[256]{0:T(256)S(1)}, s32[256]{0:T(256)}, u32[]{:S(2)}) copy-start(s32[256]{0:T(256)} %param.9) | copy-start | bytes 3076
  17.4 32.1 %all-to-all-start.1 = ((bf16[256,8,128]{2,1,0:T(8,128)(2,1)}), bf16[256,8,128]{2,1,0:T(8,128)(2,1)S(1)}, u32[]{:S(2)}, u32[]{:S(2)}) async-start(bf16[256,8,128]{2,1,0:T(8,128)(2,1)} %bitcast.9), calls=%async_computation.1 | async-start | bytes 1048576 | tf_op jit(solution)/shard_map/all_to_all | solution.py:167
  49.5 0.8 copy-start.1
  68.2 59.9 %copy-start.2 = (bf16[32,6,8,128]{3,2,1,0:T(8,128)(2,1)}, bf16[32,6,8,128]{3,2,1,0:T(8,128)(2,1)S(1)}, u32[]{:S(2)}) copy-start(bf16[32,6,8,128]{3,2,1,0:T(8,128)(2,1)S(1)} %all_to_all.20.low) | copy-start | bytes 1179652
  68.2 13.9 %all-to-all-start.3 = ((bf16[32,6,8,128]{3,2,1,0:T(8,128)(2,1)}), bf16[32,6,8,128]{3,2,1,0:T(8,128)(2,1)S(1)}, u32[]{:S(2)}, u32[]{:S(2)}) async-start(bf16[32,6,8,128]{3,2,1,0:T(8,128)(2,1)} %get-tuple-element.8), calls=%async_computation.3 | async-start | bytes 786432 | tf_op jit(solution)/shard_map/all_to_all | solution.py:170
  71.9 13.6 %collective-permute-start = (bf16[32,6,8,128]{3,2,1,0:T(8,128)(2,1)S(1)}, bf16[32,6,8,128]{3,2,1,0:T(8,128)(2,1)S(1)}, u32[]{:S(2)}, u32[]{:S(2)}) collective-permute-start(bf16[32,6,8,128]{3,2,1,0:T(8,128)(2,1)S(1)} %all_to_all.20.low), channel_id=1, source_target_pairs={{0,1},{1,2},{2,3},{3,4},{4,5},{5,6},{6,7},{7,0},{8,9},{9,10},{10,1... | collective-permute-start | bytes 1179656 | tf_op jit(solution)/shard_map/ppermute | solution.py:180
  82.1 46.1 %copy-start.3 = (bf16[32,6,8,128]{3,2,1,0:T(8,128)(2,1)}, bf16[32,6,8,128]{3,2,1,0:T(8,128)(2,1)S(1)}, u32[]{:S(2)}) copy-start(bf16[32,6,8,128]{3,2,1,0:T(8,128)(2,1)S(1)} %all-to-all-done.3.high) | copy-start | bytes 1179652
  82.1 10.7 %collective-permute-start.4 = (bf16[32,6,8,128]{3,2,1,0:T(8,128)(2,1)S(1)}, bf16[32,6,8,128]{3,2,1,0:T(8,128)(2,1)S(1)}, u32[]{:S(2)}, u32[]{:S(2)}) collective-permute-start(bf16[32,6,8,128]{3,2,1,0:T(8,128)(2,1)S(1)} %all-to-all-done.3.high), channel_id=1, source_target_pairs={{0,7},{1,0},{2,1},{3,2},{4,3},{5,4},{6,5},{7,6},{8,15},{9,8},{10,9... | collective-permute-start | bytes 1179656 | tf_op jit(solution)/shard_map/ppermute | solution.py:181
  82.1 14.3 %collective-permute-start.11 = (bf16[32,6,8,128]{3,2,1,0:T(8,128)(2,1)S(1)}, bf16[32,6,8,128]{3,2,1,0:T(8,128)(2,1)S(1)}, u32[]{:S(2)}, u32[]{:S(2)}) collective-permute-start(bf16[32,6,8,128]{3,2,1,0:T(8,128)(2,1)S(1)} %all-to-all-done.3.high), channel_id=1, source_target_pairs={{0,1},{1,2},{2,3},{3,4},{4,5},{5,6},{6,7},{7,0},{8,9},{9,10},{10,1... | collective-permute-start | bytes 1179656 | tf_op jit(solution)/shard_map/ppermute | solution.py:185
  83.6 17.7 %collective-permute-start.8 = (bf16[32,6,8,128]{3,2,1,0:T(8,128)(2,1)S(1)}, bf16[32,6,8,128]{3,2,1,0:T(8,128)(2,1)S(1)}, u32[]{:S(2)}, u32[]{:S(2)}) collective-permute-start(bf16[32,6,8,128]{3,2,1,0:T(8,128)(2,1)S(1)} %all_to_all.20.low), channel_id=1, source_target_pairs={{0,7},{1,0},{2,1},{3,2},{4,3},{5,4},{6,5},{7,6},{8,15},{9,8},{10,9... | collective-permute-start | bytes 1179656 | tf_op jit(solution)/shard_map/ppermute | solution.py:186
  85.5 47.5 %copy-start.4 = (bf16[32,6,8,128]{3,2,1,0:T(8,128)(2,1)}, bf16[32,6,8,128]{3,2,1,0:T(8,128)(2,1)S(1)}, u32[]{:S(2)}) copy-start(bf16[32,6,8,128]{3,2,1,0:T(8,128)(2,1)S(1)} %collective-permute-done.low) | copy-start | bytes 1179652
  85.5 17.3 %collective-permute-start.1 = (bf16[32,6,8,128]{3,2,1,0:T(8,128)(2,1)S(1)}, bf16[32,6,8,128]{3,2,1,0:T(8,128)(2,1)S(1)}, u32[]{:S(2)}, u32[]{:S(2)}) collective-permute-start(bf16[32,6,8,128]{3,2,1,0:T(8,128)(2,1)S(1)} %collective-permute-done.low), channel_id=1, source_target_pairs={{0,1},{1,2},{2,3},{3,4},{4,5},{5,6},{6,7},{7,0},{8,9},{9,10},{10,1... | collective-permute-start | bytes 1179656 | tf_op jit(solution)/shard_map/ppermute | solution.py:180
  92.8 40.1 %copy-start.5 = (bf16[32,6,8,128]{3,2,1,0:T(8,128)(2,1)}, bf16[32,6,8,128]{3,2,1,0:T(8,128)(2,1)S(1)}, u32[]{:S(2)}) copy-start(bf16[32,6,8,128]{3,2,1,0:T(8,128)(2,1)S(1)} %collective-permute-done.4.high) | copy-start | bytes 1179652
  92.8 17.0 %collective-permute-start.5 = (bf16[32,6,8,128]{3,2,1,0:T(8,128)(2,1)S(1)}, bf16[32,6,8,128]{3,2,1,0:T(8,128)(2,1)S(1)}, u32[]{:S(2)}, u32[]{:S(2)}) collective-permute-start(bf16[32,6,8,128]{3,2,1,0:T(8,128)(2,1)S(1)} %collective-permute-done.4.high), channel_id=1, source_target_pairs={{0,7},{1,0},{2,1},{3,2},{4,3},{5,4},{6,5},{7,6},{8,15},{9,8},{10,9... | collective-permute-start | bytes 1179656 | tf_op jit(solution)/shard_map/ppermute | solution.py:181
  96.4 36.6 %copy-start.7 = (bf16[32,6,8,128]{3,2,1,0:T(8,128)(2,1)}, bf16[32,6,8,128]{3,2,1,0:T(8,128)(2,1)S(1)}, u32[]{:S(2)}) copy-start(bf16[32,6,8,128]{3,2,1,0:T(8,128)(2,1)S(1)} %collective-permute-done.11.high) | copy-start | bytes 1179652
  96.4 18.6 %collective-permute-start.12 = (bf16[32,6,8,128]{3,2,1,0:T(8,128)(2,1)S(1)}, bf16[32,6,8,128]{3,2,1,0:T(8,128)(2,1)}, u32[]{:S(2)}, u32[]{:S(2)}) collective-permute-start(bf16[32,6,8,128]{3,2,1,0:T(8,128)(2,1)S(1)} %collective-permute-done.11.high), channel_id=1, source_target_pairs={{0,1},{1,2},{2,3},{3,4},{4,5},{5,6},{6,7},{7,0},{8,9},{9,10},{10,1... | collective-permute-start | bytes 1179656 | tf_op jit(solution)/shard_map/ppermute | solution.py:185
  101.3 31.7 %copy-start.6 = (bf16[32,6,8,128]{3,2,1,0:T(8,128)(2,1)}, bf16[32,6,8,128]{3,2,1,0:T(8,128)(2,1)S(1)}, u32[]{:S(2)}) copy-start(bf16[32,6,8,128]{3,2,1,0:T(8,128)(2,1)S(1)} %collective-permute-done.8.low) | copy-start | bytes 1179652
  101.3 17.0 %collective-permute-start.9 = (bf16[32,6,8,128]{3,2,1,0:T(8,128)(2,1)S(1)}, bf16[32,6,8,128]{3,2,1,0:T(8,128)(2,1)S(1)}, u32[]{:S(2)}, u32[]{:S(2)}) collective-permute-start(bf16[32,6,8,128]{3,2,1,0:T(8,128)(2,1)S(1)} %collective-permute-done.8.low), channel_id=1, source_target_pairs={{0,7},{1,0},{2,1},{3,2},{4,3},{5,4},{6,5},{7,6},{8,15},{9,8},{10,9... | collective-permute-start | bytes 1179656 | tf_op jit(solution)/shard_map/ppermute | solution.py:186
  102.8 30.2 %copy-start.8 = (bf16[32,6,8,128]{3,2,1,0:T(8,128)(2,1)}, bf16[32,6,8,128]{3,2,1,0:T(8,128)(2,1)S(1)}, u32[]{:S(2)}) copy-start(bf16[32,6,8,128]{3,2,1,0:T(8,128)(2,1)S(1)} %collective-permute-done.1.low) | copy-start | bytes 1179652
  102.8 18.1 %collective-permute-start.2 = (bf16[32,6,8,128]{3,2,1,0:T(8,128)(2,1)S(1)}, bf16[32,6,8,128]{3,2,1,0:T(8,128)(2,1)}, u32[]{:S(2)}, u32[]{:S(2)}) collective-permute-start(bf16[32,6,8,128]{3,2,1,0:T(8,128)(2,1)S(1)} %collective-permute-done.1.low), channel_id=1, source_target_pairs={{0,1},{1,2},{2,3},{3,4},{4,5},{5,6},{6,7},{7,0},{8,9},{9,10},{10,1... | collective-permute-start | bytes 1179656 | tf_op jit(solution)/shard_map/ppermute | solution.py:180
  109.8 23.2 %copy-start.9 = (bf16[32,6,8,128]{3,2,1,0:T(8,128)(2,1)}, bf16[32,6,8,128]{3,2,1,0:T(8,128)(2,1)S(1)}, u32[]{:S(2)}) copy-start(bf16[32,6,8,128]{3,2,1,0:T(8,128)(2,1)S(1)} %collective-permute-done.5.high) | copy-start | bytes 1179652
  109.8 16.9 %collective-permute-start.6 = (bf16[32,6,8,128]{3,2,1,0:T(8,128)(2,1)S(1)}, bf16[32,6,8,128]{3,2,1,0:T(8,128)(2,1)}, u32[]{:S(2)}, u32[]{:S(2)}) collective-permute-start(bf16[32,6,8,128]{3,2,1,0:T(8,128)(2,1)S(1)} %collective-permute-done.5.high), channel_id=1, source_target_pairs={{0,7},{1,0},{2,1},{3,2},{4,3},{5,4},{6,5},{7,6},{8,15},{9,8},{10,9... | collective-permute-start | bytes 1179656 | tf_op jit(solution)/shard_map/ppermute | solution.py:181
  115.0 37.4 %collective-permute-start.13 = (bf16[32,6,8,128]{3,2,1,0:T(8,128)(2,1)}, bf16[32,6,8,128]{3,2,1,0:T(8,128)(2,1)}, u32[]{:S(2)}, u32[]{:S(2)}) collective-permute-start(bf16[32,6,8,128]{3,2,1,0:T(8,128)(2,1)} %collective-permute-done.12.high), channel_id=1, source_target_pairs={{0,1},{1,2},{2,3},{3,4},{4,5},{5,6},{6,7},{7,0},{8,9},{9,10},{10,1... | collective-permute-start | bytes 1179656 | tf_op jit(solution)/shard_map/ppermute | solution.py:185
  118.2 14.8 %copy-start.10 = (bf16[32,6,8,128]{3,2,1,0:T(8,128)(2,1)}, bf16[32,6,8,128]{3,2,1,0:T(8,128)(2,1)S(1)}, u32[]{:S(2)}) copy-start(bf16[32,6,8,128]{3,2,1,0:T(8,128)(2,1)S(1)} %collective-permute-done.9.low) | copy-start | bytes 1179652
  118.2 38.9 %collective-permute-start.10 = (bf16[32,6,8,128]{3,2,1,0:T(8,128)(2,1)S(1)}, bf16[32,6,8,128]{3,2,1,0:T(8,128)(2,1)}, u32[]{:S(2)}, u32[]{:S(2)}) collective-permute-start(bf16[32,6,8,128]{3,2,1,0:T(8,128)(2,1)S(1)} %collective-permute-done.9.low), channel_id=1, source_target_pairs={{0,7},{1,0},{2,1},{3,2},{4,3},{5,4},{6,5},{7,6},{8,15},{9,8},{10,9... | collective-permute-start | bytes 1179656 | tf_op jit(solution)/shard_map/ppermute | solution.py:186
  120.9 41.0 %collective-permute-start.3 = (bf16[32,6,8,128]{3,2,1,0:T(8,128)(2,1)}, bf16[32,6,8,128]{3,2,1,0:T(8,128)(2,1)}, u32[]{:S(2)}, u32[]{:S(2)}) collective-permute-start(bf16[32,6,8,128]{3,2,1,0:T(8,128)(2,1)} %collective-permute-done.2.low), channel_id=1, source_target_pairs={{0,1},{1,2},{2,3},{3,4},{4,5},{5,6},{6,7},{7,0},{8,9},{9,10},{10,1... | collective-permute-start | bytes 1179656 | tf_op jit(solution)/shard_map/ppermute | solution.py:180
  126.6 35.3 %collective-permute-start.7 = (bf16[32,6,8,128]{3,2,1,0:T(8,128)(2,1)}, bf16[32,6,8,128]{3,2,1,0:T(8,128)(2,1)}, u32[]{:S(2)}, u32[]{:S(2)}) collective-permute-start(bf16[32,6,8,128]{3,2,1,0:T(8,128)(2,1)} %collective-permute-done.6.high), channel_id=1, source_target_pairs={{0,7},{1,0},{2,1},{3,2},{4,3},{5,4},{6,5},{7,6},{8,15},{9,8},{10,9... | collective-permute-start | bytes 1179656 | tf_op jit(solution)/shard_map/ppermute | solution.py:181
where the time goes:
time: 168 us; the launch traced here: 167 us
  waiting for transfers between devices  62.4 us (37%)
  Pallas kernels  41.8 us (25%)
  starting transfers between devices  34.6 us (21%)
  blocking collectives  14.7 us (9%)
  other arithmetic  8.63 us (5%)
  local copies, waits for them, and re-layouts  4.47 us (3%)
    pallas_call x8, Pallas kernels, attend(): pl.pallas_call(body, out_shape=shape, grid_spec=pltpu.PrefetchScalarGridS...  38.5 us
    all_to_all x1, waiting for transfers between devices, attention(): lax.all_to_all(own.reshape(n_seq * n_head, TILE, BS), ('seq', 'head'), 0,...  20.5 us
    ppermute x4, waiting for transfers between devices, attention(): high_down = lax.ppermute(high_down, 'head', down)  19.6 us
    all_to_all x1, blocking collectives, attention(): low = lax.all_to_all(low, 'seq', 0, 0, tiled=True)  14.7 us
    all_to_all x1, starting transfers between devices, attention(): lax.all_to_all(own.reshape(n_seq * n_head, TILE, BS), ('seq', 'head'), 0,...  11 us
    all_to_all x1, waiting for transfers between devices, attention(): high = lax.all_to_all(high, 'seq', 0, 0, tiled=True)  9.38 us
    all_to_all x1, starting transfers between devices, attention(): lax.all_to_all(jnp.broadcast_to(pool[None, None], (n_seq, 1, BS)), 'seq',...  8.58 us
    ppermute x3, waiting for transfers between devices, attention(): low_down = lax.ppermute(low_down, 'head', down)  7.93 us
  transfers between devices with their start and end apart: 17, of which 8 were waited for; matrix products, arithmetic and copies ran while one was open for 6% of the time, Pallas kernels for 20%

commit v1 on v0

v1 whole, which is shorter than its diff:
```python
import functools
import math

import jax
import jax.numpy as jnp
from jax import lax
from jax.experimental import pallas as pl
from jax.experimental.pallas import tpu as pltpu
from jax.sharding import PartitionSpec as P


BS = 128
POOL = 12
HALF = POOL // 2
TILE = 8
NEG = -1e30
GRANT = 24 << 20


def pool_of(ancestors):
    flat = ancestors.reshape(-1)
    n = flat.shape[0]
    order = jnp.arange(n, dtype=jnp.int32)
    same = flat[:, None] == flat[None, :]
    repeat = jnp.any(same & (order[None, :] < order[:, None]), axis=1)
    first = ~repeat
    rank = jnp.sum((first[None, :] & (flat[None, :] < flat[:, None])).astype(jnp.int32), axis=1)
    slots = jnp.arange(BS, dtype=jnp.int32)
    hit = first[:, None] & (rank[:, None] == slots[None, :])
    pool = jnp.sum(jnp.where(hit, flat[:, None], 0), axis=0)
    return pool, rank.reshape(ancestors.shape)


def vmem():
    return pl.BlockSpec(memory_space=pltpu.VMEM)


def smem():
    return pl.BlockSpec(memory_space=pltpu.SMEM)


def pick_kernel(pools, me, held, low, high):
    mine = me[0]

    def one(s, carry):
        row = s ^ mine
        for i in range(HALF):
            low[s, i] = held[pools[row, i]]
            high[s, i] = held[pools[row, HALF + i]]
        return carry

    lax.fori_loop(0, pools.shape[0], one, 0, unroll=2)


def pick(pools, me, held):
    groups = pools.shape[0]
    part = jax.ShapeDtypeStruct((groups, HALF, TILE, BS), held.dtype)
    return pl.pallas_call(
        pick_kernel,
        out_shape=(part, part),
        in_specs=[smem(), smem(), vmem()],
        out_specs=(vmem(), vmem()),
        compiler_params=pltpu.CompilerParams(vmem_limit_bytes=GRANT),
        name="pick",
    )(pools, me, held)


def attend_kernel(scale, call, meta, q, own, low, high, _, out, keys, vals):
    far = 8
    row = lax.broadcasted_iota(jnp.int32, (BS, BS), 0)
    g = meta[call, 0]

    def put(j, k, v, length):
        k = k.astype(jnp.float32).reshape(BS, BS)
        v = v.astype(jnp.float32).reshape(BS, BS)
        valid = row < length
        at = slice(j * BS, (j + 1) * BS)
        keys[at, :] = jnp.where(valid, k, k[0:1, :]).astype(jnp.bfloat16)
        vals[at, 0:BS] = jnp.where(valid, v, 0.0).astype(jnp.bfloat16)
        vals[at, BS:] = jnp.where(valid, 1.0, 0.0).astype(jnp.bfloat16)

    put(0, own[0:16, g], own[16:32, g], meta[call, 17])
    for j in range(far):
        place, length = meta[call, 1 + j], meta[call, 9 + j]

        @pl.when(place < HALF)
        def _():
            put(j + 1, low[0:16, place], low[16:32, place], length)

        @pl.when(place >= HALF)
        def _():
            put(j + 1, high[0:16, place - HALF], high[16:32, place - HALF], length)

    tokens = 32
    rows = tokens * 8
    token = lax.broadcasted_iota(jnp.int32, (rows, BS), 0) // 8
    offset = lax.broadcasted_iota(jnp.int32, (rows, BS), 1)
    heads = pl.ds(pl.multiple_of(g * 8, 8), 8)
    for i in range(BS // tokens):
        at = slice(i * tokens, (i + 1) * tokens)
        qt = q[at, heads].astype(jnp.float32).reshape(rows, BS).astype(jnp.bfloat16)
        s = lax.dot_general(qt, keys[...], (((1,), (1,)), ((), ())), preferred_element_type=jnp.float32)
        s_own = jnp.where(offset <= token + i * tokens, s[:, 0:BS], NEG)
        s_far = s[:, BS:]
        m = jnp.maximum(jnp.max(s_own, axis=1, keepdims=True), jnp.max(s_far, axis=1, keepdims=True))
        p_own = jnp.exp2((s_own - m) * scale).astype(jnp.bfloat16)
        p_far = jnp.exp2((s_far - m) * scale).astype(jnp.bfloat16)
        o = jnp.dot(p_own, vals[0:BS, :], preferred_element_type=jnp.float32)
        o = o + jnp.dot(p_far, vals[BS:, :], preferred_element_type=jnp.float32)
        r = o[:, 0:BS] / o[:, BS:]
        out[at] = r.reshape(tokens, 8, BS).astype(out.dtype)


def attend(call, meta, q, own, low, high, prev):
    scale = math.log2(math.e) / math.sqrt(BS)
    shape = jax.ShapeDtypeStruct(prev.shape, q.dtype)
    heads = pl.BlockSpec((BS, 8, BS), lambda i, m: (0, m[call, 0], 0))
    flops = 2 * 2 * 1024 * 1152 * 128
    return pl.pallas_call(
        functools.partial(attend_kernel, scale, call),
        out_shape=shape,
        grid_spec=pltpu.PrefetchScalarGridSpec(
            num_scalar_prefetch=1, grid=(1,),
            in_specs=[vmem(), vmem(), vmem(), vmem(), pl.BlockSpec(memory_space=pl.ANY)],
            out_specs=heads,
            scratch_shapes=[
                pltpu.VMEM((9 * BS, BS), jnp.bfloat16),
                pltpu.VMEM((9 * BS, 2 * BS), jnp.bfloat16),
            ],
        ),
        input_output_aliases={5: 0},
        compiler_params=pltpu.CompilerParams(vmem_limit_bytes=GRANT),
        cost_estimate=pl.CostEstimate(flops=flops, bytes_accessed=2 << 20, transcendentals=1024 * 1152),
        name="attend",
    )(meta, q, own, low, high, prev)


def blank_kernel(out):
    pass


def blank(like):
    return pl.pallas_call(
        blank_kernel,
        out_shape=jax.ShapeDtypeStruct(like.shape, like.dtype),
        out_specs=pl.BlockSpec(memory_space=pl.ANY),
        name="blank",
    )()


def local(n_head, queries, keys, values, ancestors, lengths):
    return attention(n_head, queries, keys, values, ancestors, lengths)


def attention(n_head, queries, keys, values, ancestors, lengths):
    n_seq = 32
    place, level = lax.axis_index("seq"), lax.axis_index("head")
    pool, rank = pool_of(ancestors)
    pools = pool[None]
    bit = 1
    while bit < n_seq:
        other = lax.ppermute(pools, "seq", [(i, i ^ bit) for i in range(n_seq)])
        pools = jnp.concatenate([pools, other], axis=0)
        bit *= 2

    named = lax.dynamic_slice_in_dim(ancestors, level, 1)
    ranks = lax.dynamic_slice_in_dim(rank, level, 1)
    far_len = jnp.take(lengths, named)
    own_len = lax.dynamic_slice_in_dim(lengths, place * n_head + level, 1)[None]
    row = jnp.concatenate([ranks, far_len, own_len], axis=1)
    shifts = [0]
    for step in range(1, n_head // 2):
        shifts += [n_head - step, step]
    shifts.append(n_head // 2)
    heads = (level + jnp.array(shifts, jnp.int32)) % n_head
    meta = jnp.concatenate([heads[:, None], jnp.broadcast_to(row, (n_head, row.shape[1]))], axis=1)

    own = jnp.concatenate([keys, values], axis=0).reshape(32, TILE, n_head, BS).transpose(0, 2, 1, 3)
    held = lax.all_to_all(own.reshape(n_seq * n_head, TILE, BS), ("seq", "head"), 0, 0, tiled=True)
    low, high = pick(pools, place.astype(jnp.int32)[None], held)
    low = lax.all_to_all(low, "seq", 0, 0, tiled=True)
    high = lax.all_to_all(high, "seq", 0, 0, tiled=True)

    up = [(i, (i + 1) % n_head) for i in range(n_head)]
    down = [(i, (i - 1) % n_head) for i in range(n_head)]
    out = blank(queries)
    out = attend(0, meta, queries, own, low, high, out)
    low_up = low_down = low
    high_up = high_down = high
    for step in range(1, n_head // 2 + 1):
        last = step == n_head // 2
        low_up = lax.ppermute(low_up, "head", up)
        high_down = lax.ppermute(high_down, "head", down)
        if last:
            out = attend(n_head - 1, meta, queries, own, low_up, high_down, out)
            break
        high_up = lax.ppermute(high_up, "head", up)
        low_down = lax.ppermute(low_down, "head", down)
        out = attend(2 * step - 1, meta, queries, own, low_up, high_up, out)
        out = attend(2 * step, meta, queries, own, low_down, high_down, out)
    return out


def solution(mesh):
    placed = (
        P(("seq", "head"), None, None),
        P(("seq", "head"), None, None),
        P(("seq", "head"), None, None),
        P("seq", None),
        P(),
    )
    body = functools.partial(local, mesh.shape["head"])
    return jax.shard_map(
        body, mesh=mesh, in_specs=placed, out_specs=P(("seq", "head"), None, None), check_vma=False
    )
```

time: 168 us -> 159 us (0.946)
  starting transfers between devices: 34.6 us -> 50.3 us
  waiting for transfers between devices: 62.4 us -> 47.5 us
  other arithmetic: 8.63 us -> 2.36 us
  Pallas kernels: 41.8 us -> 39.7 us
  local copies, waits for them, and re-layouts: 4.47 us -> 2.52 us
    all_to_all x1, waiting for transfers between devices: 20.5 us -> 3.13 us  [attention(): lax.all_to_all(own.reshape(n_seq * n_head, TILE, BS), ('seq', 'head'), 0,...]
    ppermute x0 -> x5, waiting for transfers between devices: none -> 12.5 us  [attention(): other = lax.ppermute(pools, 'seq', [(i, i ^ bit) for i in range(n_seq)])]
    ppermute x4, starting transfers between devices: 4.38 us -> 14.6 us  [attention(): high_down = lax.ppermute(high_down, 'head', down)]
    all_to_all x1 -> x0, starting transfers between devices: 8.58 us -> none  [attention(): lax.all_to_all(jnp.broadcast_to(pool[None, None], (n_seq, 1, BS)), 'seq',...]
    ppermute x4, waiting for transfers between devices: 19.6 us -> 13.5 us  [attention(): high_down = lax.ppermute(high_down, 'head', down)]
    ppermute x3, starting transfers between devices: 4.1 us -> 9.59 us  [attention(): low_down = lax.ppermute(low_down, 'head', down)]
    concatenate x4, other arithmetic: 5.08 us -> 0.03 us  [the longest x3 0.03 us: attention(): pools = jnp.concatenate([pools, other], axis=0)]
    all_to_all x1 -> x0, waiting for transfers between devices: 4.89 us -> none  [attention(): lax.all_to_all(jnp.broadcast_to(pool[None, None], (n_seq, 1, BS)), 'seq',...]
  transfers between devices with their start and end apart: 17 -> 21, of which waited for: 8 -> 12; matrix products, arithmetic and copies ran while one was open for 6% -> 2% of each run, Pallas kernels for 20% -> 21%
where the time goes in v1:
time: 159 us
  starting transfers between devices  50.3 us (32%)
  waiting for transfers between devices  47.5 us (30%)
  Pallas kernels  39.7 us (25%)
  blocking collectives  16.1 us (10%)
  local copies, waits for them, and re-layouts  2.52 us (2%)
  other arithmetic  2.36 us (1%)
    pallas_call x8, Pallas kernels, attend(): pl.pallas_call(functools.partial(attend_kernel, scale, call), out_shape=s...  37.7 us
    all_to_all x1, blocking collectives, attention(): low = lax.all_to_all(low, 'seq', 0, 0, tiled=True)  16.1 us
    all_to_all x1, starting transfers between devices, attention(): lax.all_to_all(own.reshape(n_seq * n_head, TILE, BS), ('seq', 'head'), 0,...  15.6 us
    ppermute x4, starting transfers between devices, attention(): high_down = lax.ppermute(high_down, 'head', down)  14.6 us
    ppermute x4, waiting for transfers between devices, attention(): high_down = lax.ppermute(high_down, 'head', down)  13.5 us
    ppermute x5, waiting for transfers between devices, attention(): other = lax.ppermute(pools, 'seq', [(i, i ^ bit) for i in range(n_seq)])  12.5 us
    ppermute x3, waiting for transfers between devices, attention(): low_down = lax.ppermute(low_down, 'head', down)  9.69 us
    ppermute x3, starting transfers between devices, attention(): low_down = lax.ppermute(low_down, 'head', down)  9.59 us
  transfers between devices with their start and end apart: 21, of which 12 were waited for; matrix products, arithmetic and copies ran while one was open for 2% of the time, Pallas kernels for 21%

profile of v1, /device:TPU:1, one launch (start us, length us, event | category | flops | bytes accessed | tf_op | source)
XLA Modules:
  0.0 158.6 jit_solution(16842572363355138050)
XLA Ops:
  0.0 1.1 pad_maximum_fusion
  1.1 0.0 copy-start.1
  1.1 0.9 copy.22
  2.0 15.6 %all-to-all-start = ((bf16[256,8,128]{2,1,0:T(8,128)(2,1)}), bf16[256,8,128]{2,1,0:T(8,128)(2,1)S(1)}, u32[]{:S(2)}, u32[]{:S(2)}) async-start(bf16[256,8,128]{2,1,0:T(8,128)(2,1)} %bitcast.9), calls=%async_computation | async-start | bytes 1048576 | tf_op jit(solution)/shard_map/all_to_all | solution.py:179
  17.7 0.1 eq.30
  17.8 0.2 fusion.1
  17.9 0.2 convert_reduce_fusion
  18.1 0.1 select_reduce_fusion
  18.3 2.2 %collective-permute-start = (s32[1,128]{1,0:T(1,128)S(1)}, s32[1,128]{1,0:T(1,128)S(1)}, u32[]{:S(2)}, u32[]{:S(2)}) collective-permute-start(s32[1,128]{1,0:T(1,128)S(1)} %bitcast.17), channel_id=1, source_target_pairs={{0,8},{8,0},{16,24},{24,16},{32,40},{40,32},{48,56},{56,48},{64,72... | collective-permute-start | bytes 1544 | tf_op jit(solution)/shard_map/ppermute | solution.py:162
  20.5 0.8 collective-permute-done
  21.3 0.0 collective-permute-start.1
  21.3 2.7 %collective-permute-done.1 = s32[2,128]{1,0:T(2,128)S(1)} collective-permute-done((s32[2,128]{1,0:T(2,128)S(1)}, s32[2,128]{1,0:T(2,128)S(1)}, u32[]{:S(2)}, u32[]{:S(2)}) %collective-permute-start.1) | collective-permute-done | bytes 1056 | tf_op jit(solution)/shard_map/ppermute | solution.py:162
  24.0 1.2 collective-permute-start.2
  25.2 3.1 %collective-permute-done.2 = s32[4,128]{1,0:T(4,128)S(1)} collective-permute-done((s32[4,128]{1,0:T(4,128)S(1)}, s32[4,128]{1,0:T(4,128)S(1)}, u32[]{:S(2)}, u32[]{:S(2)}) %collective-permute-start.2) | collective-permute-done | bytes 2080 | tf_op jit(solution)/shard_map/ppermute | solution.py:162
  28.4 0.1 collective-permute-start.3
  28.5 2.7 %collective-permute-done.3 = s32[8,128]{1,0:T(8,128)S(1)} collective-permute-done((s32[8,128]{1,0:T(8,128)S(1)}, s32[8,128]{1,0:T(8,128)S(1)}, u32[]{:S(2)}, u32[]{:S(2)}) %collective-permute-start.3) | collective-permute-done | bytes 4128 | tf_op jit(solution)/shard_map/ppermute | solution.py:162
  31.2 1.3 collective-permute-start.4
  32.6 3.0 %collective-permute-done.4 = s32[16,128]{1,0:T(8,128)S(1)} collective-permute-done((s32[16,128]{1,0:T(8,128)S(1)}, s32[16,128]{1,0:T(8,128)S(1)}, u32[]{:S(2)}, u32[]{:S(2)}) %collective-permute-start.4) | collective-permute-done | bytes 8224 | tf_op jit(solution)/shard_map/ppermute | solution.py:162
  35.6 3.1 %all-to-all-done.held = bf16[256,8,128]{2,1,0:T(8,128)(2,1)S(1)} async-done(((bf16[256,8,128]{2,1,0:T(8,128)(2,1)}), bf16[256,8,128]{2,1,0:T(8,128)(2,1)S(1)}, u32[]{:S(2)}, u32[]{:S(2)}) %all-to-all-start) | async-done | bytes 524320 | tf_op jit(solution)/shard_map/all_to_all | solution.py:179
  38.8 2.0 %pick.1 = (bf16[32,6,8,128]{3,2,1,0:T(8,128)(2,1)S(1)}, bf16[32,6,8,128]{3,2,1,0:T(8,128)(2,1)}) custom-call(s32[32,128]{1,0:T(8,128)S(1)} %concatenate.35.pools, s32[1]{0:T(128)} %bitcast.8.me, bf16[256,8,128]{2,1,0:T(8,128)(2,1)S(1)} %all-to-all-done.held), custom_call_target="tpu_custom_call" | custom-call | tf_op jit(solution)/shard_map/pick/pallas_call | solution.py:58
  40.8 16.1 %all_to_all.15.low = bf16[32,6,8,128]{3,2,1,0:T(8,128)(2,1)S(1)} all-to-all(bf16[32,6,8,128]{3,2,1,0:T(8,128)(2,1)S(1)} %get-tuple-element.7), channel_id=1, replica_groups=mesh['seq'=32,'head'=8] {'seq'}, dimensions={0} | all-to-all | bytes 786432 | tf_op jit(solution)/shard_map/all_to_all | solution.py:181
  56.9 3.7 %all-to-all-start.2 = ((bf16[32,6,8,128]{3,2,1,0:T(8,128)(2,1)}), bf16[32,6,8,128]{3,2,1,0:T(8,128)(2,1)S(1)}, u32[]{:S(2)}, u32[]{:S(2)}) async-start(bf16[32,6,8,128]{3,2,1,0:T(8,128)(2,1)} %get-tuple-element.8), calls=%async_computation.2 | async-start | bytes 786432 | tf_op jit(solution)/shard_map/all_to_all | solution.py:182
  60.6 1.5 collective-permute-start.5
  62.1 8.6 %all-to-all-done.2.high = bf16[32,6,8,128]{3,2,1,0:T(8,128)(2,1)S(1)} async-done(((bf16[32,6,8,128]{3,2,1,0:T(8,128)(2,1)}), bf16[32,6,8,128]{3,2,1,0:T(8,128)(2,1)S(1)}, u32[]{:S(2)}, u32[]{:S(2)}) %all-to-all-start.2) | async-done | bytes 393248 | tf_op jit(solution)/shard_map/all_to_all | solution.py:182
  70.8 4.3 %collective-permute-start.9 = (bf16[32,6,8,128]{3,2,1,0:T(8,128)(2,1)S(1)}, bf16[32,6,8,128]{3,2,1,0:T(8,128)(2,1)}, u32[]{:S(2)}, u32[]{:S(2)}) collective-permute-start(bf16[32,6,8,128]{3,2,1,0:T(8,128)(2,1)S(1)} %all-to-all-done.2.high), channel_id=1, source_target_pairs={{0,7},{1,0},{2,1},{3,2},{4,3},{5,4},{6,5},{7,6},{8,15},{9,8},{10,9... | collective-permute-start | bytes 1179656 | tf_op jit(solution)/shard_map/ppermute | solution.py:193
  75.1 0.1 reshape.31
  75.1 0.0 collective-permute-start.16
  75.2 2.7 %collective-permute-start.13 = (bf16[32,6,8,128]{3,2,1,0:T(8,128)(2,1)S(1)}, bf16[32,6,8,128]{3,2,1,0:T(8,128)(2,1)}, u32[]{:S(2)}, u32[]{:S(2)}) collective-permute-start(bf16[32,6,8,128]{3,2,1,0:T(8,128)(2,1)S(1)} %all_to_all.15.low), channel_id=1, source_target_pairs={{0,7},{1,0},{2,1},{3,2},{4,3},{5,4},{6,5},{7,6},{8,15},{9,8},{10,9... | collective-permute-start | bytes 1179656 | tf_op jit(solution)/shard_map/ppermute | solution.py:198
  77.9 0.6 gather_fusion
  78.5 0.6 dynamic_slice.11
  79.1 0.0 collective-permute-done.5.low
  79.1 0.0 collective-permute-start.6
  79.1 4.5 %collective-permute-done.9.high = bf16[32,6,8,128]{3,2,1,0:T(8,128)(2,1)} collective-permute-done((bf16[32,6,8,128]{3,2,1,0:T(8,128)(2,1)S(1)}, bf16[32,6,8,128]{3,2,1,0:T(8,128)(2,1)}, u32[]{:S(2)}, u32[]{:S(2)}) %collective-permute-start.9) | collective-permute-done | bytes 393248 | tf_op jit(solution)/shard_map/ppermute | solution.py:193
  83.6 3.5 %collective-permute-start.10 = (bf16[32,6,8,128]{3,2,1,0:T(8,128)(2,1)}, bf16[32,6,8,128]{3,2,1,0:T(8,128)(2,1)}, u32[]{:S(2)}, u32[]{:S(2)}) collective-permute-start(bf16[32,6,8,128]{3,2,1,0:T(8,128)(2,1)} %collective-permute-done.9.high), channel_id=1, source_target_pairs={{0,7},{1,0},{2,1},{3,2},{4,3},{5,4},{6,5},{7,6},{8,15},{9,8},{10,9... | collective-permute-start | bytes 1179656 | tf_op jit(solution)/shard_map/ppermute | solution.py:193
  87.1 0.0 collective-permute-done.16.high
  87.1 0.1 collective-permute-start.17
  87.2 4.8 %collective-permute-done.13.low = bf16[32,6,8,128]{3,2,1,0:T(8,128)(2,1)} collective-permute-done((bf16[32,6,8,128]{3,2,1,0:T(8,128)(2,1)S(1)}, bf16[32,6,8,128]{3,2,1,0:T(8,128)(2,1)}, u32[]{:S(2)}, u32[]{:S(2)}) %collective-permute-start.13) | collective-permute-done | bytes 393248 | tf_op jit(solution)/shard_map/ppermute | solution.py:198
  92.0 3.5 %collective-permute-start.14 = (bf16[32,6,8,128]{3,2,1,0:T(8,128)(2,1)}, bf16[32,6,8,128]{3,2,1,0:T(8,128)(2,1)}, u32[]{:S(2)}, u32[]{:S(2)}) collective-permute-start(bf16[32,6,8,128]{3,2,1,0:T(8,128)(2,1)} %collective-permute-done.13.low), channel_id=1, source_target_pairs={{0,7},{1,0},{2,1},{3,2},{4,3},{5,4},{6,5},{7,6},{8,15},{9,8},{10,9... | collective-permute-start | bytes 1179656 | tf_op jit(solution)/shard_map/ppermute | solution.py:198
  95.5 0.7 add_bitcast_fusion
  96.3 0.1 pad.12.clone
  96.3 0.0 collective-permute-done.6.low
  96.3 0.2 collective-permute-start.7
  96.6 4.0 %collective-permute-done.10.high = bf16[32,6,8,128]{3,2,1,0:T(8,128)(2,1)} collective-permute-done((bf16[32,6,8,128]{3,2,1,0:T(8,128)(2,1)}, bf16[32,6,8,128]{3,2,1,0:T(8,128)(2,1)}, u32[]{:S(2)}, u32[]{:S(2)}) %collective-permute-start.10) | collective-permute-done | bytes 393248 | tf_op jit(solution)/shard_map/ppermute | solution.py:193
  100.6 3.4 %collective-permute-start.11 = (bf16[32,6,8,128]{3,2,1,0:T(8,128)(2,1)}, bf16[32,6,8,128]{3,2,1,0:T(8,128)(2,1)}, u32[]{:S(2)}, u32[]{:S(2)}) collective-permute-start(bf16[32,6,8,128]{3,2,1,0:T(8,128)(2,1)} %collective-permute-done.10.high), channel_id=1, source_target_pairs={{0,7},{1,0},{2,1},{3,2},{4,3},{5,4},{6,5},{7,6},{8,15},{9,8},{10,9... | collective-permute-start | bytes 1179656 | tf_op jit(solution)/shard_map/ppermute | solution.py:193
  104.0 0.1 copy.18
  104.1 0.0 collective-permute-start.18
  104.1 4.9 %collective-permute-done.14.low = bf16[32,6,8,128]{3,2,1,0:T(8,128)(2,1)} collective-permute-done((bf16[32,6,8,128]{3,2,1,0:T(8,128)(2,1)}, bf16[32,6,8,128]{3,2,1,0:T(8,128)(2,1)}, u32[]{:S(2)}, u32[]{:S(2)}) %collective-permute-start.14) | collective-permute-done | bytes 393248 | tf_op jit(solution)/shard_map/ppermute | solution.py:198
  109.0 3.4 %collective-permute-start.15 = (bf16[32,6,8,128]{3,2,1,0:T(8,128)(2,1)}, bf16[32,6,8,128]{3,2,1,0:T(8,128)(2,1)}, u32[]{:S(2)}, u32[]{:S(2)}) collective-permute-start(bf16[32,6,8,128]{3,2,1,0:T(8,128)(2,1)} %collective-permute-done.14.low), channel_id=1, source_target_pairs={{0,7},{1,0},{2,1},{3,2},{4,3},{5,4},{6,5},{7,6},{8,15},{9,8},{10,9... | collective-permute-start | bytes 1179656 | tf_op jit(solution)/shard_map/ppermute | solution.py:198
  112.4 5.0 %collective-permute-done.11.high = bf16[32,6,8,128]{3,2,1,0:T(8,128)(2,1)} collective-permute-done((bf16[32,6,8,128]{3,2,1,0:T(8,128)(2,1)}, bf16[32,6,8,128]{3,2,1,0:T(8,128)(2,1)}, u32[]{:S(2)}, u32[]{:S(2)}) %collective-permute-start.11) | collective-permute-done | bytes 393248 | tf_op jit(solution)/shard_map/ppermute | solution.py:193
  117.4 3.4 %collective-permute-start.12 = (bf16[32,6,8,128]{3,2,1,0:T(8,128)(2,1)}, bf16[32,6,8,128]{3,2,1,0:T(8,128)(2,1)S(1)}, u32[]{:S(2)}, u32[]{:S(2)}) collective-permute-start(bf16[32,6,8,128]{3,2,1,0:T(8,128)(2,1)} %collective-permute-done.11.high), channel_id=1, source_target_pairs={{0,7},{1,0},{2,1},{3,2},{4,3},{5,4},{6,5},{7,6},{8,15},{9,8},{10,9... | collective-permute-start | bytes 1179656 | tf_op jit(solution)/shard_map/ppermute | solution.py:193
  120.8 0.0 collective-permute-done.7.low
  120.8 0.0 collective-permute-start.8
  120.8 4.5 %attend.8._ = bf16[128,64,128]{2,1,0:T(8,128)(2,1)} custom-call(s32[8,18]{1,0:T(8,128)S(1)} %pad_add_fusion.meta, bf16[128,64,128]{2,1,0:T(8,128)(2,1)S(1)} %copy-done, bf16[32,8,8,128]{3,2,1,0:T(8,128)(2,1)} %bitcast.15.clone.2.own, bf16[32,6,8,128]{3,2,1,0:T(8,128)(2,1)S(1)} %all_to_all.15.low, ...), custom_call_target="tpu_custom_call", output_to_operand_aliasing={{}: (5, {})} | custom-call | flops 603979776 | bytes 2097152 | tf_op jit(solution)/shard_map/attend/pallas_call | solution.py:119
  125.4 4.6 %attend.9._ = bf16[128,64,128]{2,1,0:T(8,128)(2,1)} custom-call(s32[8,18]{1,0:T(8,128)S(1)} %pad_add_fusion.meta, bf16[128,64,128]{2,1,0:T(8,128)(2,1)S(1)} %copy-done, bf16[32,8,8,128]{3,2,1,0:T(8,128)(2,1)} %bitcast.15.clone.2.own, bf16[32,6,8,128]{3,2,1,0:T(8,128)(2,1)S(1)} %collective-permute-done.5.low, ...), custom_call_target="tpu_custom_call", output_to_operand_aliasing={{}: (5, {})} | custom-call | flops 603979776 | bytes 2097152 | tf_op jit(solution)/shard_map/attend/pallas_call | solution.py:119
  130.0 4.7 %attend.10._ = bf16[128,64,128]{2,1,0:T(8,128)(2,1)} custom-call(s32[8,18]{1,0:T(8,128)S(1)} %pad_add_fusion.meta, bf16[128,64,128]{2,1,0:T(8,128)(2,1)S(1)} %copy-done, bf16[32,8,8,128]{3,2,1,0:T(8,128)(2,1)} %bitcast.15.clone.2.own, bf16[32,6,8,128]{3,2,1,0:T(8,128)(2,1)} %collective-permute-done.13.low, ...), custom_call_target="tpu_custom_call", output_to_operand_aliasing={{}: (5, {})} | custom-call | flops 603979776 | bytes 2097152 | tf_op jit(solution)/shard_map/attend/pallas_call | solution.py:119
  134.8 5.0 %attend.11._ = bf16[128,64,128]{2,1,0:T(8,128)(2,1)} custom-call(s32[8,18]{1,0:T(8,128)S(1)} %pad_add_fusion.meta, bf16[128,64,128]{2,1,0:T(8,128)(2,1)S(1)} %copy-done, bf16[32,8,8,128]{3,2,1,0:T(8,128)(2,1)} %bitcast.15.clone.2.own, bf16[32,6,8,128]{3,2,1,0:T(8,128)(2,1)} %collective-permute-done.6.low, ...), custom_call_target="tpu_custom_call", output_to_operand_aliasing={{}: (5, {})} | custom-call | flops 603979776 | bytes 2097152 | tf_op jit(solution)/shard_map/attend/pallas_call | solution.py:119
  139.7 4.8 %attend.12._ = bf16[128,64,128]{2,1,0:T(8,128)(2,1)} custom-call(s32[8,18]{1,0:T(8,128)S(1)} %pad_add_fusion.meta, bf16[128,64,128]{2,1,0:T(8,128)(2,1)S(1)} %copy-done, bf16[32,8,8,128]{3,2,1,0:T(8,128)(2,1)} %bitcast.15.clone.2.own, bf16[32,6,8,128]{3,2,1,0:T(8,128)(2,1)} %collective-permute-done.14.low, ...), custom_call_target="tpu_custom_call", output_to_operand_aliasing={{}: (5, {})} | custom-call | flops 603979776 | bytes 2097152 | tf_op jit(solution)/shard_map/attend/pallas_call | solution.py:119
  144.5 0.0 collective-permute-done.18.high
  144.5 4.8 %attend.13._ = bf16[128,64,128]{2,1,0:T(8,128)(2,1)} custom-call(s32[8,18]{1,0:T(8,128)S(1)} %pad_add_fusion.meta, bf16[128,64,128]{2,1,0:T(8,128)(2,1)S(1)} %copy-done, bf16[32,8,8,128]{3,2,1,0:T(8,128)(2,1)} %bitcast.15.clone.2.own, bf16[32,6,8,128]{3,2,1,0:T(8,128)(2,1)} %collective-permute-done.7.low, ...), custom_call_target="tpu_custom_call", output_to_operand_aliasing={{}: (5, {})} | custom-call | flops 603979776 | bytes 2097152 | tf_op jit(solution)/shard_map/attend/pallas_call | solution.py:119
  149.2 0.0 collective-permute-done.15.low
  149.3 4.8 %attend.14._ = bf16[128,64,128]{2,1,0:T(8,128)(2,1)} custom-call(s32[8,18]{1,0:T(8,128)S(1)} %pad_add_fusion.meta, bf16[128,64,128]{2,1,0:T(8,128)(2,1)S(1)} %copy-done, bf16[32,8,8,128]{3,2,1,0:T(8,128)(2,1)} %bitcast.15.clone.2.own, bf16[32,6,8,128]{3,2,1,0:T(8,128)(2,1)} %collective-permute-done.15.low, ...), custom_call_target="tpu_custom_call", output_to_operand_aliasing={{}: (5, {})} | custom-call | flops 603979776 | bytes 2097152 | tf_op jit(solution)/shard_map/attend/pallas_call | solution.py:119
  154.0 0.0 collective-permute-done.12.high
  154.0 0.0 collective-permute-done.8.low
  154.0 4.5 %attend.15 = bf16[128,64,128]{2,1,0:T(8,128)(2,1)} custom-call(s32[8,18]{1,0:T(8,128)S(1)} %pad_add_fusion.meta, bf16[128,64,128]{2,1,0:T(8,128)(2,1)S(1)} %copy-done, bf16[32,8,8,128]{3,2,1,0:T(8,128)(2,1)} %bitcast.15.clone.2.own, bf16[32,6,8,128]{3,2,1,0:T(8,128)(2,1)S(1)} %collective-permute-done.8.low, ...), custom_call_target="tpu_custom_call", output_to_operand_aliasing={{}: (5, {})} | custom-call | flops 603979776 | bytes 2097152 | tf_op jit(solution)/shard_map/attend/pallas_call | solution.py:119
  (21 shorter events, 0.1 us)
Async XLA Ops:
  0.0 17.7 %copy-start.2 = (s32[8,8]{1,0:T(8,128)S(1)}, s32[8,8]{1,0:T(8,128)}, u32[]{:S(2)}) copy-start(s32[8,8]{1,0:T(8,128)} %param.9) | copy-start | bytes 772
  1.1 76.8 %copy-start.1 = (s32[256]{0:T(256)S(1)}, s32[256]{0:T(256)}, u32[]{:S(2)}) copy-start(s32[256]{0:T(256)} %param.10) | copy-start | bytes 3076
  2.0 102.0 %copy-start.3 = (s32[8]{0:T(128)S(1)}, s32[8]{0:T(128)}, u32[]{:S(2)}) copy-start(s32[8]{0:T(128)} %constant.45.clone) | copy-start | bytes 100
  2.0 36.8 %all-to-all-start = ((bf16[256,8,128]{2,1,0:T(8,128)(2,1)}), bf16[256,8,128]{2,1,0:T(8,128)(2,1)S(1)}, u32[]{:S(2)}, u32[]{:S(2)}) async-start(bf16[256,8,128]{2,1,0:T(8,128)(2,1)} %bitcast.9), calls=%async_computation | async-start | bytes 1048576 | tf_op jit(solution)/shard_map/all_to_all | solution.py:179
  18.3 3.0 %collective-permute-start = (s32[1,128]{1,0:T(1,128)S(1)}, s32[1,128]{1,0:T(1,128)S(1)}, u32[]{:S(2)}, u32[]{:S(2)}) collective-permute-start(s32[1,128]{1,0:T(1,128)S(1)} %bitcast.17), channel_id=1, source_target_pairs={{0,8},{8,0},{16,24},{24,16},{32,40},{40,32},{48,56},{56,48},{64,72... | collective-permute-start | bytes 1544 | tf_op jit(solution)/shard_map/ppermute | solution.py:162
  21.3 2.7 %collective-permute-start.1 = (s32[2,128]{1,0:T(2,128)S(1)}, s32[2,128]{1,0:T(2,128)S(1)}, u32[]{:S(2)}, u32[]{:S(2)}) collective-permute-start(s32[2,128]{1,0:T(2,128)S(1)} %pad_add_fusion.3), channel_id=1, source_target_pairs={{0,16},{8,24},{16,0},{24,8},{32,48},{40,56},{48,32},{56,40},{64,80... | collective-permute-start | bytes 3080 | tf_op jit(solution)/shard_map/ppermute | solution.py:162
  24.0 4.3 %collective-permute-start.2 = (s32[4,128]{1,0:T(4,128)S(1)}, s32[4,128]{1,0:T(4,128)S(1)}, u32[]{:S(2)}, u32[]{:S(2)}) collective-permute-start(s32[4,128]{1,0:T(4,128)S(1)} %pad_add_fusion.2), channel_id=1, source_target_pairs={{0,32},{8,40},{16,48},{24,56},{32,0},{40,8},{48,16},{56,24},{64,96... | collective-permute-start | bytes 6152 | tf_op jit(solution)/shard_map/ppermute | solution.py:162
  28.4 2.8 %collective-permute-start.3 = (s32[8,128]{1,0:T(8,128)S(1)}, s32[8,128]{1,0:T(8,128)S(1)}, u32[]{:S(2)}, u32[]{:S(2)}) collective-permute-start(s32[8,128]{1,0:T(8,128)S(1)} %pad_add_fusion.1), channel_id=1, source_target_pairs={{0,64},{8,72},{16,80},{24,88},{32,96},{40,104},{48,112},{56,120},{... | collective-permute-start | bytes 12296 | tf_op jit(solution)/shard_map/ppermute | solution.py:162
  31.2 4.4 %collective-permute-start.4 = (s32[16,128]{1,0:T(8,128)S(1)}, s32[16,128]{1,0:T(8,128)S(1)}, u32[]{:S(2)}, u32[]{:S(2)}) collective-permute-start(s32[16,128]{1,0:T(8,128)S(1)} %concatenate.34), channel_id=1, source_target_pairs={{0,128},{8,136},{16,144},{24,152},{32,160},{40,168},{48,176},{56,1... | collective-permute-start | bytes 24584 | tf_op jit(solution)/shard_map/ppermute | solution.py:162
  40.8 80.0 %copy-start = (bf16[128,64,128]{2,1,0:T(8,128)(2,1)S(1)}, bf16[128,64,128]{2,1,0:T(8,128)(2,1)}, u32[]{:S(2)}) copy-start(bf16[128,64,128]{2,1,0:T(8,128)(2,1)} %q.15) | copy-start | bytes 6291460
  56.9 13.9 %all-to-all-start.2 = ((bf16[32,6,8,128]{3,2,1,0:T(8,128)(2,1)}), bf16[32,6,8,128]{3,2,1,0:T(8,128)(2,1)S(1)}, u32[]{:S(2)}, u32[]{:S(2)}) async-start(bf16[32,6,8,128]{3,2,1,0:T(8,128)(2,1)} %get-tuple-element.8), calls=%async_computation.2 | async-start | bytes 786432 | tf_op jit(solution)/shard_map/all_to_all | solution.py:182
  60.6 18.5 %collective-permute-start.5 = (bf16[32,6,8,128]{3,2,1,0:T(8,128)(2,1)S(1)}, bf16[32,6,8,128]{3,2,1,0:T(8,128)(2,1)S(1)}, u32[]{:S(2)}, u32[]{:S(2)}) collective-permute-start(bf16[32,6,8,128]{3,2,1,0:T(8,128)(2,1)S(1)} %all_to_all.15.low), channel_id=1, source_target_pairs={{0,1},{1,2},{2,3},{3,4},{4,5},{5,6},{6,7},{7,0},{8,9},{9,10},{10,1... | collective-permute-start | bytes 1179656 | tf_op jit(solution)/shard_map/ppermute | solution.py:192
  70.8 12.8 %collective-permute-start.9 = (bf16[32,6,8,128]{3,2,1,0:T(8,128)(2,1)S(1)}, bf16[32,6,8,128]{3,2,1,0:T(8,128)(2,1)}, u32[]{:S(2)}, u32[]{:S(2)}) collective-permute-start(bf16[32,6,8,128]{3,2,1,0:T(8,128)(2,1)S(1)} %all-to-all-done.2.high), channel_id=1, source_target_pairs={{0,7},{1,0},{2,1},{3,2},{4,3},{5,4},{6,5},{7,6},{8,15},{9,8},{10,9... | collective-permute-start | bytes 1179656 | tf_op jit(solution)/shard_map/ppermute | solution.py:193
  75.1 12.0 %collective-permute-start.16 = (bf16[32,6,8,128]{3,2,1,0:T(8,128)(2,1)S(1)}, bf16[32,6,8,128]{3,2,1,0:T(8,128)(2,1)}, u32[]{:S(2)}, u32[]{:S(2)}) collective-permute-start(bf16[32,6,8,128]{3,2,1,0:T(8,128)(2,1)S(1)} %all-to-all-done.2.high), channel_id=1, source_target_pairs={{0,1},{1,2},{2,3},{3,4},{4,5},{5,6},{6,7},{7,0},{8,9},{9,10},{10,1... | collective-permute-start | bytes 1179656 | tf_op jit(solution)/shard_map/ppermute | solution.py:197
  75.2 16.9 %collective-permute-start.13 = (bf16[32,6,8,128]{3,2,1,0:T(8,128)(2,1)S(1)}, bf16[32,6,8,128]{3,2,1,0:T(8,128)(2,1)}, u32[]{:S(2)}, u32[]{:S(2)}) collective-permute-start(bf16[32,6,8,128]{3,2,1,0:T(8,128)(2,1)S(1)} %all_to_all.15.low), channel_id=1, source_target_pairs={{0,7},{1,0},{2,1},{3,2},{4,3},{5,4},{6,5},{7,6},{8,15},{9,8},{10,9... | collective-permute-start | bytes 1179656 | tf_op jit(solution)/shard_map/ppermute | solution.py:198
  79.1 17.3 %collective-permute-start.6 = (bf16[32,6,8,128]{3,2,1,0:T(8,128)(2,1)S(1)}, bf16[32,6,8,128]{3,2,1,0:T(8,128)(2,1)}, u32[]{:S(2)}, u32[]{:S(2)}) collective-permute-start(bf16[32,6,8,128]{3,2,1,0:T(8,128)(2,1)S(1)} %collective-permute-done.5.low), channel_id=1, source_target_pairs={{0,1},{1,2},{2,3},{3,4},{4,5},{5,6},{6,7},{7,0},{8,9},{9,10},{10,1... | collective-permute-start | bytes 1179656 | tf_op jit(solution)/shard_map/ppermute | solution.py:192
  83.6 17.0 %collective-permute-start.10 = (bf16[32,6,8,128]{3,2,1,0:T(8,128)(2,1)}, bf16[32,6,8,128]{3,2,1,0:T(8,128)(2,1)}, u32[]{:S(2)}, u32[]{:S(2)}) collective-permute-start(bf16[32,6,8,128]{3,2,1,0:T(8,128)(2,1)} %collective-permute-done.9.high), channel_id=1, source_target_pairs={{0,7},{1,0},{2,1},{3,2},{4,3},{5,4},{6,5},{7,6},{8,15},{9,8},{10,9... | collective-permute-start | bytes 1179656 | tf_op jit(solution)/shard_map/ppermute | solution.py:193
  87.1 16.9 %collective-permute-start.17 = (bf16[32,6,8,128]{3,2,1,0:T(8,128)(2,1)}, bf16[32,6,8,128]{3,2,1,0:T(8,128)(2,1)}, u32[]{:S(2)}, u32[]{:S(2)}) collective-permute-start(bf16[32,6,8,128]{3,2,1,0:T(8,128)(2,1)} %collective-permute-done.16.high), channel_id=1, source_target_pairs={{0,1},{1,2},{2,3},{3,4},{4,5},{5,6},{6,7},{7,0},{8,9},{9,10},{10,1... | collective-permute-start | bytes 1179656 | tf_op jit(solution)/shard_map/ppermute | solution.py:197
  92.0 17.0 %collective-permute-start.14 = (bf16[32,6,8,128]{3,2,1,0:T(8,128)(2,1)}, bf16[32,6,8,128]{3,2,1,0:T(8,128)(2,1)}, u32[]{:S(2)}, u32[]{:S(2)}) collective-permute-start(bf16[32,6,8,128]{3,2,1,0:T(8,128)(2,1)} %collective-permute-done.13.low), channel_id=1, source_target_pairs={{0,7},{1,0},{2,1},{3,2},{4,3},{5,4},{6,5},{7,6},{8,15},{9,8},{10,9... | collective-permute-start | bytes 1179656 | tf_op jit(solution)/shard_map/ppermute | solution.py:198
  96.3 24.5 %collective-permute-start.7 = (bf16[32,6,8,128]{3,2,1,0:T(8,128)(2,1)}, bf16[32,6,8,128]{3,2,1,0:T(8,128)(2,1)}, u32[]{:S(2)}, u32[]{:S(2)}) collective-permute-start(bf16[32,6,8,128]{3,2,1,0:T(8,128)(2,1)} %collective-permute-done.6.low), channel_id=1, source_target_pairs={{0,1},{1,2},{2,3},{3,4},{4,5},{5,6},{6,7},{7,0},{8,9},{9,10},{10,1... | collective-permute-start | bytes 1179656 | tf_op jit(solution)/shard_map/ppermute | solution.py:192
  100.6 16.9 %collective-permute-start.11 = (bf16[32,6,8,128]{3,2,1,0:T(8,128)(2,1)}, bf16[32,6,8,128]{3,2,1,0:T(8,128)(2,1)}, u32[]{:S(2)}, u32[]{:S(2)}) collective-permute-start(bf16[32,6,8,128]{3,2,1,0:T(8,128)(2,1)} %collective-permute-done.10.high), channel_id=1, source_target_pairs={{0,7},{1,0},{2,1},{3,2},{4,3},{5,4},{6,5},{7,6},{8,15},{9,8},{10,9... | collective-permute-start | bytes 1179656 | tf_op jit(solution)/shard_map/ppermute | solution.py:193
  104.1 40.4 %collective-permute-start.18 = (bf16[32,6,8,128]{3,2,1,0:T(8,128)(2,1)}, bf16[32,6,8,128]{3,2,1,0:T(8,128)(2,1)}, u32[]{:S(2)}, u32[]{:S(2)}) collective-permute-start(bf16[32,6,8,128]{3,2,1,0:T(8,128)(2,1)} %collective-permute-done.17.high), channel_id=1, source_target_pairs={{0,1},{1,2},{2,3},{3,4},{4,5},{5,6},{6,7},{7,0},{8,9},{9,10},{10,1... | collective-permute-start | bytes 1179656 | tf_op jit(solution)/shard_map/ppermute | solution.py:197
  109.0 40.3 %collective-permute-start.15 = (bf16[32,6,8,128]{3,2,1,0:T(8,128)(2,1)}, bf16[32,6,8,128]{3,2,1,0:T(8,128)(2,1)}, u32[]{:S(2)}, u32[]{:S(2)}) collective-permute-start(bf16[32,6,8,128]{3,2,1,0:T(8,128)(2,1)} %collective-permute-done.14.low), channel_id=1, source_target_pairs={{0,7},{1,0},{2,1},{3,2},{4,3},{5,4},{6,5},{7,6},{8,15},{9,8},{10,9... | collective-permute-start | bytes 1179656 | tf_op jit(solution)/shard_map/ppermute | solution.py:198
  117.4 36.6 %collective-permute-start.12 = (bf16[32,6,8,128]{3,2,1,0:T(8,128)(2,1)}, bf16[32,6,8,128]{3,2,1,0:T(8,128)(2,1)S(1)}, u32[]{:S(2)}, u32[]{:S(2)}) collective-permute-start(bf16[32,6,8,128]{3,2,1,0:T(8,128)(2,1)} %collective-permute-done.11.high), channel_id=1, source_target_pairs={{0,7},{1,0},{2,1},{3,2},{4,3},{5,4},{6,5},{7,6},{8,15},{9,8},{10,9... | collective-permute-start | bytes 1179656 | tf_op jit(solution)/shard_map/ppermute | solution.py:193
  120.8 33.2 %collective-permute-start.8 = (bf16[32,6,8,128]{3,2,1,0:T(8,128)(2,1)}, bf16[32,6,8,128]{3,2,1,0:T(8,128)(2,1)S(1)}, u32[]{:S(2)}, u32[]{:S(2)}) collective-permute-start(bf16[32,6,8,128]{3,2,1,0:T(8,128)(2,1)} %collective-permute-done.7.low), channel_id=1, source_target_pairs={{0,1},{1,2},{2,3},{3,4},{4,5},{5,6},{6,7},{7,0},{8,9},{9,10},{10,1... | collective-permute-start | bytes 1179656 | tf_op jit(solution)/shard_map/ppermute | solution.py:192

commit v2 on v1

v2 whole, which is shorter than its diff:
```python
import functools
import math

import jax
import jax.numpy as jnp
from jax import lax
from jax.experimental import pallas as pl
from jax.experimental.pallas import tpu as pltpu
from jax.sharding import PartitionSpec as P


BS = 128
POOL = 12
TILE = 8
NEG = -1e30
GRANT = 24 << 20


def pool_of(ancestors):
    flat = ancestors.reshape(-1)
    n = flat.shape[0]
    order = jnp.arange(n, dtype=jnp.int32)
    same = flat[:, None] == flat[None, :]
    repeat = jnp.any(same & (order[None, :] < order[:, None]), axis=1)
    first = ~repeat
    rank = jnp.sum((first[None, :] & (flat[None, :] < flat[:, None])).astype(jnp.int32), axis=1)
    slots = jnp.arange(BS, dtype=jnp.int32)
    hit = first[:, None] & (rank[:, None] == slots[None, :])
    pool = jnp.sum(jnp.where(hit, flat[:, None], 0), axis=0)
    return pool, rank.reshape(ancestors.shape)


def vmem():
    return pl.BlockSpec(memory_space=pltpu.VMEM)


def smem():
    return pl.BlockSpec(memory_space=pltpu.SMEM)


def pick_kernel(pools, me, held, out):
    mine = me[0]

    def one(s, carry):
        row = s ^ mine
        for i in range(POOL):
            out[s, i] = held[pools[row, i]]
        return carry

    lax.fori_loop(0, pools.shape[0], one, 0, unroll=2)


def pick(pools, me, held):
    return pl.pallas_call(
        pick_kernel,
        out_shape=jax.ShapeDtypeStruct((pools.shape[0], POOL, TILE, BS), held.dtype),
        in_specs=[smem(), smem(), vmem()],
        out_specs=vmem(),
        compiler_params=pltpu.CompilerParams(vmem_limit_bytes=GRANT),
        name="pick",
    )(pools, me, held)


def attend_kernel(scale, call, meta, q, own, far_k, far_v, _, out, keys, vals, held, sems):
    far = 8
    g = meta[call, 0]
    lane = lax.broadcasted_iota(jnp.int32, (1, BS), 1)
    keys[0:BS, :] = own[0:16, g].reshape(BS, BS)
    vals[0:BS, 0:BS] = own[16:32, g].reshape(BS, BS)
    bias = []
    for j in range(far):
        at = slice((j + 1) * BS, (j + 2) * BS)
        place = meta[call, 1 + j]
        keys[at, :] = far_k[0:16, place].reshape(BS, BS)
        vals[at, 0:BS] = far_v[0:16, place].reshape(BS, BS)
        bias.append(jnp.where(lane < meta[call, 9 + j], 0.0, NEG))
    vals[:, BS:] = jnp.ones((vals.shape[0], BS), jnp.bfloat16)

    tokens = 32
    rows = tokens * 8
    parts = BS // tokens
    token = lax.broadcasted_iota(jnp.int32, (rows, BS), 0) // 8
    offset = lax.broadcasted_iota(jnp.int32, (rows, BS), 1)
    inside = offset < meta[call, 17]
    heads = pl.ds(pl.multiple_of(g * 8, 8), 8)

    def leave(i):
        at = pl.ds(i * tokens, tokens)
        return pltpu.make_async_copy(held.at[at], out.at[at, heads], sems.at[i])

    for i in range(parts):
        at = slice(i * tokens, (i + 1) * tokens)
        qt = q[at, heads].astype(jnp.float32).reshape(rows, BS).astype(jnp.bfloat16)
        s = lax.dot_general(qt, keys[...], (((1,), (1,)), ((), ())), preferred_element_type=jnp.float32)
        s = [jnp.where((offset <= token + i * tokens) & inside, s[:, 0:BS], NEG)] + [
            s[:, (j + 1) * BS : (j + 2) * BS] + bias[j] for j in range(far)
        ]
        m = jnp.max(functools.reduce(jnp.maximum, s), axis=1, keepdims=True)
        p = jnp.concatenate([jnp.exp2((x - m) * scale).astype(jnp.bfloat16) for x in s], axis=1)
        o = jnp.dot(p, vals[...], preferred_element_type=jnp.float32)
        r = o[:, 0:BS] / o[:, BS:]
        held[at] = r.reshape(tokens, 8, BS).astype(out.dtype)
        leave(i).start()
    for i in range(parts):
        leave(i).wait()


def attend(call, meta, q, own, far_k, far_v, prev):
    scale = math.log2(math.e) / math.sqrt(BS)
    flops = 2 * 2 * 1024 * 1152 * 128
    hbm = pl.BlockSpec(memory_space=pl.ANY)
    return pl.pallas_call(
        functools.partial(attend_kernel, scale, call),
        out_shape=jax.ShapeDtypeStruct(prev.shape, q.dtype),
        in_specs=[smem(), vmem(), vmem(), vmem(), vmem(), hbm],
        out_specs=hbm,
        scratch_shapes=[
            pltpu.VMEM((9 * BS, BS), jnp.bfloat16),
            pltpu.VMEM((9 * BS, 2 * BS), jnp.bfloat16),
            pltpu.VMEM((BS, 8, BS), jnp.bfloat16),
            pltpu.SemaphoreType.DMA((4,)),
        ],
        input_output_aliases={5: 0},
        compiler_params=pltpu.CompilerParams(vmem_limit_bytes=GRANT),
        cost_estimate=pl.CostEstimate(flops=flops, bytes_accessed=2 << 20, transcendentals=1024 * 1152),
        name="attend",
    )(meta, q, own, far_k, far_v, prev)


def blank_kernel(out):
    pass


def blank(like):
    return pl.pallas_call(
        blank_kernel,
        out_shape=jax.ShapeDtypeStruct(like.shape, like.dtype),
        out_specs=pl.BlockSpec(memory_space=pl.ANY),
        name="blank",
    )()


def local(n_head, queries, keys, values, ancestors, lengths):
    return attention(n_head, queries, keys, values, ancestors, lengths)


def attention(n_head, queries, keys, values, ancestors, lengths):
    n_seq = 32
    place, level = lax.axis_index("seq"), lax.axis_index("head")
    pool, rank = pool_of(ancestors)
    pools = pool[None]
    bit = 1
    while bit < n_seq:
        other = lax.ppermute(pools, "seq", [(i, i ^ bit) for i in range(n_seq)])
        pools = jnp.concatenate([pools, other], axis=0)
        bit *= 2

    named = lax.dynamic_slice_in_dim(ancestors, level, 1)
    ranks = lax.dynamic_slice_in_dim(rank, level, 1)
    far_len = jnp.take(lengths, named)
    own_len = lax.dynamic_slice_in_dim(lengths, place * n_head + level, 1)[None]
    row = jnp.concatenate([ranks, far_len, own_len], axis=1)
    shifts = [0]
    for step in range(1, n_head // 2):
        shifts += [n_head - step, step]
    shifts.append(n_head // 2)
    heads = (level + jnp.array(shifts, jnp.int32)) % n_head
    meta = jnp.concatenate([heads[:, None], jnp.broadcast_to(row, (n_head, row.shape[1]))], axis=1)

    own = jnp.concatenate([keys, values], axis=0).reshape(32, TILE, n_head, BS).transpose(0, 2, 1, 3)
    held = lax.all_to_all(own.reshape(n_seq * n_head, TILE, BS), ("seq", "head"), 0, 0, tiled=True)
    picked = pick(pools, place.astype(jnp.int32)[None], held)
    far = lax.all_to_all(picked, "seq", 0, 0, tiled=True)
    far_k, far_v = far[:16], far[16:]

    up = [(i, (i + 1) % n_head) for i in range(n_head)]
    down = [(i, (i - 1) % n_head) for i in range(n_head)]
    out = blank(queries)
    out = attend(0, meta, queries, own, far_k, far_v, out)
    k_up = k_down = far_k
    v_up = v_down = far_v
    for step in range(1, n_head // 2 + 1):
        k_up = lax.ppermute(k_up, "head", up)
        v_down = lax.ppermute(v_down, "head", down)
        if step == n_head // 2:
            out = attend(n_head - 1, meta, queries, own, k_up, v_down, out)
            break
        v_up = lax.ppermute(v_up, "head", up)
        k_down = lax.ppermute(k_down, "head", down)
        out = attend(2 * step - 1, meta, queries, own, k_up, v_up, out)
        out = attend(2 * step, meta, queries, own, k_down, v_down, out)
    return out


def solution(mesh):
    placed = (
        P(("seq", "head"), None, None),
        P(("seq", "head"), None, None),
        P(("seq", "head"), None, None),
        P("seq", None),
        P(),
    )
    body = functools.partial(local, mesh.shape["head"])
    return jax.shard_map(
        body, mesh=mesh, in_specs=placed, out_specs=P(("seq", "head"), None, None), check_vma=False
    )
```

time: 159 us -> 145 us (0.912)
  starting transfers between devices: 50.3 us -> 41.8 us
  Pallas kernels: 39.7 us -> 34.3 us
  waiting for transfers between devices: 47.5 us -> 42.3 us
  blocking collectives: 16.1 us -> 19.9 us
    all_to_all x1 -> x0, waiting for transfers between devices: 8.64 us -> none  [attention(): high = lax.all_to_all(high, 'seq', 0, 0, tiled=True)]
    pallas_call x9, Pallas kernels: 39.7 us -> 34.3 us  [the longest x8 33 us: attend(): pl.pallas_call(functools.partial(attend_kernel, scale, call), out_shape=j...]
    ppermute x14, starting transfers between devices: 26.1 us -> 21.3 us  [the longest x4 11.7 us: attention(): v_down = lax.ppermute(v_down, 'head', down)]
    all_to_all x1, blocking collectives: 16.1 us -> 19.9 us  [attention(): far = lax.all_to_all(picked, 'seq', 0, 0, tiled=True)]
    all_to_all x1 -> x0, starting transfers between devices: 3.67 us -> none  [attention(): high = lax.all_to_all(high, 'seq', 0, 0, tiled=True)]
    ppermute x14, waiting for transfers between devices: 23.2 us -> 26.7 us  [the longest x3 11.5 us: attention(): v_up = lax.ppermute(v_up, 'head', up)]
  transfers between devices with their start and end apart: 21 -> 20, of which waited for: 12 -> 11; matrix products, arithmetic and copies ran while one was open for 2% -> 2% of each run, Pallas kernels for 21% -> 20%
where the time goes in v2:
time: 145 us; the launch traced here: 144 us
  waiting for transfers between devices  42.3 us (29%)
  starting transfers between devices  41.8 us (29%)
  Pallas kernels  34.3 us (24%)
  blocking collectives  19.9 us (14%)
  local copies, waits for them, and re-layouts  2.56 us (2%)
  other arithmetic  2.36 us (2%)
    pallas_call x8, Pallas kernels, attend(): pl.pallas_call(functools.partial(attend_kernel, scale, call), out_shape=j...  33 us
    all_to_all x1, blocking collectives, attention(): far = lax.all_to_all(picked, 'seq', 0, 0, tiled=True)  19.9 us
    all_to_all x1, starting transfers between devices, attention(): lax.all_to_all(own.reshape(n_seq * n_head, TILE, BS), ('seq', 'head'), 0,...  15.6 us
    ppermute x5, waiting for transfers between devices, attention(): other = lax.ppermute(pools, 'seq', [(i, i ^ bit) for i in range(n_seq)])  12.5 us
    ppermute x4, starting transfers between devices, attention(): v_down = lax.ppermute(v_down, 'head', down)  11.7 us
    ppermute x3, waiting for transfers between devices, attention(): v_up = lax.ppermute(v_up, 'head', up)  11.5 us
    ppermute x4, waiting for transfers between devices, attention(): k_up = lax.ppermute(k_up, 'head', up)  10.4 us
    ppermute x3, starting transfers between devices, attention(): k_down = lax.ppermute(k_down, 'head', down)  8.01 us
  transfers between devices with their start and end apart: 20, of which 11 were waited for; matrix products, arithmetic and copies ran while one was open for 2% of the time, Pallas kernels for 20%

profile of v2, /device:TPU:1, one launch (start us, length us, event | category | flops | bytes accessed | tf_op | source)
XLA Modules:
  0.0 143.6 jit_solution(1692906090192647563)
XLA Ops:
  0.0 1.1 pad_maximum_fusion
  1.1 0.9 copy.22
  2.0 15.6 %all-to-all-start = ((bf16[256,8,128]{2,1,0:T(8,128)(2,1)}), bf16[256,8,128]{2,1,0:T(8,128)(2,1)S(1)}, u32[]{:S(2)}, u32[]{:S(2)}) async-start(bf16[256,8,128]{2,1,0:T(8,128)(2,1)} %bitcast.9), calls=%async_computation | async-start | bytes 1048576 | tf_op jit(solution)/shard_map/all_to_all | solution.py:171
  17.7 0.1 eq.30
  17.7 0.2 fusion.1
  17.9 0.2 convert_reduce_fusion
  18.1 0.1 select_reduce_fusion
  18.2 2.2 %collective-permute-start = (s32[1,128]{1,0:T(1,128)S(1)}, s32[1,128]{1,0:T(1,128)S(1)}, u32[]{:S(2)}, u32[]{:S(2)}) collective-permute-start(s32[1,128]{1,0:T(1,128)S(1)} %bitcast.17), channel_id=1, source_target_pairs={{0,8},{8,0},{16,24},{24,16},{32,40},{40,32},{48,56},{56,48},{64,72... | collective-permute-start | bytes 1544 | tf_op jit(solution)/shard_map/ppermute | solution.py:154
  20.5 0.8 collective-permute-done
  21.3 0.0 collective-permute-start.1
  21.3 2.7 %collective-permute-done.1 = s32[2,128]{1,0:T(2,128)S(1)} collective-permute-done((s32[2,128]{1,0:T(2,128)S(1)}, s32[2,128]{1,0:T(2,128)S(1)}, u32[]{:S(2)}, u32[]{:S(2)}) %collective-permute-start.1) | collective-permute-done | bytes 1056 | tf_op jit(solution)/shard_map/ppermute | solution.py:154
  24.0 1.2 collective-permute-start.2
  25.2 3.1 %collective-permute-done.2 = s32[4,128]{1,0:T(4,128)S(1)} collective-permute-done((s32[4,128]{1,0:T(4,128)S(1)}, s32[4,128]{1,0:T(4,128)S(1)}, u32[]{:S(2)}, u32[]{:S(2)}) %collective-permute-start.2) | collective-permute-done | bytes 2080 | tf_op jit(solution)/shard_map/ppermute | solution.py:154
  28.4 0.1 collective-permute-start.3
  28.5 2.7 %collective-permute-done.3 = s32[8,128]{1,0:T(8,128)S(1)} collective-permute-done((s32[8,128]{1,0:T(8,128)S(1)}, s32[8,128]{1,0:T(8,128)S(1)}, u32[]{:S(2)}, u32[]{:S(2)}) %collective-permute-start.3) | collective-permute-done | bytes 4128 | tf_op jit(solution)/shard_map/ppermute | solution.py:154
  31.2 1.3 collective-permute-start.4
  32.6 3.0 %collective-permute-done.4 = s32[16,128]{1,0:T(8,128)S(1)} collective-permute-done((s32[16,128]{1,0:T(8,128)S(1)}, s32[16,128]{1,0:T(8,128)S(1)}, u32[]{:S(2)}, u32[]{:S(2)}) %collective-permute-start.4) | collective-permute-done | bytes 8224 | tf_op jit(solution)/shard_map/ppermute | solution.py:154
  35.6 3.1 %all-to-all-done.held = bf16[256,8,128]{2,1,0:T(8,128)(2,1)S(1)} async-done(((bf16[256,8,128]{2,1,0:T(8,128)(2,1)}), bf16[256,8,128]{2,1,0:T(8,128)(2,1)S(1)}, u32[]{:S(2)}, u32[]{:S(2)}) %all-to-all-start) | async-done | bytes 524320 | tf_op jit(solution)/shard_map/all_to_all | solution.py:171
  38.8 1.3 pick.1
  40.1 0.0 copy-start.3
  40.1 19.9 %all_to_all.10 = bf16[32,12,8,128]{3,2,1,0:T(8,128)(2,1)S(1)} all-to-all(bf16[32,12,8,128]{3,2,1,0:T(8,128)(2,1)S(1)} %pick.1), channel_id=1, replica_groups=mesh['seq'=32,'head'=8] {'seq'}, dimensions={0} | all-to-all | bytes 1572864 | tf_op jit(solution)/shard_map/all_to_all | solution.py:173
  60.0 0.1 fusion.6
  60.0 1.5 %collective-permute-start.5 = (bf16[16,12,8,128]{3,2,1,0:T(8,128)(2,1)S(1)}, bf16[16,12,8,128]{3,2,1,0:T(8,128)(2,1)S(1)}, u32[]{:S(2)}, u32[]{:S(2)}) collective-permute-start(bf16[16,12,8,128]{3,2,1,0:T(8,128)(2,1)S(1)} %get-tuple-element.6.far_k), channel_id=1, source_target_pairs={{0,1},{1,2},{2,3},{3,4},{4,5},{5,6},{6,7},{7,0},{8,9},{9,10},{10,1... | collective-permute-start | bytes 1179656 | tf_op jit(solution)/shard_map/ppermute | solution.py:183
  61.6 2.9 %collective-permute-start.9 = (bf16[16,12,8,128]{3,2,1,0:T(8,128)(2,1)S(1)}, bf16[16,12,8,128]{3,2,1,0:T(8,128)(2,1)}, u32[]{:S(2)}, u32[]{:S(2)}) collective-permute-start(bf16[16,12,8,128]{3,2,1,0:T(8,128)(2,1)S(1)} %get-tuple-element.5.far_v), channel_id=1, source_target_pairs={{0,7},{1,0},{2,1},{3,2},{4,3},{5,4},{6,5},{7,6},{8,15},{9,8},{10,9... | collective-permute-start | bytes 1179656 | tf_op jit(solution)/shard_map/ppermute | solution.py:184
  64.5 0.1 reshape.31
  64.6 0.0 collective-permute-start.16
  64.6 2.7 %collective-permute-start.13 = (bf16[16,12,8,128]{3,2,1,0:T(8,128)(2,1)S(1)}, bf16[16,12,8,128]{3,2,1,0:T(8,128)(2,1)}, u32[]{:S(2)}, u32[]{:S(2)}) collective-permute-start(bf16[16,12,8,128]{3,2,1,0:T(8,128)(2,1)S(1)} %get-tuple-element.6.far_k), channel_id=1, source_target_pairs={{0,7},{1,0},{2,1},{3,2},{4,3},{5,4},{6,5},{7,6},{8,15},{9,8},{10,9... | collective-permute-start | bytes 1179656 | tf_op jit(solution)/shard_map/ppermute | solution.py:189
  67.3 0.6 gather_fusion
  68.0 0.6 dynamic_slice.11
  68.6 5.4 %collective-permute-done.5.far_k = bf16[16,12,8,128]{3,2,1,0:T(8,128)(2,1)S(1)} collective-permute-done((bf16[16,12,8,128]{3,2,1,0:T(8,128)(2,1)S(1)}, bf16[16,12,8,128]{3,2,1,0:T(8,128)(2,1)S(1)}, u32[]{:S(2)}, u32[]{:S(2)}) %collective-permute-start.5) | collective-permute-done | bytes 393248 | tf_op jit(solution)/shard_map/ppermute | solution.py:183
  74.0 0.0 collective-permute-start.6
  74.0 0.0 collective-permute-done.9.far_v
  74.0 2.7 %collective-permute-start.10 = (bf16[16,12,8,128]{3,2,1,0:T(8,128)(2,1)}, bf16[16,12,8,128]{3,2,1,0:T(8,128)(2,1)}, u32[]{:S(2)}, u32[]{:S(2)}) collective-permute-start(bf16[16,12,8,128]{3,2,1,0:T(8,128)(2,1)} %collective-permute-done.9.far_v), channel_id=1, source_target_pairs={{0,7},{1,0},{2,1},{3,2},{4,3},{5,4},{6,5},{7,6},{8,15},{9,8},{10,9... | collective-permute-start | bytes 1179656 | tf_op jit(solution)/shard_map/ppermute | solution.py:184
  76.7 5.8 %collective-permute-done.16.far_v = bf16[16,12,8,128]{3,2,1,0:T(8,128)(2,1)} collective-permute-done((bf16[16,12,8,128]{3,2,1,0:T(8,128)(2,1)S(1)}, bf16[16,12,8,128]{3,2,1,0:T(8,128)(2,1)}, u32[]{:S(2)}, u32[]{:S(2)}) %collective-permute-start.16) | collective-permute-done | bytes 393248 | tf_op jit(solution)/shard_map/ppermute | solution.py:188
  82.5 0.0 collective-permute-start.17
  82.5 0.0 collective-permute-done.13.far_k
  82.5 2.7 %collective-permute-start.14 = (bf16[16,12,8,128]{3,2,1,0:T(8,128)(2,1)}, bf16[16,12,8,128]{3,2,1,0:T(8,128)(2,1)}, u32[]{:S(2)}, u32[]{:S(2)}) collective-permute-start(bf16[16,12,8,128]{3,2,1,0:T(8,128)(2,1)} %collective-permute-done.13.far_k), channel_id=1, source_target_pairs={{0,7},{1,0},{2,1},{3,2},{4,3},{5,4},{6,5},{7,6},{8,15},{9,8},{10,9... | collective-permute-start | bytes 1179656 | tf_op jit(solution)/shard_map/ppermute | solution.py:189
  85.2 0.7 add_bitcast_fusion
  85.9 0.1 pad.12.clone
  86.0 4.9 %collective-permute-done.6.far_k = bf16[16,12,8,128]{3,2,1,0:T(8,128)(2,1)} collective-permute-done((bf16[16,12,8,128]{3,2,1,0:T(8,128)(2,1)S(1)}, bf16[16,12,8,128]{3,2,1,0:T(8,128)(2,1)}, u32[]{:S(2)}, u32[]{:S(2)}) %collective-permute-start.6) | collective-permute-done | bytes 393248 | tf_op jit(solution)/shard_map/ppermute | solution.py:183
  91.0 0.0 collective-permute-start.7
  91.0 0.0 collective-permute-done.10.far_v
  91.0 2.7 %collective-permute-start.11 = (bf16[16,12,8,128]{3,2,1,0:T(8,128)(2,1)}, bf16[16,12,8,128]{3,2,1,0:T(8,128)(2,1)}, u32[]{:S(2)}, u32[]{:S(2)}) collective-permute-start(bf16[16,12,8,128]{3,2,1,0:T(8,128)(2,1)} %collective-permute-done.10.far_v), channel_id=1, source_target_pairs={{0,7},{1,0},{2,1},{3,2},{4,3},{5,4},{6,5},{7,6},{8,15},{9,8},{10,9... | collective-permute-start | bytes 1179656 | tf_op jit(solution)/shard_map/ppermute | solution.py:184
  93.7 0.1 copy.18
  93.7 5.6 %collective-permute-done.17.far_v = bf16[16,12,8,128]{3,2,1,0:T(8,128)(2,1)} collective-permute-done((bf16[16,12,8,128]{3,2,1,0:T(8,128)(2,1)}, bf16[16,12,8,128]{3,2,1,0:T(8,128)(2,1)}, u32[]{:S(2)}, u32[]{:S(2)}) %collective-permute-start.17) | collective-permute-done | bytes 393248 | tf_op jit(solution)/shard_map/ppermute | solution.py:188
  99.4 0.0 collective-permute-start.18
  99.4 0.0 collective-permute-done.14.far_k
  99.4 2.7 %collective-permute-start.15 = (bf16[16,12,8,128]{3,2,1,0:T(8,128)(2,1)}, bf16[16,12,8,128]{3,2,1,0:T(8,128)(2,1)}, u32[]{:S(2)}, u32[]{:S(2)}) collective-permute-start(bf16[16,12,8,128]{3,2,1,0:T(8,128)(2,1)} %collective-permute-done.14.far_k), channel_id=1, source_target_pairs={{0,7},{1,0},{2,1},{3,2},{4,3},{5,4},{6,5},{7,6},{8,15},{9,8},{10,9... | collective-permute-start | bytes 1179656 | tf_op jit(solution)/shard_map/ppermute | solution.py:189
  102.1 4.8 %collective-permute-done.11.far_v = bf16[16,12,8,128]{3,2,1,0:T(8,128)(2,1)} collective-permute-done((bf16[16,12,8,128]{3,2,1,0:T(8,128)(2,1)}, bf16[16,12,8,128]{3,2,1,0:T(8,128)(2,1)}, u32[]{:S(2)}, u32[]{:S(2)}) %collective-permute-start.11) | collective-permute-done | bytes 393248 | tf_op jit(solution)/shard_map/ppermute | solution.py:184
  106.9 3.4 %collective-permute-start.12 = (bf16[16,12,8,128]{3,2,1,0:T(8,128)(2,1)}, bf16[16,12,8,128]{3,2,1,0:T(8,128)(2,1)S(1)}, u32[]{:S(2)}, u32[]{:S(2)}) collective-permute-start(bf16[16,12,8,128]{3,2,1,0:T(8,128)(2,1)} %collective-permute-done.11.far_v), channel_id=1, source_target_pairs={{0,7},{1,0},{2,1},{3,2},{4,3},{5,4},{6,5},{7,6},{8,15},{9,8},{10,9... | collective-permute-start | bytes 1179656 | tf_op jit(solution)/shard_map/ppermute | solution.py:184
  110.3 0.0 collective-permute-done.7.far_k
  110.3 0.0 collective-permute-start.8
  110.3 3.9 %attend.8._ = bf16[128,64,128]{2,1,0:T(8,128)(2,1)} custom-call(s32[8,18]{1,0:T(8,128)S(1)} %pad_add_fusion.meta, bf16[128,64,128]{2,1,0:T(8,128)(2,1)S(1)} %copy-done, bf16[32,8,8,128]{3,2,1,0:T(8,128)(2,1)} %bitcast.15.clone.2.own, bf16[16,12,8,128]{3,2,1,0:T(8,128)(2,1)S(1)} %get-tuple-element.6.far_k, ...), custom_call_target="tpu_custom_call", output_to_operand_aliasing={{}: (5, {})} | custom-call | flops 603979776 | bytes 2097152 | tf_op jit(solution)/shard_map/attend/pallas_call | solution.py:112
  114.3 4.1 %attend.9._ = bf16[128,64,128]{2,1,0:T(8,128)(2,1)} custom-call(s32[8,18]{1,0:T(8,128)S(1)} %pad_add_fusion.meta, bf16[128,64,128]{2,1,0:T(8,128)(2,1)S(1)} %copy-done, bf16[32,8,8,128]{3,2,1,0:T(8,128)(2,1)} %bitcast.15.clone.2.own, bf16[16,12,8,128]{3,2,1,0:T(8,128)(2,1)S(1)} %collective-permute-done.5.far_k, ...), custom_call_target="tpu_custom_call", output_to_operand_aliasing={{}: (5, {})} | custom-call | flops 603979776 | bytes 2097152 | tf_op jit(solution)/shard_map/attend/pallas_call | solution.py:112
  118.3 4.2 %attend.10._ = bf16[128,64,128]{2,1,0:T(8,128)(2,1)} custom-call(s32[8,18]{1,0:T(8,128)S(1)} %pad_add_fusion.meta, bf16[128,64,128]{2,1,0:T(8,128)(2,1)S(1)} %copy-done, bf16[32,8,8,128]{3,2,1,0:T(8,128)(2,1)} %bitcast.15.clone.2.own, bf16[16,12,8,128]{3,2,1,0:T(8,128)(2,1)} %collective-permute-done.13.far_k, ...), custom_call_target="tpu_custom_call", output_to_operand_aliasing={{}: (5, {})} | custom-call | flops 603979776 | bytes 2097152 | tf_op jit(solution)/shard_map/attend/pallas_call | solution.py:112
  122.5 4.2 %attend.11._ = bf16[128,64,128]{2,1,0:T(8,128)(2,1)} custom-call(s32[8,18]{1,0:T(8,128)S(1)} %pad_add_fusion.meta, bf16[128,64,128]{2,1,0:T(8,128)(2,1)S(1)} %copy-done, bf16[32,8,8,128]{3,2,1,0:T(8,128)(2,1)} %bitcast.15.clone.2.own, bf16[16,12,8,128]{3,2,1,0:T(8,128)(2,1)} %collective-permute-done.6.far_k, ...), custom_call_target="tpu_custom_call", output_to_operand_aliasing={{}: (5, {})} | custom-call | flops 603979776 | bytes 2097152 | tf_op jit(solution)/shard_map/attend/pallas_call | solution.py:112
  126.7 4.2 %attend.12._ = bf16[128,64,128]{2,1,0:T(8,128)(2,1)} custom-call(s32[8,18]{1,0:T(8,128)S(1)} %pad_add_fusion.meta, bf16[128,64,128]{2,1,0:T(8,128)(2,1)S(1)} %copy-done, bf16[32,8,8,128]{3,2,1,0:T(8,128)(2,1)} %bitcast.15.clone.2.own, bf16[16,12,8,128]{3,2,1,0:T(8,128)(2,1)} %collective-permute-done.14.far_k, ...), custom_call_target="tpu_custom_call", output_to_operand_aliasing={{}: (5, {})} | custom-call | flops 603979776 | bytes 2097152 | tf_op jit(solution)/shard_map/attend/pallas_call | solution.py:112
  130.8 0.0 collective-permute-done.18.far_v
  130.8 4.4 %attend.13._ = bf16[128,64,128]{2,1,0:T(8,128)(2,1)} custom-call(s32[8,18]{1,0:T(8,128)S(1)} %pad_add_fusion.meta, bf16[128,64,128]{2,1,0:T(8,128)(2,1)S(1)} %copy-done, bf16[32,8,8,128]{3,2,1,0:T(8,128)(2,1)} %bitcast.15.clone.2.own, bf16[16,12,8,128]{3,2,1,0:T(8,128)(2,1)} %collective-permute-done.7.far_k, ...), custom_call_target="tpu_custom_call", output_to_operand_aliasing={{}: (5, {})} | custom-call | flops 603979776 | bytes 2097152 | tf_op jit(solution)/shard_map/attend/pallas_call | solution.py:112
  135.3 0.0 collective-permute-done.15.far_k
  135.3 4.2 %attend.14._ = bf16[128,64,128]{2,1,0:T(8,128)(2,1)} custom-call(s32[8,18]{1,0:T(8,128)S(1)} %pad_add_fusion.meta, bf16[128,64,128]{2,1,0:T(8,128)(2,1)S(1)} %copy-done, bf16[32,8,8,128]{3,2,1,0:T(8,128)(2,1)} %bitcast.15.clone.2.own, bf16[16,12,8,128]{3,2,1,0:T(8,128)(2,1)} %collective-permute-done.15.far_k, ...), custom_call_target="tpu_custom_call", output_to_operand_aliasing={{}: (5, {})} | custom-call | flops 603979776 | bytes 2097152 | tf_op jit(solution)/shard_map/attend/pallas_call | solution.py:112
  139.5 0.0 collective-permute-done.12.far_v
  139.5 0.0 collective-permute-done.8.far_k
  139.5 3.9 %attend.15 = bf16[128,64,128]{2,1,0:T(8,128)(2,1)} custom-call(s32[8,18]{1,0:T(8,128)S(1)} %pad_add_fusion.meta, bf16[128,64,128]{2,1,0:T(8,128)(2,1)S(1)} %copy-done, bf16[32,8,8,128]{3,2,1,0:T(8,128)(2,1)} %bitcast.15.clone.2.own, bf16[16,12,8,128]{3,2,1,0:T(8,128)(2,1)S(1)} %collective-permute-done.8.far_k, ...), custom_call_target="tpu_custom_call", output_to_operand_aliasing={{}: (5, {})} | custom-call | flops 603979776 | bytes 2097152 | tf_op jit(solution)/shard_map/attend/pallas_call | solution.py:112
  (20 shorter events, 0.1 us)
Async XLA Ops:
  0.0 17.6 %copy-start.2 = (s32[8,8]{1,0:T(8,128)S(1)}, s32[8,8]{1,0:T(8,128)}, u32[]{:S(2)}) copy-start(s32[8,8]{1,0:T(8,128)} %param.9) | copy-start | bytes 772
  2.0 36.8 %all-to-all-start = ((bf16[256,8,128]{2,1,0:T(8,128)(2,1)}), bf16[256,8,128]{2,1,0:T(8,128)(2,1)S(1)}, u32[]{:S(2)}, u32[]{:S(2)}) async-start(bf16[256,8,128]{2,1,0:T(8,128)(2,1)} %bitcast.9), calls=%async_computation | async-start | bytes 1048576 | tf_op jit(solution)/shard_map/all_to_all | solution.py:171
  18.2 3.0 %collective-permute-start = (s32[1,128]{1,0:T(1,128)S(1)}, s32[1,128]{1,0:T(1,128)S(1)}, u32[]{:S(2)}, u32[]{:S(2)}) collective-permute-start(s32[1,128]{1,0:T(1,128)S(1)} %bitcast.17), channel_id=1, source_target_pairs={{0,8},{8,0},{16,24},{24,16},{32,40},{40,32},{48,56},{56,48},{64,72... | collective-permute-start | bytes 1544 | tf_op jit(solution)/shard_map/ppermute | solution.py:154
  21.3 2.7 %collective-permute-start.1 = (s32[2,128]{1,0:T(2,128)S(1)}, s32[2,128]{1,0:T(2,128)S(1)}, u32[]{:S(2)}, u32[]{:S(2)}) collective-permute-start(s32[2,128]{1,0:T(2,128)S(1)} %pad_add_fusion.3), channel_id=1, source_target_pairs={{0,16},{8,24},{16,0},{24,8},{32,48},{40,56},{48,32},{56,40},{64,80... | collective-permute-start | bytes 3080 | tf_op jit(solution)/shard_map/ppermute | solution.py:154
  24.0 4.3 %collective-permute-start.2 = (s32[4,128]{1,0:T(4,128)S(1)}, s32[4,128]{1,0:T(4,128)S(1)}, u32[]{:S(2)}, u32[]{:S(2)}) collective-permute-start(s32[4,128]{1,0:T(4,128)S(1)} %pad_add_fusion.2), channel_id=1, source_target_pairs={{0,32},{8,40},{16,48},{24,56},{32,0},{40,8},{48,16},{56,24},{64,96... | collective-permute-start | bytes 6152 | tf_op jit(solution)/shard_map/ppermute | solution.py:154
  28.4 2.8 %collective-permute-start.3 = (s32[8,128]{1,0:T(8,128)S(1)}, s32[8,128]{1,0:T(8,128)S(1)}, u32[]{:S(2)}, u32[]{:S(2)}) collective-permute-start(s32[8,128]{1,0:T(8,128)S(1)} %pad_add_fusion.1), channel_id=1, source_target_pairs={{0,64},{8,72},{16,80},{24,88},{32,96},{40,104},{48,112},{56,120},{... | collective-permute-start | bytes 12296 | tf_op jit(solution)/shard_map/ppermute | solution.py:154
  31.2 4.4 %collective-permute-start.4 = (s32[16,128]{1,0:T(8,128)S(1)}, s32[16,128]{1,0:T(8,128)S(1)}, u32[]{:S(2)}, u32[]{:S(2)}) collective-permute-start(s32[16,128]{1,0:T(8,128)S(1)} %concatenate.34), channel_id=1, source_target_pairs={{0,128},{8,136},{16,144},{24,152},{32,160},{40,168},{48,176},{56,1... | collective-permute-start | bytes 24584 | tf_op jit(solution)/shard_map/ppermute | solution.py:154
  38.8 28.6 %copy-start.1 = (s32[256]{0:T(256)S(1)}, s32[256]{0:T(256)}, u32[]{:S(2)}) copy-start(s32[256]{0:T(256)} %param.10) | copy-start | bytes 3076
  40.1 53.6 %copy-start.3 = (s32[8]{0:T(128)S(1)}, s32[8]{0:T(128)}, u32[]{:S(2)}) copy-start(s32[8]{0:T(128)} %constant.45.clone) | copy-start | bytes 100
  60.0 50.3 %copy-start = (bf16[128,64,128]{2,1,0:T(8,128)(2,1)S(1)}, bf16[128,64,128]{2,1,0:T(8,128)(2,1)}, u32[]{:S(2)}) copy-start(bf16[128,64,128]{2,1,0:T(8,128)(2,1)} %q.15) | copy-start | bytes 6291460
  60.0 14.0 %collective-permute-start.5 = (bf16[16,12,8,128]{3,2,1,0:T(8,128)(2,1)S(1)}, bf16[16,12,8,128]{3,2,1,0:T(8,128)(2,1)S(1)}, u32[]{:S(2)}, u32[]{:S(2)}) collective-permute-start(bf16[16,12,8,128]{3,2,1,0:T(8,128)(2,1)S(1)} %get-tuple-element.6.far_k), channel_id=1, source_target_pairs={{0,1},{1,2},{2,3},{3,4},{4,5},{5,6},{6,7},{7,0},{8,9},{9,10},{10,1... | collective-permute-start | bytes 1179656 | tf_op jit(solution)/shard_map/ppermute | solution.py:183
  61.6 12.4 %collective-permute-start.9 = (bf16[16,12,8,128]{3,2,1,0:T(8,128)(2,1)S(1)}, bf16[16,12,8,128]{3,2,1,0:T(8,128)(2,1)}, u32[]{:S(2)}, u32[]{:S(2)}) collective-permute-start(bf16[16,12,8,128]{3,2,1,0:T(8,128)(2,1)S(1)} %get-tuple-element.5.far_v), channel_id=1, source_target_pairs={{0,7},{1,0},{2,1},{3,2},{4,3},{5,4},{6,5},{7,6},{8,15},{9,8},{10,9... | collective-permute-start | bytes 1179656 | tf_op jit(solution)/shard_map/ppermute | solution.py:184
  64.6 17.9 %collective-permute-start.16 = (bf16[16,12,8,128]{3,2,1,0:T(8,128)(2,1)S(1)}, bf16[16,12,8,128]{3,2,1,0:T(8,128)(2,1)}, u32[]{:S(2)}, u32[]{:S(2)}) collective-permute-start(bf16[16,12,8,128]{3,2,1,0:T(8,128)(2,1)S(1)} %get-tuple-element.5.far_v), channel_id=1, source_target_pairs={{0,1},{1,2},{2,3},{3,4},{4,5},{5,6},{6,7},{7,0},{8,9},{9,10},{10,1... | collective-permute-start | bytes 1179656 | tf_op jit(solution)/shard_map/ppermute | solution.py:188
  64.6 17.9 %collective-permute-start.13 = (bf16[16,12,8,128]{3,2,1,0:T(8,128)(2,1)S(1)}, bf16[16,12,8,128]{3,2,1,0:T(8,128)(2,1)}, u32[]{:S(2)}, u32[]{:S(2)}) collective-permute-start(bf16[16,12,8,128]{3,2,1,0:T(8,128)(2,1)S(1)} %get-tuple-element.6.far_k), channel_id=1, source_target_pairs={{0,7},{1,0},{2,1},{3,2},{4,3},{5,4},{6,5},{7,6},{8,15},{9,8},{10,9... | collective-permute-start | bytes 1179656 | tf_op jit(solution)/shard_map/ppermute | solution.py:189
  74.0 17.0 %collective-permute-start.6 = (bf16[16,12,8,128]{3,2,1,0:T(8,128)(2,1)S(1)}, bf16[16,12,8,128]{3,2,1,0:T(8,128)(2,1)}, u32[]{:S(2)}, u32[]{:S(2)}) collective-permute-start(bf16[16,12,8,128]{3,2,1,0:T(8,128)(2,1)S(1)} %collective-permute-done.5.far_k), channel_id=1, source_target_pairs={{0,1},{1,2},{2,3},{3,4},{4,5},{5,6},{6,7},{7,0},{8,9},{9,10},{10,1... | collective-permute-start | bytes 1179656 | tf_op jit(solution)/shard_map/ppermute | solution.py:183
  74.0 17.0 %collective-permute-start.10 = (bf16[16,12,8,128]{3,2,1,0:T(8,128)(2,1)}, bf16[16,12,8,128]{3,2,1,0:T(8,128)(2,1)}, u32[]{:S(2)}, u32[]{:S(2)}) collective-permute-start(bf16[16,12,8,128]{3,2,1,0:T(8,128)(2,1)} %collective-permute-done.9.far_v), channel_id=1, source_target_pairs={{0,7},{1,0},{2,1},{3,2},{4,3},{5,4},{6,5},{7,6},{8,15},{9,8},{10,9... | collective-permute-start | bytes 1179656 | tf_op jit(solution)/shard_map/ppermute | solution.py:184
  82.5 16.9 %collective-permute-start.17 = (bf16[16,12,8,128]{3,2,1,0:T(8,128)(2,1)}, bf16[16,12,8,128]{3,2,1,0:T(8,128)(2,1)}, u32[]{:S(2)}, u32[]{:S(2)}) collective-permute-start(bf16[16,12,8,128]{3,2,1,0:T(8,128)(2,1)} %collective-permute-done.16.far_v), channel_id=1, source_target_pairs={{0,1},{1,2},{2,3},{3,4},{4,5},{5,6},{6,7},{7,0},{8,9},{9,10},{10,1... | collective-permute-start | bytes 1179656 | tf_op jit(solution)/shard_map/ppermute | solution.py:188
  82.5 16.9 %collective-permute-start.14 = (bf16[16,12,8,128]{3,2,1,0:T(8,128)(2,1)}, bf16[16,12,8,128]{3,2,1,0:T(8,128)(2,1)}, u32[]{:S(2)}, u32[]{:S(2)}) collective-permute-start(bf16[16,12,8,128]{3,2,1,0:T(8,128)(2,1)} %collective-permute-done.13.far_k), channel_id=1, source_target_pairs={{0,7},{1,0},{2,1},{3,2},{4,3},{5,4},{6,5},{7,6},{8,15},{9,8},{10,9... | collective-permute-start | bytes 1179656 | tf_op jit(solution)/shard_map/ppermute | solution.py:189
  91.0 19.3 %collective-permute-start.7 = (bf16[16,12,8,128]{3,2,1,0:T(8,128)(2,1)}, bf16[16,12,8,128]{3,2,1,0:T(8,128)(2,1)}, u32[]{:S(2)}, u32[]{:S(2)}) collective-permute-start(bf16[16,12,8,128]{3,2,1,0:T(8,128)(2,1)} %collective-permute-done.6.far_k), channel_id=1, source_target_pairs={{0,1},{1,2},{2,3},{3,4},{4,5},{5,6},{6,7},{7,0},{8,9},{9,10},{10,1... | collective-permute-start | bytes 1179656 | tf_op jit(solution)/shard_map/ppermute | solution.py:183
  91.0 15.9 %collective-permute-start.11 = (bf16[16,12,8,128]{3,2,1,0:T(8,128)(2,1)}, bf16[16,12,8,128]{3,2,1,0:T(8,128)(2,1)}, u32[]{:S(2)}, u32[]{:S(2)}) collective-permute-start(bf16[16,12,8,128]{3,2,1,0:T(8,128)(2,1)} %collective-permute-done.10.far_v), channel_id=1, source_target_pairs={{0,7},{1,0},{2,1},{3,2},{4,3},{5,4},{6,5},{7,6},{8,15},{9,8},{10,9... | collective-permute-start | bytes 1179656 | tf_op jit(solution)/shard_map/ppermute | solution.py:184
  99.4 31.4 %collective-permute-start.18 = (bf16[16,12,8,128]{3,2,1,0:T(8,128)(2,1)}, bf16[16,12,8,128]{3,2,1,0:T(8,128)(2,1)}, u32[]{:S(2)}, u32[]{:S(2)}) collective-permute-start(bf16[16,12,8,128]{3,2,1,0:T(8,128)(2,1)} %collective-permute-done.17.far_v), channel_id=1, source_target_pairs={{0,1},{1,2},{2,3},{3,4},{4,5},{5,6},{6,7},{7,0},{8,9},{9,10},{10,1... | collective-permute-start | bytes 1179656 | tf_op jit(solution)/shard_map/ppermute | solution.py:188
  99.4 35.9 %collective-permute-start.15 = (bf16[16,12,8,128]{3,2,1,0:T(8,128)(2,1)}, bf16[16,12,8,128]{3,2,1,0:T(8,128)(2,1)}, u32[]{:S(2)}, u32[]{:S(2)}) collective-permute-start(bf16[16,12,8,128]{3,2,1,0:T(8,128)(2,1)} %collective-permute-done.14.far_k), channel_id=1, source_target_pairs={{0,7},{1,0},{2,1},{3,2},{4,3},{5,4},{6,5},{7,6},{8,15},{9,8},{10,9... | collective-permute-start | bytes 1179656 | tf_op jit(solution)/shard_map/ppermute | solution.py:189
  106.9 32.6 %collective-permute-start.12 = (bf16[16,12,8,128]{3,2,1,0:T(8,128)(2,1)}, bf16[16,12,8,128]{3,2,1,0:T(8,128)(2,1)S(1)}, u32[]{:S(2)}, u32[]{:S(2)}) collective-permute-start(bf16[16,12,8,128]{3,2,1,0:T(8,128)(2,1)} %collective-permute-done.11.far_v), channel_id=1, source_target_pairs={{0,7},{1,0},{2,1},{3,2},{4,3},{5,4},{6,5},{7,6},{8,15},{9,8},{10,9... | collective-permute-start | bytes 1179656 | tf_op jit(solution)/shard_map/ppermute | solution.py:184
  110.3 29.2 %collective-permute-start.8 = (bf16[16,12,8,128]{3,2,1,0:T(8,128)(2,1)}, bf16[16,12,8,128]{3,2,1,0:T(8,128)(2,1)S(1)}, u32[]{:S(2)}, u32[]{:S(2)}) collective-permute-start(bf16[16,12,8,128]{3,2,1,0:T(8,128)(2,1)} %collective-permute-done.7.far_k), channel_id=1, source_target_pairs={{0,1},{1,2},{2,3},{3,4},{4,5},{5,6},{6,7},{7,0},{8,9},{9,10},{10,1... | collective-permute-start | bytes 1179656 | tf_op jit(solution)/shard_map/ppermute | solution.py:183

commit v3 on v2

--- a/solution.py
+++ b/solution.py
@@ -11,6 +11,9 @@
 
 BS = 128
 POOL = 12
+PIECES = BS // 8
+ALL = POOL * PIECES
+ROOM = 152
 TILE = 8
 NEG = -1e30
 GRANT = 24 << 20
@@ -61,19 +64,76 @@
     )(pools, me, held)
 
 
-def attend_kernel(scale, call, meta, q, own, far_k, far_v, _, out, keys, vals, held, sems):
+def pack_kernel(offs, far, main_k, main_v, rest, all_k, all_v):
+    zero = jnp.zeros(all_k.shape, all_k.dtype)
+    all_k[...] = zero
+    all_v[...] = zero
+    for i in range(POOL):
+        at = pl.ds(offs[i], PIECES)
+        all_k[at] = far[0:PIECES, i]
+        all_v[at] = far[PIECES : 2 * PIECES, i]
+    all_k[pl.ds(offs[POOL], PIECES)] = zero[0:PIECES]
+    all_v[pl.ds(offs[POOL], PIECES)] = zero[0:PIECES]
+    main_k[...] = all_k[0:ROOM]
+    main_v[...] = all_v[0:ROOM]
+    rest[0] = all_k[ROOM:ALL]
+    rest[1] = all_v[ROOM:ALL]
+
+
+def pack(offs, far):
+    part = jax.ShapeDtypeStruct((ROOM, TILE, BS), far.dtype)
+    rest = jax.ShapeDtypeStruct((2, ALL - ROOM, TILE, BS), far.dtype)
+    work = pltpu.VMEM((ALL + PIECES, TILE, BS), far.dtype)
+    return pl.pallas_call(
+        pack_kernel,
+        out_shape=(part, part, rest),
+        in_specs=[smem(), vmem()],
+        out_specs=(vmem(), vmem(), vmem()),
+        scratch_shapes=[work, work],
+        compiler_params=pltpu.CompilerParams(vmem_limit_bytes=GRANT),
+        name="pack",
+    )(offs, far)
+
+
+def attend_kernel(scale, call, meta, q, own, far_k, far_v, rest, _, out, keys, vals, held, all_k, all_v, sems):
     far = 8
     g = meta[call, 0]
+    over = meta[call, 18]
     lane = lax.broadcasted_iota(jnp.int32, (1, BS), 1)
     keys[0:BS, :] = own[0:16, g].reshape(BS, BS)
     vals[0:BS, 0:BS] = own[16:32, g].reshape(BS, BS)
+
+    def start(j, room):
+        return jnp.minimum(meta[call, 1 + j], room - PIECES)
+
+    def load(from_k, from_v, room):
+        for j in range(far):
+            at = slice((j + 1) * BS, (j + 2) * BS)
+            pieces = pl.ds(start(j, room), PIECES)
+            keys[at, :] = from_k[pieces].reshape(BS, BS)
+            vals[at, 0:BS] = from_v[pieces].reshape(BS, BS)
+
+    @pl.when(over == 0)
+    def _():
+        load(far_k, far_v, ROOM)
+
+    @pl.when(over != 0)
+    def _():
+        more_k = pltpu.make_async_copy(rest.at[g, 0], all_k.at[ROOM:ALL], sems.at[4])
+        more_v = pltpu.make_async_copy(rest.at[g, 1], all_v.at[ROOM:ALL], sems.at[5])
+        more_k.start()
+        more_v.start()
+        all_k[0:ROOM] = far_k[...]
+        all_v[0:ROOM] = far_v[...]
+        more_k.wait()
+        more_v.wait()
+        load(all_k, all_v, ALL)
+
+    room = jnp.where(over != 0, ALL, ROOM)
     bias = []
     for j in range(far):
-        at = slice((j + 1) * BS, (j + 2) * BS)
-        place = meta[call, 1 + j]
-        keys[at, :] = far_k[0:16, place].reshape(BS, BS)
-        vals[at, 0:BS] = far_v[0:16, place].reshape(BS, BS)
-        bias.append(jnp.where(lane < meta[call, 9 + j], 0.0, NEG))
+        low = (meta[call, 1 + j] - start(j, room)) * TILE
+        bias.append(jnp.where((lane >= low) & (lane < low + meta[call, 9 + j]), 0.0, NEG))
     vals[:, BS:] = jnp.ones((vals.shape[0], BS), jnp.bfloat16)
 
     tokens = 32
@@ -105,36 +165,38 @@
         leave(i).wait()
 
 
-def attend(call, meta, q, own, far_k, far_v, prev):
+def attend(call, meta, q, own, far_k, far_v, rest, prev):
     scale = math.log2(math.e) / math.sqrt(BS)
     flops = 2 * 2 * 1024 * 1152 * 128
     hbm = pl.BlockSpec(memory_space=pl.ANY)
     return pl.pallas_call(
         functools.partial(attend_kernel, scale, call),
         out_shape=jax.ShapeDtypeStruct(prev.shape, q.dtype),
-        in_specs=[smem(), vmem(), vmem(), vmem(), vmem(), hbm],
+        in_specs=[smem(), vmem(), vmem(), vmem(), vmem(), hbm, hbm],
         out_specs=hbm,
         scratch_shapes=[
             pltpu.VMEM((9 * BS, BS), jnp.bfloat16),
             pltpu.VMEM((9 * BS, 2 * BS), jnp.bfloat16),
             pltpu.VMEM((BS, 8, BS), jnp.bfloat16),
-            pltpu.SemaphoreType.DMA((4,)),
+            pltpu.VMEM((ALL, TILE, BS), jnp.bfloat16),
+            pltpu.VMEM((ALL, TILE, BS), jnp.bfloat16),
+            pltpu.SemaphoreType.DMA((6,)),
         ],
-        input_output_aliases={5: 0},
+        input_output_aliases={6: 0},
         compiler_params=pltpu.CompilerParams(vmem_limit_bytes=GRANT),
         cost_estimate=pl.CostEstimate(flops=flops, bytes_accessed=2 << 20, transcendentals=1024 * 1152),
         name="attend",
-    )(meta, q, own, far_k, far_v, prev)
+    )(meta, q, own, far_k, far_v, rest, prev)
 
 
 def blank_kernel(out):
     pass
 
 
-def blank(like):
+def blank(shape, dtype):
     return pl.pallas_call(
         blank_kernel,
-        out_shape=jax.ShapeDtypeStruct(like.shape, like.dtype),
+        out_shape=jax.ShapeDtypeStruct(shape, dtype),
         out_specs=pl.BlockSpec(memory_space=pl.ANY),
         name="blank",
     )()
@@ -159,7 +221,12 @@
     ranks = lax.dynamic_slice_in_dim(rank, level, 1)
     far_len = jnp.take(lengths, named)
     own_len = lax.dynamic_slice_in_dim(lengths, place * n_head + level, 1)[None]
-    row = jnp.concatenate([ranks, far_len, own_len], axis=1)
+    count = (jnp.take(lengths, pool[:POOL]) + TILE - 1) // TILE
+    slot = jnp.arange(POOL + 1, dtype=jnp.int32)
+    offs = jnp.sum(jnp.where(slot[None, :POOL] < slot[:, None], count[None, :], 0), axis=1)
+    over = offs[POOL] > ROOM
+    far_off = jnp.sum(jnp.where(ranks.reshape(-1, 1) == slot[None, :POOL], offs[None, :POOL], 0), axis=1)[None]
+    row = jnp.concatenate([far_off, far_len, own_len, over.astype(jnp.int32).reshape(1, 1)], axis=1)
     shifts = [0]
     for step in range(1, n_head // 2):
         shifts += [n_head - step, step]
@@ -171,24 +238,31 @@
     held = lax.all_to_all(own.reshape(n_seq * n_head, TILE, BS), ("seq", "head"), 0, 0, tiled=True)
     picked = pick(pools, place.astype(jnp.int32)[None], held)
     far = lax.all_to_all(picked, "seq", 0, 0, tiled=True)
-    far_k, far_v = far[:16], far[16:]
+    far_k, far_v, rest = pack(offs, far)
+    shape = (n_head,) + rest.shape
+    rest = lax.cond(
+        over,
+        lambda r: lax.all_to_all(jnp.broadcast_to(r[None], shape), "head", 0, 0, tiled=True),
+        lambda r: blank(shape, r.dtype),
+        rest,
+    )
 
     up = [(i, (i + 1) % n_head) for i in range(n_head)]
     down = [(i, (i - 1) % n_head) for i in range(n_head)]
-    out = blank(queries)
-    out = attend(0, meta, queries, own, far_k, far_v, out)
+    out = blank(queries.shape, queries.dtype)
+    out = attend(0, meta, queries, own, far_k, far_v, rest, out)
     k_up = k_down = far_k
     v_up = v_down = far_v
     for step in range(1, n_head // 2 + 1):
         k_up = lax.ppermute(k_up, "head", up)
         v_down = lax.ppermute(v_down, "head", down)
         if step == n_head // 2:
-            out = attend(n_head - 1, meta, queries, own, k_up, v_down, out)
+            out = attend(n_head - 1, meta, queries, own, k_up, v_down, rest, out)
             break
         v_up = lax.ppermute(v_up, "head", up)
         k_down = lax.ppermute(k_down, "head", down)
-        out = attend(2 * step - 1, meta, queries, own, k_up, v_up, out)
-        out = attend(2 * step, meta, queries, own, k_down, v_down, out)
+        out = attend(2 * step - 1, meta, queries, own, k_up, v_up, rest, out)
+        out = attend(2 * step, meta, queries, own, k_down, v_down, rest, out)
     return out
 
 

time: 145 us -> 134 us (0.924)
  blocking collectives: 19.9 us -> 0 us
  starting transfers between devices: 41.8 us -> 46 us
  local copies, waits for them, and re-layouts: 2.56 us -> 4.83 us
  Pallas kernels: 34.3 us -> 35.8 us
    all_to_all x1 -> x0, blocking collectives: 19.9 us -> none  [attention(): far = lax.all_to_all(picked, 'seq', 0, 0, tiled=True)]
    all_to_all x0 -> x1, waiting for transfers between devices: none -> 10.7 us  [attention(): far = lax.all_to_all(picked, 'seq', 0, 0, tiled=True)]
    all_to_all x0 -> x1, starting transfers between devices: none -> 5.89 us  [attention(): far = lax.all_to_all(picked, 'seq', 0, 0, tiled=True)]
    ppermute x4, waiting for transfers between devices: 4.82 us -> 0.01 us  [attention(): v_down = lax.ppermute(v_down, 'head', down)]
    ppermute x3, waiting for transfers between devices: 11.5 us -> 6.94 us  [attention(): v_up = lax.ppermute(v_up, 'head', up)]
    ppermute x4, starting transfers between devices: 11.7 us -> 9.81 us  [attention(): v_down = lax.ppermute(v_down, 'head', down)]
  transfers between devices with their start and end apart: 20 -> 21, of which waited for: 11 -> 11; matrix products, arithmetic and copies ran while one was open for 2% -> 3% of each run, Pallas kernels for 20% -> 22%
where the time goes in v3:
time: 134 us; the launch traced here: 133 us
  starting transfers between devices  46 us (34%)
  waiting for transfers between devices  42.2 us (31%)
  Pallas kernels  35.8 us (27%)
  local copies, waits for them, and re-layouts  4.83 us (4%)
  other arithmetic  2.66 us (2%)
    pallas_call x8, Pallas kernels, attend(): pl.pallas_call(functools.partial(attend_kernel, scale, call), out_shape=j...  32.8 us
    all_to_all x1, starting transfers between devices, attention(): lax.all_to_all(own.reshape(n_seq * n_head, TILE, BS), ('seq', 'head'), 0,...  15.6 us
    ppermute x5, waiting for transfers between devices, attention(): other = lax.ppermute(pools, 'seq', [(i, i ^ bit) for i in range(n_seq)])  12.5 us
    all_to_all x1, waiting for transfers between devices, attention(): far = lax.all_to_all(picked, 'seq', 0, 0, tiled=True)  10.7 us
    ppermute x4, starting transfers between devices, attention(): v_down = lax.ppermute(v_down, 'head', down)  9.81 us
    ppermute x4, waiting for transfers between devices, attention(): k_up = lax.ppermute(k_up, 'head', up)  8.97 us
    ppermute x3, starting transfers between devices, attention(): k_down = lax.ppermute(k_down, 'head', down)  8.21 us
    ppermute x3, waiting for transfers between devices, attention(): v_up = lax.ppermute(v_up, 'head', up)  6.94 us
  transfers between devices with their start and end apart: 21, of which 11 were waited for; matrix products, arithmetic and copies ran while one was open for 3% of the time, Pallas kernels for 22%

profile of v3, /device:TPU:1, one launch (start us, length us, event | category | flops | bytes accessed | tf_op | source)
XLA Modules:
  0.0 132.6 jit_solution(12531602853808976642)
XLA Ops:
  0.0 1.1 pad_maximum_fusion
  1.1 0.9 copy.22
  2.0 15.6 %all-to-all-start.1 = ((bf16[256,8,128]{2,1,0:T(8,128)(2,1)}), bf16[256,8,128]{2,1,0:T(8,128)(2,1)S(1)}, u32[]{:S(2)}, u32[]{:S(2)}) async-start(bf16[256,8,128]{2,1,0:T(8,128)(2,1)} %bitcast.12), calls=%async_computation.1 | async-start | bytes 1048576 | tf_op jit(solution)/shard_map/all_to_all | solution.py:238
  17.7 0.1 eq.45
  17.7 0.2 fusion.1
  17.9 0.2 convert_reduce_fusion
  18.1 0.1 select_reduce_fusion
  18.2 2.2 %collective-permute-start = (s32[1,128]{1,0:T(1,128)S(1)}, s32[1,128]{1,0:T(1,128)S(1)}, u32[]{:S(2)}, u32[]{:S(2)}) collective-permute-start(s32[1,128]{1,0:T(1,128)S(1)} %bitcast.25), channel_id=1, source_target_pairs={{0,8},{8,0},{16,24},{24,16},{32,40},{40,32},{48,56},{56,48},{64,72... | collective-permute-start | bytes 1544 | tf_op jit(solution)/shard_map/ppermute | solution.py:216
  20.5 0.8 collective-permute-done
  21.3 0.0 collective-permute-start.1
  21.3 2.7 %collective-permute-done.1 = s32[2,128]{1,0:T(2,128)S(1)} collective-permute-done((s32[2,128]{1,0:T(2,128)S(1)}, s32[2,128]{1,0:T(2,128)S(1)}, u32[]{:S(2)}, u32[]{:S(2)}) %collective-permute-start.1) | collective-permute-done | bytes 1056 | tf_op jit(solution)/shard_map/ppermute | solution.py:216
  24.0 1.2 collective-permute-start.2
  25.2 3.1 %collective-permute-done.2 = s32[4,128]{1,0:T(4,128)S(1)} collective-permute-done((s32[4,128]{1,0:T(4,128)S(1)}, s32[4,128]{1,0:T(4,128)S(1)}, u32[]{:S(2)}, u32[]{:S(2)}) %collective-permute-start.2) | collective-permute-done | bytes 2080 | tf_op jit(solution)/shard_map/ppermute | solution.py:216
  28.4 0.1 collective-permute-start.3
  28.5 2.7 %collective-permute-done.3 = s32[8,128]{1,0:T(8,128)S(1)} collective-permute-done((s32[8,128]{1,0:T(8,128)S(1)}, s32[8,128]{1,0:T(8,128)S(1)}, u32[]{:S(2)}, u32[]{:S(2)}) %collective-permute-start.3) | collective-permute-done | bytes 4128 | tf_op jit(solution)/shard_map/ppermute | solution.py:216
  31.2 1.3 %collective-permute-start.4 = (s32[16,128]{1,0:T(8,128)S(1)}, s32[16,128]{1,0:T(8,128)S(1)}, u32[]{:S(2)}, u32[]{:S(2)}) collective-permute-start(s32[16,128]{1,0:T(8,128)S(1)} %concatenate.34), channel_id=1, source_target_pairs={{0,128},{8,136},{16,144},{24,152},{32,160},{40,168},{48,176},{56,1... | collective-permute-start | bytes 24584 | tf_op jit(solution)/shard_map/ppermute | solution.py:216
  32.6 3.0 %collective-permute-done.4 = s32[16,128]{1,0:T(8,128)S(1)} collective-permute-done((s32[16,128]{1,0:T(8,128)S(1)}, s32[16,128]{1,0:T(8,128)S(1)}, u32[]{:S(2)}, u32[]{:S(2)}) %collective-permute-start.4) | collective-permute-done | bytes 8224 | tf_op jit(solution)/shard_map/ppermute | solution.py:216
  35.6 3.1 %all-to-all-done.1.held = bf16[256,8,128]{2,1,0:T(8,128)(2,1)S(1)} async-done(((bf16[256,8,128]{2,1,0:T(8,128)(2,1)}), bf16[256,8,128]{2,1,0:T(8,128)(2,1)S(1)}, u32[]{:S(2)}, u32[]{:S(2)}) %all-to-all-start.1) | async-done | bytes 524320 | tf_op jit(solution)/shard_map/all_to_all | solution.py:238
  38.8 2.2 %pick.1 = bf16[32,12,8,128]{3,2,1,0:T(8,128)(2,1)} custom-call(s32[32,128]{1,0:T(8,128)S(1)} %concatenate.35.pools, s32[1]{0:T(128)} %bitcast.11.me, bf16[256,8,128]{2,1,0:T(8,128)(2,1)S(1)} %all-to-all-done.1.held), custom_call_target="tpu_custom_call" | custom-call | tf_op jit(solution)/shard_map/pick/pallas_call | solution.py:57
  40.9 5.9 %all-to-all-start.2 = ((bf16[32,12,8,128]{3,2,1,0:T(8,128)(2,1)}), bf16[32,12,8,128]{3,2,1,0:T(8,128)(2,1)S(1)}, u32[]{:S(2)}, u32[]{:S(2)}) async-start(bf16[32,12,8,128]{3,2,1,0:T(8,128)(2,1)} %pick.1), calls=%async_computation.2 | async-start | bytes 1572864 | tf_op jit(solution)/shard_map/all_to_all | solution.py:240
  46.8 0.1 reshape.68
  46.9 0.7 gather_fusion
  47.6 0.1 select_reduce_fusion.1.offs
  47.8 0.7 slice.18
  49.1 0.6 gather_fusion.1
  49.8 0.6 dynamic_slice.11
  50.4 10.7 %all-to-all-done.2.far = bf16[32,12,8,128]{3,2,1,0:T(8,128)(2,1)S(1)} async-done(((bf16[32,12,8,128]{3,2,1,0:T(8,128)(2,1)}), bf16[32,12,8,128]{3,2,1,0:T(8,128)(2,1)S(1)}, u32[]{:S(2)}, u32[]{:S(2)}) %all-to-all-start.2) | async-done | bytes 786464 | tf_op jit(solution)/shard_map/all_to_all | solution.py:240
  61.1 0.8 pack.1
  61.9 1.5 %collective-permute-start.5 = (bf16[152,8,128]{2,1,0:T(8,128)(2,1)S(1)}, bf16[152,8,128]{2,1,0:T(8,128)(2,1)S(1)}, u32[]{:S(2)}, u32[]{:S(2)}) collective-permute-start(bf16[152,8,128]{2,1,0:T(8,128)(2,1)S(1)} %get-tuple-element.12.far_k), channel_id=1, source_target_pairs={{0,1},{1,2},{2,3},{3,4},{4,5},{5,6},{6,7},{7,0},{8,9},{9,10},{10,1... | collective-permute-start | bytes 933896 | tf_op jit(solution)/shard_map/ppermute | solution.py:257
  63.5 2.9 %collective-permute-start.9 = (bf16[152,8,128]{2,1,0:T(8,128)(2,1)S(1)}, bf16[152,8,128]{2,1,0:T(8,128)(2,1)S(1)}, u32[]{:S(2)}, u32[]{:S(2)}) collective-permute-start(bf16[152,8,128]{2,1,0:T(8,128)(2,1)S(1)} %get-tuple-element.13.far_v), channel_id=1, source_target_pairs={{0,7},{1,0},{2,1},{3,2},{4,3},{5,4},{6,5},{7,6},{8,15},{9,8},{10,9... | collective-permute-start | bytes 933896 | tf_op jit(solution)/shard_map/ppermute | solution.py:258
  66.4 0.0 collective-permute-start.16
  66.4 2.7 %collective-permute-start.13 = (bf16[152,8,128]{2,1,0:T(8,128)(2,1)S(1)}, bf16[152,8,128]{2,1,0:T(8,128)(2,1)}, u32[]{:S(2)}, u32[]{:S(2)}) collective-permute-start(bf16[152,8,128]{2,1,0:T(8,128)(2,1)S(1)} %get-tuple-element.12.far_k), channel_id=1, source_target_pairs={{0,7},{1,0},{2,1},{3,2},{4,3},{5,4},{6,5},{7,6},{8,15},{9,8},{10,9... | collective-permute-start | bytes 933896 | tf_op jit(solution)/shard_map/ppermute | solution.py:263
  69.1 5.0 %collective-permute-done.5.far_k = bf16[152,8,128]{2,1,0:T(8,128)(2,1)S(1)} collective-permute-done((bf16[152,8,128]{2,1,0:T(8,128)(2,1)S(1)}, bf16[152,8,128]{2,1,0:T(8,128)(2,1)S(1)}, u32[]{:S(2)}, u32[]{:S(2)}) %collective-permute-start.5) | collective-permute-done | bytes 311328 | tf_op jit(solution)/shard_map/ppermute | solution.py:257
  74.1 0.0 collective-permute-start.6
  74.1 0.0 collective-permute-done.9.far_v
  74.1 2.7 %collective-permute-start.10 = (bf16[152,8,128]{2,1,0:T(8,128)(2,1)S(1)}, bf16[152,8,128]{2,1,0:T(8,128)(2,1)}, u32[]{:S(2)}, u32[]{:S(2)}) collective-permute-start(bf16[152,8,128]{2,1,0:T(8,128)(2,1)S(1)} %collective-permute-done.9.far_v), channel_id=1, source_target_pairs={{0,7},{1,0},{2,1},{3,2},{4,3},{5,4},{6,5},{7,6},{8,15},{9,8},{10,9... | collective-permute-start | bytes 933896 | tf_op jit(solution)/shard_map/ppermute | solution.py:258
  76.8 0.2 select_reduce_fusion.2
  77.0 3.8 %collective-permute-done.16.far_v = bf16[152,8,128]{2,1,0:T(8,128)(2,1)S(1)} collective-permute-done((bf16[152,8,128]{2,1,0:T(8,128)(2,1)S(1)}, bf16[152,8,128]{2,1,0:T(8,128)(2,1)S(1)}, u32[]{:S(2)}, u32[]{:S(2)}) %collective-permute-start.16) | collective-permute-done | bytes 311328 | tf_op jit(solution)/shard_map/ppermute | solution.py:262
  80.8 0.0 collective-permute-done.13.far_k
  80.8 2.7 %collective-permute-start.14 = (bf16[152,8,128]{2,1,0:T(8,128)(2,1)}, bf16[152,8,128]{2,1,0:T(8,128)(2,1)}, u32[]{:S(2)}, u32[]{:S(2)}) collective-permute-start(bf16[152,8,128]{2,1,0:T(8,128)(2,1)} %collective-permute-done.13.far_k), channel_id=1, source_target_pairs={{0,7},{1,0},{2,1},{3,2},{4,3},{5,4},{6,5},{7,6},{8,15},{9,8},{10,9... | collective-permute-start | bytes 933896 | tf_op jit(solution)/shard_map/ppermute | solution.py:263
  83.6 4.0 %collective-permute-done.6.far_k = bf16[152,8,128]{2,1,0:T(8,128)(2,1)} collective-permute-done((bf16[152,8,128]{2,1,0:T(8,128)(2,1)S(1)}, bf16[152,8,128]{2,1,0:T(8,128)(2,1)}, u32[]{:S(2)}, u32[]{:S(2)}) %collective-permute-start.6) | collective-permute-done | bytes 311328 | tf_op jit(solution)/shard_map/ppermute | solution.py:257
  87.6 0.0 collective-permute-start.7
  87.6 2.7 %collective-permute-start.11 = (bf16[152,8,128]{2,1,0:T(8,128)(2,1)}, bf16[152,8,128]{2,1,0:T(8,128)(2,1)}, u32[]{:S(2)}, u32[]{:S(2)}) collective-permute-start(bf16[152,8,128]{2,1,0:T(8,128)(2,1)} %collective-permute-done.10.far_v), channel_id=1, source_target_pairs={{0,7},{1,0},{2,1},{3,2},{4,3},{5,4},{6,5},{7,6},{8,15},{9,8},{10,9... | collective-permute-start | bytes 933896 | tf_op jit(solution)/shard_map/ppermute | solution.py:258
  90.2 0.7 add_bitcast_fusion
  90.9 0.1 pad.12.clone
  91.0 0.1 copy.18
  91.1 3.1 %collective-permute-done.17.far_v = bf16[152,8,128]{2,1,0:T(8,128)(2,1)} collective-permute-done((bf16[152,8,128]{2,1,0:T(8,128)(2,1)S(1)}, bf16[152,8,128]{2,1,0:T(8,128)(2,1)}, u32[]{:S(2)}, u32[]{:S(2)}) %collective-permute-start.17) | collective-permute-done | bytes 311328 | tf_op jit(solution)/shard_map/ppermute | solution.py:262
  94.2 0.0 collective-permute-start.18
  94.3 0.0 copy-start
  94.3 0.0 collective-permute-done.14.far_k
  94.3 2.7 %collective-permute-start.15 = (bf16[152,8,128]{2,1,0:T(8,128)(2,1)}, bf16[152,8,128]{2,1,0:T(8,128)(2,1)S(1)}, u32[]{:S(2)}, u32[]{:S(2)}) collective-permute-start(bf16[152,8,128]{2,1,0:T(8,128)(2,1)} %collective-permute-done.14.far_k), channel_id=1, source_target_pairs={{0,7},{1,0},{2,1},{3,2},{4,3},{5,4},{6,5},{7,6},{8,15},{9,8},{10,9... | collective-permute-start | bytes 933896 | tf_op jit(solution)/shard_map/ppermute | solution.py:263
  97.0 1.0 copy-done.2
  98.0 4.1 %attend.8._ = bf16[128,64,128]{2,1,0:T(8,128)(2,1)} custom-call(s32[8,19]{1,0:T(8,128)S(1)} %pad_add_fusion.meta, bf16[128,64,128]{2,1,0:T(8,128)(2,1)S(1)} %copy-done, bf16[32,8,8,128]{3,2,1,0:T(8,128)(2,1)} %bitcast.20.clone.2.own, bf16[152,8,128]{2,1,0:T(8,128)(2,1)S(1)} %get-tuple-element.12.far_k, ...), custom_call_target="tpu_custom_call", output_to_operand_aliasing={{}: (6, {})} | custom-call | flops 603979776 | bytes 2097152 | tf_op jit(solution)/shard_map/attend/pallas_call | solution.py:172
  102.1 0.0 collective-permute-done.11.far_v
  102.1 1.5 %collective-permute-start.12 = (bf16[152,8,128]{2,1,0:T(8,128)(2,1)}, bf16[152,8,128]{2,1,0:T(8,128)(2,1)S(1)}, u32[]{:S(2)}, u32[]{:S(2)}) collective-permute-start(bf16[152,8,128]{2,1,0:T(8,128)(2,1)} %collective-permute-done.11.far_v), channel_id=1, source_target_pairs={{0,7},{1,0},{2,1},{3,2},{4,3},{5,4},{6,5},{7,6},{8,15},{9,8},{10,9... | collective-permute-start | bytes 933896 | tf_op jit(solution)/shard_map/ppermute | solution.py:258
  103.6 0.0 collective-permute-start.8
  103.6 4.0 %attend.9._ = bf16[128,64,128]{2,1,0:T(8,128)(2,1)} custom-call(s32[8,19]{1,0:T(8,128)S(1)} %pad_add_fusion.meta, bf16[128,64,128]{2,1,0:T(8,128)(2,1)S(1)} %copy-done, bf16[32,8,8,128]{3,2,1,0:T(8,128)(2,1)} %bitcast.20.clone.2.own, bf16[152,8,128]{2,1,0:T(8,128)(2,1)S(1)} %collective-permute-done.5.far_k, ...), custom_call_target="tpu_custom_call", output_to_operand_aliasing={{}: (6, {})} | custom-call | flops 603979776 | bytes 2097152 | tf_op jit(solution)/shard_map/attend/pallas_call | solution.py:172
  107.6 4.1 %attend.10._ = bf16[128,64,128]{2,1,0:T(8,128)(2,1)} custom-call(s32[8,19]{1,0:T(8,128)S(1)} %pad_add_fusion.meta, bf16[128,64,128]{2,1,0:T(8,128)(2,1)S(1)} %copy-done, bf16[32,8,8,128]{3,2,1,0:T(8,128)(2,1)} %bitcast.20.clone.2.own, bf16[152,8,128]{2,1,0:T(8,128)(2,1)} %collective-permute-done.13.far_k, ...), custom_call_target="tpu_custom_call", output_to_operand_aliasing={{}: (6, {})} | custom-call | flops 603979776 | bytes 2097152 | tf_op jit(solution)/shard_map/attend/pallas_call | solution.py:172
  111.7 4.4 %attend.11._ = bf16[128,64,128]{2,1,0:T(8,128)(2,1)} custom-call(s32[8,19]{1,0:T(8,128)S(1)} %pad_add_fusion.meta, bf16[128,64,128]{2,1,0:T(8,128)(2,1)S(1)} %copy-done, bf16[32,8,8,128]{3,2,1,0:T(8,128)(2,1)} %bitcast.20.clone.2.own, bf16[152,8,128]{2,1,0:T(8,128)(2,1)} %collective-permute-done.6.far_k, ...), custom_call_target="tpu_custom_call", output_to_operand_aliasing={{}: (6, {})} | custom-call | flops 603979776 | bytes 2097152 | tf_op jit(solution)/shard_map/attend/pallas_call | solution.py:172
  116.1 4.1 %attend.12._ = bf16[128,64,128]{2,1,0:T(8,128)(2,1)} custom-call(s32[8,19]{1,0:T(8,128)S(1)} %pad_add_fusion.meta, bf16[128,64,128]{2,1,0:T(8,128)(2,1)S(1)} %copy-done, bf16[32,8,8,128]{3,2,1,0:T(8,128)(2,1)} %bitcast.20.clone.2.own, bf16[152,8,128]{2,1,0:T(8,128)(2,1)} %collective-permute-done.14.far_k, ...), custom_call_target="tpu_custom_call", output_to_operand_aliasing={{}: (6, {})} | custom-call | flops 603979776 | bytes 2097152 | tf_op jit(solution)/shard_map/attend/pallas_call | solution.py:172
  120.2 0.0 collective-permute-done.18.far_v
  120.2 4.2 %attend.13._ = bf16[128,64,128]{2,1,0:T(8,128)(2,1)} custom-call(s32[8,19]{1,0:T(8,128)S(1)} %pad_add_fusion.meta, bf16[128,64,128]{2,1,0:T(8,128)(2,1)S(1)} %copy-done, bf16[32,8,8,128]{3,2,1,0:T(8,128)(2,1)} %bitcast.20.clone.2.own, bf16[152,8,128]{2,1,0:T(8,128)(2,1)} %collective-permute-done.7.far_k, ...), custom_call_target="tpu_custom_call", output_to_operand_aliasing={{}: (6, {})} | custom-call | flops 603979776 | bytes 2097152 | tf_op jit(solution)/shard_map/attend/pallas_call | solution.py:172
  124.4 4.1 %attend.14._ = bf16[128,64,128]{2,1,0:T(8,128)(2,1)} custom-call(s32[8,19]{1,0:T(8,128)S(1)} %pad_add_fusion.meta, bf16[128,64,128]{2,1,0:T(8,128)(2,1)S(1)} %copy-done, bf16[32,8,8,128]{3,2,1,0:T(8,128)(2,1)} %bitcast.20.clone.2.own, bf16[152,8,128]{2,1,0:T(8,128)(2,1)S(1)} %collective-permute-done.15.far_k, ...), custom_call_target="tpu_custom_call", output_to_operand_aliasing={{}: (6, {})} | custom-call | flops 603979776 | bytes 2097152 | tf_op jit(solution)/shard_map/attend/pallas_call | solution.py:172
  128.5 4.0 %attend.15 = bf16[128,64,128]{2,1,0:T(8,128)(2,1)} custom-call(s32[8,19]{1,0:T(8,128)S(1)} %pad_add_fusion.meta, bf16[128,64,128]{2,1,0:T(8,128)(2,1)S(1)} %copy-done, bf16[32,8,8,128]{3,2,1,0:T(8,128)(2,1)} %bitcast.20.clone.2.own, bf16[152,8,128]{2,1,0:T(8,128)(2,1)S(1)} %collective-permute-done.8.far_k, ...), custom_call_target="tpu_custom_call", output_to_operand_aliasing={{}: (6, {})} | custom-call | flops 603979776 | bytes 2097152 | tf_op jit(solution)/shard_map/attend/pallas_call | solution.py:172
  (37 shorter events, 0.2 us)
Async XLA Ops:
  0.0 17.7 %copy-start.5 = (s32[8,8]{1,0:T(8,128)S(1)}, s32[8,8]{1,0:T(8,128)}, u32[]{:S(2)}) copy-start(s32[8,8]{1,0:T(8,128)} %param.11) | copy-start | bytes 772
  2.0 44.9 %copy-start.3 = (s32[256]{0:T(256)S(1)}, s32[256]{0:T(256)}, u32[]{:S(2)}) copy-start(s32[256]{0:T(256)} %param.12) | copy-start | bytes 3076
  2.0 36.8 %all-to-all-start.1 = ((bf16[256,8,128]{2,1,0:T(8,128)(2,1)}), bf16[256,8,128]{2,1,0:T(8,128)(2,1)S(1)}, u32[]{:S(2)}, u32[]{:S(2)}) async-start(bf16[256,8,128]{2,1,0:T(8,128)(2,1)} %bitcast.12), calls=%async_computation.1 | async-start | bytes 1048576 | tf_op jit(solution)/shard_map/all_to_all | solution.py:238
  18.2 3.0 %collective-permute-start = (s32[1,128]{1,0:T(1,128)S(1)}, s32[1,128]{1,0:T(1,128)S(1)}, u32[]{:S(2)}, u32[]{:S(2)}) collective-permute-start(s32[1,128]{1,0:T(1,128)S(1)} %bitcast.25), channel_id=1, source_target_pairs={{0,8},{8,0},{16,24},{24,16},{32,40},{40,32},{48,56},{56,48},{64,72... | collective-permute-start | bytes 1544 | tf_op jit(solution)/shard_map/ppermute | solution.py:216
  21.3 2.7 %collective-permute-start.1 = (s32[2,128]{1,0:T(2,128)S(1)}, s32[2,128]{1,0:T(2,128)S(1)}, u32[]{:S(2)}, u32[]{:S(2)}) collective-permute-start(s32[2,128]{1,0:T(2,128)S(1)} %pad_add_fusion.3), channel_id=1, source_target_pairs={{0,16},{8,24},{16,0},{24,8},{32,48},{40,56},{48,32},{56,40},{64,80... | collective-permute-start | bytes 3080 | tf_op jit(solution)/shard_map/ppermute | solution.py:216
  24.0 4.3 %collective-permute-start.2 = (s32[4,128]{1,0:T(4,128)S(1)}, s32[4,128]{1,0:T(4,128)S(1)}, u32[]{:S(2)}, u32[]{:S(2)}) collective-permute-start(s32[4,128]{1,0:T(4,128)S(1)} %pad_add_fusion.2), channel_id=1, source_target_pairs={{0,32},{8,40},{16,48},{24,56},{32,0},{40,8},{48,16},{56,24},{64,96... | collective-permute-start | bytes 6152 | tf_op jit(solution)/shard_map/ppermute | solution.py:216
  28.4 2.8 %collective-permute-start.3 = (s32[8,128]{1,0:T(8,128)S(1)}, s32[8,128]{1,0:T(8,128)S(1)}, u32[]{:S(2)}, u32[]{:S(2)}) collective-permute-start(s32[8,128]{1,0:T(8,128)S(1)} %pad_add_fusion.1), channel_id=1, source_target_pairs={{0,64},{8,72},{16,80},{24,88},{32,96},{40,104},{48,112},{56,120},{... | collective-permute-start | bytes 12296 | tf_op jit(solution)/shard_map/ppermute | solution.py:216
  31.2 4.4 %collective-permute-start.4 = (s32[16,128]{1,0:T(8,128)S(1)}, s32[16,128]{1,0:T(8,128)S(1)}, u32[]{:S(2)}, u32[]{:S(2)}) collective-permute-start(s32[16,128]{1,0:T(8,128)S(1)} %concatenate.34), channel_id=1, source_target_pairs={{0,128},{8,136},{16,144},{24,152},{32,160},{40,168},{48,176},{56,1... | collective-permute-start | bytes 24584 | tf_op jit(solution)/shard_map/ppermute | solution.py:216
  38.8 42.0 %copy-start.6 = (s32[8]{0:T(128)S(1)}, s32[8]{0:T(128)}, u32[]{:S(2)}) copy-start(s32[8]{0:T(128)} %constant.77.clone) | copy-start | bytes 100
  40.9 20.1 %all-to-all-start.2 = ((bf16[32,12,8,128]{3,2,1,0:T(8,128)(2,1)}), bf16[32,12,8,128]{3,2,1,0:T(8,128)(2,1)S(1)}, u32[]{:S(2)}, u32[]{:S(2)}) async-start(bf16[32,12,8,128]{3,2,1,0:T(8,128)(2,1)} %pick.1), calls=%async_computation.2 | async-start | bytes 1572864 | tf_op jit(solution)/shard_map/all_to_all | solution.py:240
  61.9 32.4 %copy-start.1 = (bf16[152,8,128]{2,1,0:T(8,128)(2,1)}, bf16[152,8,128]{2,1,0:T(8,128)(2,1)S(1)}, u32[]{:S(2)}) copy-start(bf16[152,8,128]{2,1,0:T(8,128)(2,1)S(1)} %get-tuple-element.13.far_v) | copy-start | bytes 933892
  61.9 12.2 %collective-permute-start.5 = (bf16[152,8,128]{2,1,0:T(8,128)(2,1)S(1)}, bf16[152,8,128]{2,1,0:T(8,128)(2,1)S(1)}, u32[]{:S(2)}, u32[]{:S(2)}) collective-permute-start(bf16[152,8,128]{2,1,0:T(8,128)(2,1)S(1)} %get-tuple-element.12.far_k), channel_id=1, source_target_pairs={{0,1},{1,2},{2,3},{3,4},{4,5},{5,6},{6,7},{7,0},{8,9},{9,10},{10,1... | collective-permute-start | bytes 933896 | tf_op jit(solution)/shard_map/ppermute | solution.py:257
  63.5 10.7 %collective-permute-start.9 = (bf16[152,8,128]{2,1,0:T(8,128)(2,1)S(1)}, bf16[152,8,128]{2,1,0:T(8,128)(2,1)S(1)}, u32[]{:S(2)}, u32[]{:S(2)}) collective-permute-start(bf16[152,8,128]{2,1,0:T(8,128)(2,1)S(1)} %get-tuple-element.13.far_v), channel_id=1, source_target_pairs={{0,7},{1,0},{2,1},{3,2},{4,3},{5,4},{6,5},{7,6},{8,15},{9,8},{10,9... | collective-permute-start | bytes 933896 | tf_op jit(solution)/shard_map/ppermute | solution.py:258
  66.4 14.4 %collective-permute-start.16 = (bf16[152,8,128]{2,1,0:T(8,128)(2,1)S(1)}, bf16[152,8,128]{2,1,0:T(8,128)(2,1)S(1)}, u32[]{:S(2)}, u32[]{:S(2)}) collective-permute-start(bf16[152,8,128]{2,1,0:T(8,128)(2,1)S(1)} %get-tuple-element.13.far_v), channel_id=1, source_target_pairs={{0,1},{1,2},{2,3},{3,4},{4,5},{5,6},{6,7},{7,0},{8,9},{9,10},{10,1... | collective-permute-start | bytes 933896 | tf_op jit(solution)/shard_map/ppermute | solution.py:262
  66.4 14.4 %collective-permute-start.13 = (bf16[152,8,128]{2,1,0:T(8,128)(2,1)S(1)}, bf16[152,8,128]{2,1,0:T(8,128)(2,1)}, u32[]{:S(2)}, u32[]{:S(2)}) collective-permute-start(bf16[152,8,128]{2,1,0:T(8,128)(2,1)S(1)} %get-tuple-element.12.far_k), channel_id=1, source_target_pairs={{0,7},{1,0},{2,1},{3,2},{4,3},{5,4},{6,5},{7,6},{8,15},{9,8},{10,9... | collective-permute-start | bytes 933896 | tf_op jit(solution)/shard_map/ppermute | solution.py:263
  74.1 13.4 %collective-permute-start.6 = (bf16[152,8,128]{2,1,0:T(8,128)(2,1)S(1)}, bf16[152,8,128]{2,1,0:T(8,128)(2,1)}, u32[]{:S(2)}, u32[]{:S(2)}) collective-permute-start(bf16[152,8,128]{2,1,0:T(8,128)(2,1)S(1)} %collective-permute-done.5.far_k), channel_id=1, source_target_pairs={{0,1},{1,2},{2,3},{3,4},{4,5},{5,6},{6,7},{7,0},{8,9},{9,10},{10,1... | collective-permute-start | bytes 933896 | tf_op jit(solution)/shard_map/ppermute | solution.py:257
  74.1 13.4 %collective-permute-start.10 = (bf16[152,8,128]{2,1,0:T(8,128)(2,1)S(1)}, bf16[152,8,128]{2,1,0:T(8,128)(2,1)}, u32[]{:S(2)}, u32[]{:S(2)}) collective-permute-start(bf16[152,8,128]{2,1,0:T(8,128)(2,1)S(1)} %collective-permute-done.9.far_v), channel_id=1, source_target_pairs={{0,7},{1,0},{2,1},{3,2},{4,3},{5,4},{6,5},{7,6},{8,15},{9,8},{10,9... | collective-permute-start | bytes 933896 | tf_op jit(solution)/shard_map/ppermute | solution.py:258
  80.8 13.4 %collective-permute-start.17 = (bf16[152,8,128]{2,1,0:T(8,128)(2,1)S(1)}, bf16[152,8,128]{2,1,0:T(8,128)(2,1)}, u32[]{:S(2)}, u32[]{:S(2)}) collective-permute-start(bf16[152,8,128]{2,1,0:T(8,128)(2,1)S(1)} %collective-permute-done.16.far_v), channel_id=1, source_target_pairs={{0,1},{1,2},{2,3},{3,4},{4,5},{5,6},{6,7},{7,0},{8,9},{9,10},{10,1... | collective-permute-start | bytes 933896 | tf_op jit(solution)/shard_map/ppermute | solution.py:262
  80.8 13.5 %collective-permute-start.14 = (bf16[152,8,128]{2,1,0:T(8,128)(2,1)}, bf16[152,8,128]{2,1,0:T(8,128)(2,1)}, u32[]{:S(2)}, u32[]{:S(2)}) collective-permute-start(bf16[152,8,128]{2,1,0:T(8,128)(2,1)} %collective-permute-done.13.far_k), channel_id=1, source_target_pairs={{0,7},{1,0},{2,1},{3,2},{4,3},{5,4},{6,5},{7,6},{8,15},{9,8},{10,9... | collective-permute-start | bytes 933896 | tf_op jit(solution)/shard_map/ppermute | solution.py:263
  87.6 16.1 %collective-permute-start.7 = (bf16[152,8,128]{2,1,0:T(8,128)(2,1)}, bf16[152,8,128]{2,1,0:T(8,128)(2,1)}, u32[]{:S(2)}, u32[]{:S(2)}) collective-permute-start(bf16[152,8,128]{2,1,0:T(8,128)(2,1)} %collective-permute-done.6.far_k), channel_id=1, source_target_pairs={{0,1},{1,2},{2,3},{3,4},{4,5},{5,6},{6,7},{7,0},{8,9},{9,10},{10,1... | collective-permute-start | bytes 933896 | tf_op jit(solution)/shard_map/ppermute | solution.py:257
  87.6 14.5 %collective-permute-start.11 = (bf16[152,8,128]{2,1,0:T(8,128)(2,1)}, bf16[152,8,128]{2,1,0:T(8,128)(2,1)}, u32[]{:S(2)}, u32[]{:S(2)}) collective-permute-start(bf16[152,8,128]{2,1,0:T(8,128)(2,1)} %collective-permute-done.10.far_v), channel_id=1, source_target_pairs={{0,7},{1,0},{2,1},{3,2},{4,3},{5,4},{6,5},{7,6},{8,15},{9,8},{10,9... | collective-permute-start | bytes 933896 | tf_op jit(solution)/shard_map/ppermute | solution.py:258
  94.2 26.0 %collective-permute-start.18 = (bf16[152,8,128]{2,1,0:T(8,128)(2,1)}, bf16[152,8,128]{2,1,0:T(8,128)(2,1)}, u32[]{:S(2)}, u32[]{:S(2)}) collective-permute-start(bf16[152,8,128]{2,1,0:T(8,128)(2,1)} %collective-permute-done.17.far_v), channel_id=1, source_target_pairs={{0,1},{1,2},{2,3},{3,4},{4,5},{5,6},{6,7},{7,0},{8,9},{9,10},{10,1... | collective-permute-start | bytes 933896 | tf_op jit(solution)/shard_map/ppermute | solution.py:262
  94.3 2.8 %copy-start = (bf16[128,64,128]{2,1,0:T(8,128)(2,1)S(1)}, bf16[128,64,128]{2,1,0:T(8,128)(2,1)}, u32[]{:S(2)}) copy-start(bf16[128,64,128]{2,1,0:T(8,128)(2,1)} %q.15) | copy-start | bytes 6291460
  94.3 30.1 %collective-permute-start.15 = (bf16[152,8,128]{2,1,0:T(8,128)(2,1)}, bf16[152,8,128]{2,1,0:T(8,128)(2,1)S(1)}, u32[]{:S(2)}, u32[]{:S(2)}) collective-permute-start(bf16[152,8,128]{2,1,0:T(8,128)(2,1)} %collective-permute-done.14.far_k), channel_id=1, source_target_pairs={{0,7},{1,0},{2,1},{3,2},{4,3},{5,4},{6,5},{7,6},{8,15},{9,8},{10,9... | collective-permute-start | bytes 933896 | tf_op jit(solution)/shard_map/ppermute | solution.py:263
  97.0 1.0 copy-start.2
  98.0 5.6 %copy-start.4 = (bf16[8,2,40,8,128]{4,3,2,1,0:T(8,128)(2,1)S(1)}, bf16[8,2,40,8,128]{4,3,2,1,0:T(8,128)(2,1)}, u32[]{:S(2)}) copy-start(bf16[8,2,40,8,128]{4,3,2,1,0:T(8,128)(2,1)} %get-tuple-element.17.rest) | copy-start | bytes 3932164
  102.1 26.4 %collective-permute-start.12 = (bf16[152,8,128]{2,1,0:T(8,128)(2,1)}, bf16[152,8,128]{2,1,0:T(8,128)(2,1)S(1)}, u32[]{:S(2)}, u32[]{:S(2)}) collective-permute-start(bf16[152,8,128]{2,1,0:T(8,128)(2,1)} %collective-permute-done.11.far_v), channel_id=1, source_target_pairs={{0,7},{1,0},{2,1},{3,2},{4,3},{5,4},{6,5},{7,6},{8,15},{9,8},{10,9... | collective-permute-start | bytes 933896 | tf_op jit(solution)/shard_map/ppermute | solution.py:258
  103.6 24.8 %collective-permute-start.8 = (bf16[152,8,128]{2,1,0:T(8,128)(2,1)}, bf16[152,8,128]{2,1,0:T(8,128)(2,1)S(1)}, u32[]{:S(2)}, u32[]{:S(2)}) collective-permute-start(bf16[152,8,128]{2,1,0:T(8,128)(2,1)} %collective-permute-done.7.far_k), channel_id=1, source_target_pairs={{0,1},{1,2},{2,3},{3,4},{4,5},{5,6},{6,7},{7,0},{8,9},{9,10},{10,1... | collective-permute-start | bytes 933896 | tf_op jit(solution)/shard_map/ppermute | solution.py:257

commit v4 on v3

--- a/solution.py
+++ b/solution.py
@@ -148,18 +148,23 @@
         at = pl.ds(i * tokens, tokens)
         return pltpu.make_async_copy(held.at[at], out.at[at, heads], sems.at[i])
 
-    for i in range(parts):
-        at = slice(i * tokens, (i + 1) * tokens)
-        qt = q[at, heads].astype(jnp.float32).reshape(rows, BS).astype(jnp.bfloat16)
+    def scores(i):
+        qt = q[g, i * tokens : (i + 1) * tokens].reshape(rows, BS)
         s = lax.dot_general(qt, keys[...], (((1,), (1,)), ((), ())), preferred_element_type=jnp.float32)
-        s = [jnp.where((offset <= token + i * tokens) & inside, s[:, 0:BS], NEG)] + [
+        return [jnp.where((offset <= token + i * tokens) & inside, s[:, 0:BS], NEG)] + [
             s[:, (j + 1) * BS : (j + 2) * BS] + bias[j] for j in range(far)
         ]
-        m = jnp.max(functools.reduce(jnp.maximum, s), axis=1, keepdims=True)
-        p = jnp.concatenate([jnp.exp2((x - m) * scale).astype(jnp.bfloat16) for x in s], axis=1)
-        o = jnp.dot(p, vals[...], preferred_element_type=jnp.float32)
+
+    def weights(s):
+        m = jnp.max(functools.reduce(jnp.maximum, s), axis=1, keepdims=True) * scale
+        return jnp.concatenate([jnp.exp2(x * scale - m).astype(jnp.bfloat16) for x in s], axis=1)
+
+    every = [scores(i) for i in range(parts)]
+    every = [weights(s) for s in every]
+    for i in range(parts):
+        o = jnp.dot(every[i], vals[...], preferred_element_type=jnp.float32)
         r = o[:, 0:BS] / o[:, BS:]
-        held[at] = r.reshape(tokens, 8, BS).astype(out.dtype)
+        held[i * tokens : (i + 1) * tokens] = r.reshape(tokens, 8, BS).astype(out.dtype)
         leave(i).start()
     for i in range(parts):
         leave(i).wait()
@@ -171,7 +176,7 @@
     hbm = pl.BlockSpec(memory_space=pl.ANY)
     return pl.pallas_call(
         functools.partial(attend_kernel, scale, call),
-        out_shape=jax.ShapeDtypeStruct(prev.shape, q.dtype),
+        out_shape=jax.ShapeDtypeStruct(prev.shape, prev.dtype),
         in_specs=[smem(), vmem(), vmem(), vmem(), vmem(), hbm, hbm],
         out_specs=hbm,
         scratch_shapes=[
@@ -187,6 +192,26 @@
         cost_estimate=pl.CostEstimate(flops=flops, bytes_accessed=2 << 20, transcendentals=1024 * 1152),
         name="attend",
     )(meta, q, own, far_k, far_v, rest, prev)
+
+
+def stage_kernel(q, out, sems):
+    copies = [pltpu.make_async_copy(q.at[:, h * 8 : (h + 1) * 8], out.at[h], sems.at[h]) for h in range(8)]
+    for copy in copies:
+        copy.start()
+    for copy in copies:
+        copy.wait()
+
+
+def stage(q):
+    return pl.pallas_call(
+        stage_kernel,
+        out_shape=jax.ShapeDtypeStruct((8, BS, 8, BS), q.dtype),
+        in_specs=[pl.BlockSpec(memory_space=pl.ANY)],
+        out_specs=vmem(),
+        scratch_shapes=[pltpu.SemaphoreType.DMA((8,))],
+        compiler_params=pltpu.CompilerParams(vmem_limit_bytes=GRANT),
+        name="stage",
+    )(q)
 
 
 def blank_kernel(out):
@@ -250,6 +275,7 @@
     up = [(i, (i + 1) % n_head) for i in range(n_head)]
     down = [(i, (i - 1) % n_head) for i in range(n_head)]
     out = blank(queries.shape, queries.dtype)
+    queries = stage(queries)
     out = attend(0, meta, queries, own, far_k, far_v, rest, out)
     k_up = k_down = far_k
     v_up = v_down = far_v

time: 134 us -> 133 us (level)
  local copies, waits for them, and re-layouts: 4.83 us -> 7.11 us
  Pallas kernels: 35.8 us -> 33.6 us
    pallas_call x8, Pallas kernels: 32.8 us -> 30 us  [attend(): pl.pallas_call(functools.partial(attend_kernel, scale, call), out_shape=j...]
    unnamed x14, local copies, waits for them, and re-layouts: 0.99 us -> 3.27 us
    ppermute x4, starting transfers between devices: 9.81 us -> 8.36 us  [attention(): v_down = lax.ppermute(v_down, 'head', down)]
    ppermute x4, starting transfers between devices: 1.55 us -> 2.99 us  [attention(): k_up = lax.ppermute(k_up, 'head', up)]
  transfers between devices with their start and end apart: 21 -> 21, of which waited for: 11 -> 11; matrix products, arithmetic and copies ran while one was open for 3% -> 3% of each run, Pallas kernels for 22% -> 20%
where the time goes in v4:
time: 133 us; the launch traced here: 132 us
  starting transfers between devices  46 us (35%)
  waiting for transfers between devices  41.5 us (31%)
  Pallas kernels  33.6 us (25%)
  local copies, waits for them, and re-layouts  7.11 us (5%)
  other arithmetic  2.65 us (2%)
    pallas_call x8, Pallas kernels, attend(): pl.pallas_call(functools.partial(attend_kernel, scale, call), out_shape=j...  30 us
    all_to_all x1, starting transfers between devices, attention(): lax.all_to_all(own.reshape(n_seq * n_head, TILE, BS), ('seq', 'head'), 0,...  15.6 us
    ppermute x5, waiting for transfers between devices, attention(): other = lax.ppermute(pools, 'seq', [(i, i ^ bit) for i in range(n_seq)])  12.5 us
    all_to_all x1, waiting for transfers between devices, attention(): far = lax.all_to_all(picked, 'seq', 0, 0, tiled=True)  10.7 us
    ppermute x4, starting transfers between devices, attention(): v_down = lax.ppermute(v_down, 'head', down)  8.36 us
    ppermute x4, waiting for transfers between devices, attention(): k_up = lax.ppermute(k_up, 'head', up)  8.26 us
    ppermute x3, starting transfers between devices, attention(): k_down = lax.ppermute(k_down, 'head', down)  8.23 us
    ppermute x3, waiting for transfers between devices, attention(): v_up = lax.ppermute(v_up, 'head', up)  6.94 us
  transfers between devices with their start and end apart: 21, of which 11 were waited for; matrix products, arithmetic and copies ran while one was open for 3% of the time, Pallas kernels for 20%

profile of v4, /device:TPU:1, one launch (start us, length us, event | category | flops | bytes accessed | tf_op | source)
XLA Modules:
  0.0 132.1 jit_solution(15123413372818829688)
XLA Ops:
  0.0 1.1 pad_maximum_fusion
  1.1 0.9 copy.22
  2.0 15.6 %all-to-all-start.1 = ((bf16[256,8,128]{2,1,0:T(8,128)(2,1)}), bf16[256,8,128]{2,1,0:T(8,128)(2,1)S(1)}, u32[]{:S(2)}, u32[]{:S(2)}) async-start(bf16[256,8,128]{2,1,0:T(8,128)(2,1)} %bitcast.12), calls=%async_computation.1 | async-start | bytes 1048576 | tf_op jit(solution)/shard_map/all_to_all | solution.py:263
  17.7 0.1 eq.45
  17.7 0.2 fusion.1
  17.9 0.2 convert_reduce_fusion
  18.1 0.1 select_reduce_fusion
  18.2 2.2 %collective-permute-start = (s32[1,128]{1,0:T(1,128)S(1)}, s32[1,128]{1,0:T(1,128)S(1)}, u32[]{:S(2)}, u32[]{:S(2)}) collective-permute-start(s32[1,128]{1,0:T(1,128)S(1)} %bitcast.25), channel_id=1, source_target_pairs={{0,8},{8,0},{16,24},{24,16},{32,40},{40,32},{48,56},{56,48},{64,72... | collective-permute-start | bytes 1544 | tf_op jit(solution)/shard_map/ppermute | solution.py:241
  20.5 0.8 collective-permute-done
  21.3 0.0 collective-permute-start.1
  21.3 2.7 %collective-permute-done.1 = s32[2,128]{1,0:T(2,128)S(1)} collective-permute-done((s32[2,128]{1,0:T(2,128)S(1)}, s32[2,128]{1,0:T(2,128)S(1)}, u32[]{:S(2)}, u32[]{:S(2)}) %collective-permute-start.1) | collective-permute-done | bytes 1056 | tf_op jit(solution)/shard_map/ppermute | solution.py:241
  24.0 1.2 collective-permute-start.2
  25.2 3.1 %collective-permute-done.2 = s32[4,128]{1,0:T(4,128)S(1)} collective-permute-done((s32[4,128]{1,0:T(4,128)S(1)}, s32[4,128]{1,0:T(4,128)S(1)}, u32[]{:S(2)}, u32[]{:S(2)}) %collective-permute-start.2) | collective-permute-done | bytes 2080 | tf_op jit(solution)/shard_map/ppermute | solution.py:241
  28.4 0.1 collective-permute-start.3
  28.5 2.7 %collective-permute-done.3 = s32[8,128]{1,0:T(8,128)S(1)} collective-permute-done((s32[8,128]{1,0:T(8,128)S(1)}, s32[8,128]{1,0:T(8,128)S(1)}, u32[]{:S(2)}, u32[]{:S(2)}) %collective-permute-start.3) | collective-permute-done | bytes 4128 | tf_op jit(solution)/shard_map/ppermute | solution.py:241
  31.2 1.3 %collective-permute-start.4 = (s32[16,128]{1,0:T(8,128)S(1)}, s32[16,128]{1,0:T(8,128)S(1)}, u32[]{:S(2)}, u32[]{:S(2)}) collective-permute-start(s32[16,128]{1,0:T(8,128)S(1)} %concatenate.34), channel_id=1, source_target_pairs={{0,128},{8,136},{16,144},{24,152},{32,160},{40,168},{48,176},{56,1... | collective-permute-start | bytes 24584 | tf_op jit(solution)/shard_map/ppermute | solution.py:241
  32.6 3.0 %collective-permute-done.4 = s32[16,128]{1,0:T(8,128)S(1)} collective-permute-done((s32[16,128]{1,0:T(8,128)S(1)}, s32[16,128]{1,0:T(8,128)S(1)}, u32[]{:S(2)}, u32[]{:S(2)}) %collective-permute-start.4) | collective-permute-done | bytes 8224 | tf_op jit(solution)/shard_map/ppermute | solution.py:241
  35.6 3.1 %all-to-all-done.1.held = bf16[256,8,128]{2,1,0:T(8,128)(2,1)S(1)} async-done(((bf16[256,8,128]{2,1,0:T(8,128)(2,1)}), bf16[256,8,128]{2,1,0:T(8,128)(2,1)S(1)}, u32[]{:S(2)}, u32[]{:S(2)}) %all-to-all-start.1) | async-done | bytes 524320 | tf_op jit(solution)/shard_map/all_to_all | solution.py:263
  38.8 2.2 %pick.1 = bf16[32,12,8,128]{3,2,1,0:T(8,128)(2,1)} custom-call(s32[32,128]{1,0:T(8,128)S(1)} %concatenate.35.pools, s32[1]{0:T(128)} %bitcast.11.me, bf16[256,8,128]{2,1,0:T(8,128)(2,1)S(1)} %all-to-all-done.1.held), custom_call_target="tpu_custom_call" | custom-call | tf_op jit(solution)/shard_map/pick/pallas_call | solution.py:57
  40.9 5.9 %all-to-all-start.2 = ((bf16[32,12,8,128]{3,2,1,0:T(8,128)(2,1)}), bf16[32,12,8,128]{3,2,1,0:T(8,128)(2,1)S(1)}, u32[]{:S(2)}, u32[]{:S(2)}) async-start(bf16[32,12,8,128]{3,2,1,0:T(8,128)(2,1)} %pick.1), calls=%async_computation.2 | async-start | bytes 1572864 | tf_op jit(solution)/shard_map/all_to_all | solution.py:265
  46.8 0.1 reshape.68
  46.9 0.7 gather_fusion
  47.6 0.1 select_reduce_fusion.1.offs
  47.8 0.7 slice.18
  49.1 0.6 gather_fusion.1
  49.8 0.6 dynamic_slice.11
  50.4 10.7 %all-to-all-done.2.far = bf16[32,12,8,128]{3,2,1,0:T(8,128)(2,1)S(1)} async-done(((bf16[32,12,8,128]{3,2,1,0:T(8,128)(2,1)}), bf16[32,12,8,128]{3,2,1,0:T(8,128)(2,1)S(1)}, u32[]{:S(2)}, u32[]{:S(2)}) %all-to-all-start.2) | async-done | bytes 786464 | tf_op jit(solution)/shard_map/all_to_all | solution.py:265
  61.1 0.8 pack.1
  61.9 1.5 %collective-permute-start.5 = (bf16[152,8,128]{2,1,0:T(8,128)(2,1)S(1)}, bf16[152,8,128]{2,1,0:T(8,128)(2,1)S(1)}, u32[]{:S(2)}, u32[]{:S(2)}) collective-permute-start(bf16[152,8,128]{2,1,0:T(8,128)(2,1)S(1)} %get-tuple-element.12.far_k), channel_id=1, source_target_pairs={{0,1},{1,2},{2,3},{3,4},{4,5},{5,6},{6,7},{7,0},{8,9},{9,10},{10,1... | collective-permute-start | bytes 933896 | tf_op jit(solution)/shard_map/ppermute | solution.py:283
  63.4 2.9 %collective-permute-start.9 = (bf16[152,8,128]{2,1,0:T(8,128)(2,1)S(1)}, bf16[152,8,128]{2,1,0:T(8,128)(2,1)S(1)}, u32[]{:S(2)}, u32[]{:S(2)}) collective-permute-start(bf16[152,8,128]{2,1,0:T(8,128)(2,1)S(1)} %get-tuple-element.13.far_v), channel_id=1, source_target_pairs={{0,7},{1,0},{2,1},{3,2},{4,3},{5,4},{6,5},{7,6},{8,15},{9,8},{10,9... | collective-permute-start | bytes 933896 | tf_op jit(solution)/shard_map/ppermute | solution.py:284
  66.4 0.7 copy-done.1
  67.1 2.7 %collective-permute-start.13 = (bf16[152,8,128]{2,1,0:T(8,128)(2,1)S(1)}, bf16[152,8,128]{2,1,0:T(8,128)(2,1)}, u32[]{:S(2)}, u32[]{:S(2)}) collective-permute-start(bf16[152,8,128]{2,1,0:T(8,128)(2,1)S(1)} %get-tuple-element.12.far_k), channel_id=1, source_target_pairs={{0,7},{1,0},{2,1},{3,2},{4,3},{5,4},{6,5},{7,6},{8,15},{9,8},{10,9... | collective-permute-start | bytes 933896 | tf_op jit(solution)/shard_map/ppermute | solution.py:289
  69.8 4.3 %collective-permute-done.5.far_k = bf16[152,8,128]{2,1,0:T(8,128)(2,1)S(1)} collective-permute-done((bf16[152,8,128]{2,1,0:T(8,128)(2,1)S(1)}, bf16[152,8,128]{2,1,0:T(8,128)(2,1)S(1)}, u32[]{:S(2)}, u32[]{:S(2)}) %collective-permute-start.5) | collective-permute-done | bytes 311328 | tf_op jit(solution)/shard_map/ppermute | solution.py:283
  74.1 2.7 %collective-permute-start.10 = (bf16[152,8,128]{2,1,0:T(8,128)(2,1)S(1)}, bf16[152,8,128]{2,1,0:T(8,128)(2,1)}, u32[]{:S(2)}, u32[]{:S(2)}) collective-permute-start(bf16[152,8,128]{2,1,0:T(8,128)(2,1)S(1)} %collective-permute-done.9.far_v), channel_id=1, source_target_pairs={{0,7},{1,0},{2,1},{3,2},{4,3},{5,4},{6,5},{7,6},{8,15},{9,8},{10,9... | collective-permute-start | bytes 933896 | tf_op jit(solution)/shard_map/ppermute | solution.py:284
  76.8 0.2 select_reduce_fusion.2
  77.0 3.8 %collective-permute-done.16.far_v = bf16[152,8,128]{2,1,0:T(8,128)(2,1)S(1)} collective-permute-done((bf16[152,8,128]{2,1,0:T(8,128)(2,1)S(1)}, bf16[152,8,128]{2,1,0:T(8,128)(2,1)S(1)}, u32[]{:S(2)}, u32[]{:S(2)}) %collective-permute-start.16) | collective-permute-done | bytes 311328 | tf_op jit(solution)/shard_map/ppermute | solution.py:288
  80.8 0.0 collective-permute-start.17
  80.8 0.0 collective-permute-done.13.far_k
  80.8 2.7 %collective-permute-start.14 = (bf16[152,8,128]{2,1,0:T(8,128)(2,1)}, bf16[152,8,128]{2,1,0:T(8,128)(2,1)}, u32[]{:S(2)}, u32[]{:S(2)}) collective-permute-start(bf16[152,8,128]{2,1,0:T(8,128)(2,1)} %collective-permute-done.13.far_k), channel_id=1, source_target_pairs={{0,7},{1,0},{2,1},{3,2},{4,3},{5,4},{6,5},{7,6},{8,15},{9,8},{10,9... | collective-permute-start | bytes 933896 | tf_op jit(solution)/shard_map/ppermute | solution.py:289
  83.5 4.0 %collective-permute-done.6.far_k = bf16[152,8,128]{2,1,0:T(8,128)(2,1)} collective-permute-done((bf16[152,8,128]{2,1,0:T(8,128)(2,1)S(1)}, bf16[152,8,128]{2,1,0:T(8,128)(2,1)}, u32[]{:S(2)}, u32[]{:S(2)}) %collective-permute-start.6) | collective-permute-done | bytes 311328 | tf_op jit(solution)/shard_map/ppermute | solution.py:283
  87.5 0.0 collective-permute-start.7
  87.5 0.0 collective-permute-done.10.far_v
  87.6 2.7 %collective-permute-start.11 = (bf16[152,8,128]{2,1,0:T(8,128)(2,1)}, bf16[152,8,128]{2,1,0:T(8,128)(2,1)}, u32[]{:S(2)}, u32[]{:S(2)}) collective-permute-start(bf16[152,8,128]{2,1,0:T(8,128)(2,1)} %collective-permute-done.10.far_v), channel_id=1, source_target_pairs={{0,7},{1,0},{2,1},{3,2},{4,3},{5,4},{6,5},{7,6},{8,15},{9,8},{10,9... | collective-permute-start | bytes 933896 | tf_op jit(solution)/shard_map/ppermute | solution.py:284
  90.2 0.7 add_bitcast_fusion
  90.9 0.1 pad.12.clone
  91.0 0.1 copy.18
  91.1 3.1 %collective-permute-done.17.far_v = bf16[152,8,128]{2,1,0:T(8,128)(2,1)} collective-permute-done((bf16[152,8,128]{2,1,0:T(8,128)(2,1)S(1)}, bf16[152,8,128]{2,1,0:T(8,128)(2,1)}, u32[]{:S(2)}, u32[]{:S(2)}) %collective-permute-start.17) | collective-permute-done | bytes 311328 | tf_op jit(solution)/shard_map/ppermute | solution.py:288
  94.2 0.0 copy-start
  94.2 1.6 %copy-done = bf16[128,64,128]{2,1,0:T(8,128)(2,1)S(1)} copy-done((bf16[128,64,128]{2,1,0:T(8,128)(2,1)S(1)}, bf16[128,64,128]{2,1,0:T(8,128)(2,1)}, u32[]{:S(2)}) %copy-start) | copy-done | bytes 2097176
  95.8 0.6 stage.1.q
  96.5 2.7 %collective-permute-start.15 = (bf16[152,8,128]{2,1,0:T(8,128)(2,1)}, bf16[152,8,128]{2,1,0:T(8,128)(2,1)S(1)}, u32[]{:S(2)}, u32[]{:S(2)}) collective-permute-start(bf16[152,8,128]{2,1,0:T(8,128)(2,1)} %collective-permute-done.14.far_k), channel_id=1, source_target_pairs={{0,7},{1,0},{2,1},{3,2},{4,3},{5,4},{6,5},{7,6},{8,15},{9,8},{10,9... | collective-permute-start | bytes 933896 | tf_op jit(solution)/shard_map/ppermute | solution.py:289
  99.2 1.0 copy-done.2
  100.2 3.7 %attend.8._ = bf16[128,64,128]{2,1,0:T(8,128)(2,1)} custom-call(s32[8,19]{1,0:T(8,128)S(1)} %pad_add_fusion.meta, bf16[8,128,8,128]{3,2,1,0:T(8,128)(2,1)S(1)} %stage.1.q, bf16[32,8,8,128]{3,2,1,0:T(8,128)(2,1)} %bitcast.20.clone.2.own, bf16[152,8,128]{2,1,0:T(8,128)(2,1)S(1)} %get-tuple-element.12.far_k, ...), custom_call_target="tpu_custom_call", output_to_operand_aliasing={{}: (6, {})} | custom-call | flops 603979776 | bytes 2097152 | tf_op jit(solution)/shard_map/attend/pallas_call | solution.py:177
  103.9 0.0 collective-permute-done.11.far_v
  104.0 0.1 collective-permute-start.12
  104.0 0.0 collective-permute-done.7.far_k
  104.1 1.4 %collective-permute-start.8 = (bf16[152,8,128]{2,1,0:T(8,128)(2,1)}, bf16[152,8,128]{2,1,0:T(8,128)(2,1)S(1)}, u32[]{:S(2)}, u32[]{:S(2)}) collective-permute-start(bf16[152,8,128]{2,1,0:T(8,128)(2,1)} %collective-permute-done.7.far_k), channel_id=1, source_target_pairs={{0,1},{1,2},{2,3},{3,4},{4,5},{5,6},{6,7},{7,0},{8,9},{9,10},{10,1... | collective-permute-start | bytes 933896 | tf_op jit(solution)/shard_map/ppermute | solution.py:283
  105.5 3.6 %attend.9._ = bf16[128,64,128]{2,1,0:T(8,128)(2,1)} custom-call(s32[8,19]{1,0:T(8,128)S(1)} %pad_add_fusion.meta, bf16[8,128,8,128]{3,2,1,0:T(8,128)(2,1)S(1)} %stage.1.q, bf16[32,8,8,128]{3,2,1,0:T(8,128)(2,1)} %bitcast.20.clone.2.own, bf16[152,8,128]{2,1,0:T(8,128)(2,1)S(1)} %collective-permute-done.5.far_k, ...), custom_call_target="tpu_custom_call", output_to_operand_aliasing={{}: (6, {})} | custom-call | flops 603979776 | bytes 2097152 | tf_op jit(solution)/shard_map/attend/pallas_call | solution.py:177
  109.1 3.7 %attend.10._ = bf16[128,64,128]{2,1,0:T(8,128)(2,1)} custom-call(s32[8,19]{1,0:T(8,128)S(1)} %pad_add_fusion.meta, bf16[8,128,8,128]{3,2,1,0:T(8,128)(2,1)S(1)} %stage.1.q, bf16[32,8,8,128]{3,2,1,0:T(8,128)(2,1)} %bitcast.20.clone.2.own, bf16[152,8,128]{2,1,0:T(8,128)(2,1)} %collective-permute-done.13.far_k, ...), custom_call_target="tpu_custom_call", output_to_operand_aliasing={{}: (6, {})} | custom-call | flops 603979776 | bytes 2097152 | tf_op jit(solution)/shard_map/attend/pallas_call | solution.py:177
  112.9 4.0 %attend.11._ = bf16[128,64,128]{2,1,0:T(8,128)(2,1)} custom-call(s32[8,19]{1,0:T(8,128)S(1)} %pad_add_fusion.meta, bf16[8,128,8,128]{3,2,1,0:T(8,128)(2,1)S(1)} %stage.1.q, bf16[32,8,8,128]{3,2,1,0:T(8,128)(2,1)} %bitcast.20.clone.2.own, bf16[152,8,128]{2,1,0:T(8,128)(2,1)} %collective-permute-done.6.far_k, ...), custom_call_target="tpu_custom_call", output_to_operand_aliasing={{}: (6, {})} | custom-call | flops 603979776 | bytes 2097152 | tf_op jit(solution)/shard_map/attend/pallas_call | solution.py:177
  116.9 3.8 %attend.12._ = bf16[128,64,128]{2,1,0:T(8,128)(2,1)} custom-call(s32[8,19]{1,0:T(8,128)S(1)} %pad_add_fusion.meta, bf16[8,128,8,128]{3,2,1,0:T(8,128)(2,1)S(1)} %stage.1.q, bf16[32,8,8,128]{3,2,1,0:T(8,128)(2,1)} %bitcast.20.clone.2.own, bf16[152,8,128]{2,1,0:T(8,128)(2,1)} %collective-permute-done.14.far_k, ...), custom_call_target="tpu_custom_call", output_to_operand_aliasing={{}: (6, {})} | custom-call | flops 603979776 | bytes 2097152 | tf_op jit(solution)/shard_map/attend/pallas_call | solution.py:177
  120.7 3.8 %attend.13._ = bf16[128,64,128]{2,1,0:T(8,128)(2,1)} custom-call(s32[8,19]{1,0:T(8,128)S(1)} %pad_add_fusion.meta, bf16[8,128,8,128]{3,2,1,0:T(8,128)(2,1)S(1)} %stage.1.q, bf16[32,8,8,128]{3,2,1,0:T(8,128)(2,1)} %bitcast.20.clone.2.own, bf16[152,8,128]{2,1,0:T(8,128)(2,1)} %collective-permute-done.7.far_k, ...), custom_call_target="tpu_custom_call", output_to_operand_aliasing={{}: (6, {})} | custom-call | flops 603979776 | bytes 2097152 | tf_op jit(solution)/shard_map/attend/pallas_call | solution.py:177
  124.5 3.7 %attend.14._ = bf16[128,64,128]{2,1,0:T(8,128)(2,1)} custom-call(s32[8,19]{1,0:T(8,128)S(1)} %pad_add_fusion.meta, bf16[8,128,8,128]{3,2,1,0:T(8,128)(2,1)S(1)} %stage.1.q, bf16[32,8,8,128]{3,2,1,0:T(8,128)(2,1)} %bitcast.20.clone.2.own, bf16[152,8,128]{2,1,0:T(8,128)(2,1)S(1)} %collective-permute-done.15.far_k, ...), custom_call_target="tpu_custom_call", output_to_operand_aliasing={{}: (6, {})} | custom-call | flops 603979776 | bytes 2097152 | tf_op jit(solution)/shard_map/attend/pallas_call | solution.py:177
  128.3 3.6 %attend.15 = bf16[128,64,128]{2,1,0:T(8,128)(2,1)} custom-call(s32[8,19]{1,0:T(8,128)S(1)} %pad_add_fusion.meta, bf16[8,128,8,128]{3,2,1,0:T(8,128)(2,1)S(1)} %stage.1.q, bf16[32,8,8,128]{3,2,1,0:T(8,128)(2,1)} %bitcast.20.clone.2.own, bf16[152,8,128]{2,1,0:T(8,128)(2,1)S(1)} %collective-permute-done.8.far_k, ...), custom_call_target="tpu_custom_call", output_to_operand_aliasing={{}: (6, {})} | custom-call | flops 603979776 | bytes 2097152 | tf_op jit(solution)/shard_map/attend/pallas_call | solution.py:177
  (38 shorter events, 0.2 us)
Async XLA Ops:
  0.0 17.7 %copy-start.5 = (s32[8,8]{1,0:T(8,128)S(1)}, s32[8,8]{1,0:T(8,128)}, u32[]{:S(2)}) copy-start(s32[8,8]{1,0:T(8,128)} %param.11) | copy-start | bytes 772
  2.0 44.9 %copy-start.3 = (s32[256]{0:T(256)S(1)}, s32[256]{0:T(256)}, u32[]{:S(2)}) copy-start(s32[256]{0:T(256)} %param.12) | copy-start | bytes 3076
  2.0 36.8 %all-to-all-start.1 = ((bf16[256,8,128]{2,1,0:T(8,128)(2,1)}), bf16[256,8,128]{2,1,0:T(8,128)(2,1)S(1)}, u32[]{:S(2)}, u32[]{:S(2)}) async-start(bf16[256,8,128]{2,1,0:T(8,128)(2,1)} %bitcast.12), calls=%async_computation.1 | async-start | bytes 1048576 | tf_op jit(solution)/shard_map/all_to_all | solution.py:263
  18.2 3.0 %collective-permute-start = (s32[1,128]{1,0:T(1,128)S(1)}, s32[1,128]{1,0:T(1,128)S(1)}, u32[]{:S(2)}, u32[]{:S(2)}) collective-permute-start(s32[1,128]{1,0:T(1,128)S(1)} %bitcast.25), channel_id=1, source_target_pairs={{0,8},{8,0},{16,24},{24,16},{32,40},{40,32},{48,56},{56,48},{64,72... | collective-permute-start | bytes 1544 | tf_op jit(solution)/shard_map/ppermute | solution.py:241
  21.3 2.7 %collective-permute-start.1 = (s32[2,128]{1,0:T(2,128)S(1)}, s32[2,128]{1,0:T(2,128)S(1)}, u32[]{:S(2)}, u32[]{:S(2)}) collective-permute-start(s32[2,128]{1,0:T(2,128)S(1)} %pad_add_fusion.3), channel_id=1, source_target_pairs={{0,16},{8,24},{16,0},{24,8},{32,48},{40,56},{48,32},{56,40},{64,80... | collective-permute-start | bytes 3080 | tf_op jit(solution)/shard_map/ppermute | solution.py:241
  24.0 4.3 %collective-permute-start.2 = (s32[4,128]{1,0:T(4,128)S(1)}, s32[4,128]{1,0:T(4,128)S(1)}, u32[]{:S(2)}, u32[]{:S(2)}) collective-permute-start(s32[4,128]{1,0:T(4,128)S(1)} %pad_add_fusion.2), channel_id=1, source_target_pairs={{0,32},{8,40},{16,48},{24,56},{32,0},{40,8},{48,16},{56,24},{64,96... | collective-permute-start | bytes 6152 | tf_op jit(solution)/shard_map/ppermute | solution.py:241
  28.4 2.8 %collective-permute-start.3 = (s32[8,128]{1,0:T(8,128)S(1)}, s32[8,128]{1,0:T(8,128)S(1)}, u32[]{:S(2)}, u32[]{:S(2)}) collective-permute-start(s32[8,128]{1,0:T(8,128)S(1)} %pad_add_fusion.1), channel_id=1, source_target_pairs={{0,64},{8,72},{16,80},{24,88},{32,96},{40,104},{48,112},{56,120},{... | collective-permute-start | bytes 12296 | tf_op jit(solution)/shard_map/ppermute | solution.py:241
  31.2 4.4 %collective-permute-start.4 = (s32[16,128]{1,0:T(8,128)S(1)}, s32[16,128]{1,0:T(8,128)S(1)}, u32[]{:S(2)}, u32[]{:S(2)}) collective-permute-start(s32[16,128]{1,0:T(8,128)S(1)} %concatenate.34), channel_id=1, source_target_pairs={{0,128},{8,136},{16,144},{24,152},{32,160},{40,168},{48,176},{56,1... | collective-permute-start | bytes 24584 | tf_op jit(solution)/shard_map/ppermute | solution.py:241
  38.8 42.0 %copy-start.6 = (s32[8]{0:T(128)S(1)}, s32[8]{0:T(128)}, u32[]{:S(2)}) copy-start(s32[8]{0:T(128)} %constant.77.clone) | copy-start | bytes 100
  40.9 20.1 %all-to-all-start.2 = ((bf16[32,12,8,128]{3,2,1,0:T(8,128)(2,1)}), bf16[32,12,8,128]{3,2,1,0:T(8,128)(2,1)S(1)}, u32[]{:S(2)}, u32[]{:S(2)}) async-start(bf16[32,12,8,128]{3,2,1,0:T(8,128)(2,1)} %pick.1), calls=%async_computation.2 | async-start | bytes 1572864 | tf_op jit(solution)/shard_map/all_to_all | solution.py:265
  61.9 12.2 %collective-permute-start.5 = (bf16[152,8,128]{2,1,0:T(8,128)(2,1)S(1)}, bf16[152,8,128]{2,1,0:T(8,128)(2,1)S(1)}, u32[]{:S(2)}, u32[]{:S(2)}) collective-permute-start(bf16[152,8,128]{2,1,0:T(8,128)(2,1)S(1)} %get-tuple-element.12.far_k), channel_id=1, source_target_pairs={{0,1},{1,2},{2,3},{3,4},{4,5},{5,6},{6,7},{7,0},{8,9},{9,10},{10,1... | collective-permute-start | bytes 933896 | tf_op jit(solution)/shard_map/ppermute | solution.py:283
  63.4 10.7 %collective-permute-start.9 = (bf16[152,8,128]{2,1,0:T(8,128)(2,1)S(1)}, bf16[152,8,128]{2,1,0:T(8,128)(2,1)S(1)}, u32[]{:S(2)}, u32[]{:S(2)}) collective-permute-start(bf16[152,8,128]{2,1,0:T(8,128)(2,1)S(1)} %get-tuple-element.13.far_v), channel_id=1, source_target_pairs={{0,7},{1,0},{2,1},{3,2},{4,3},{5,4},{6,5},{7,6},{8,15},{9,8},{10,9... | collective-permute-start | bytes 933896 | tf_op jit(solution)/shard_map/ppermute | solution.py:284
  66.4 14.4 %collective-permute-start.16 = (bf16[152,8,128]{2,1,0:T(8,128)(2,1)S(1)}, bf16[152,8,128]{2,1,0:T(8,128)(2,1)S(1)}, u32[]{:S(2)}, u32[]{:S(2)}) collective-permute-start(bf16[152,8,128]{2,1,0:T(8,128)(2,1)S(1)} %get-tuple-element.13.far_v), channel_id=1, source_target_pairs={{0,1},{1,2},{2,3},{3,4},{4,5},{5,6},{6,7},{7,0},{8,9},{9,10},{10,1... | collective-permute-start | bytes 933896 | tf_op jit(solution)/shard_map/ppermute | solution.py:288
  66.4 0.7 copy-start.1
  67.1 13.7 %collective-permute-start.13 = (bf16[152,8,128]{2,1,0:T(8,128)(2,1)S(1)}, bf16[152,8,128]{2,1,0:T(8,128)(2,1)}, u32[]{:S(2)}, u32[]{:S(2)}) collective-permute-start(bf16[152,8,128]{2,1,0:T(8,128)(2,1)S(1)} %get-tuple-element.12.far_k), channel_id=1, source_target_pairs={{0,7},{1,0},{2,1},{3,2},{4,3},{5,4},{6,5},{7,6},{8,15},{9,8},{10,9... | collective-permute-start | bytes 933896 | tf_op jit(solution)/shard_map/ppermute | solution.py:289
  74.1 13.4 %collective-permute-start.6 = (bf16[152,8,128]{2,1,0:T(8,128)(2,1)S(1)}, bf16[152,8,128]{2,1,0:T(8,128)(2,1)}, u32[]{:S(2)}, u32[]{:S(2)}) collective-permute-start(bf16[152,8,128]{2,1,0:T(8,128)(2,1)S(1)} %collective-permute-done.5.far_k), channel_id=1, source_target_pairs={{0,1},{1,2},{2,3},{3,4},{4,5},{5,6},{6,7},{7,0},{8,9},{9,10},{10,1... | collective-permute-start | bytes 933896 | tf_op jit(solution)/shard_map/ppermute | solution.py:283
  74.1 13.4 %collective-permute-start.10 = (bf16[152,8,128]{2,1,0:T(8,128)(2,1)S(1)}, bf16[152,8,128]{2,1,0:T(8,128)(2,1)}, u32[]{:S(2)}, u32[]{:S(2)}) collective-permute-start(bf16[152,8,128]{2,1,0:T(8,128)(2,1)S(1)} %collective-permute-done.9.far_v), channel_id=1, source_target_pairs={{0,7},{1,0},{2,1},{3,2},{4,3},{5,4},{6,5},{7,6},{8,15},{9,8},{10,9... | collective-permute-start | bytes 933896 | tf_op jit(solution)/shard_map/ppermute | solution.py:284
  80.8 13.4 %collective-permute-start.17 = (bf16[152,8,128]{2,1,0:T(8,128)(2,1)S(1)}, bf16[152,8,128]{2,1,0:T(8,128)(2,1)}, u32[]{:S(2)}, u32[]{:S(2)}) collective-permute-start(bf16[152,8,128]{2,1,0:T(8,128)(2,1)S(1)} %collective-permute-done.16.far_v), channel_id=1, source_target_pairs={{0,1},{1,2},{2,3},{3,4},{4,5},{5,6},{6,7},{7,0},{8,9},{9,10},{10,1... | collective-permute-start | bytes 933896 | tf_op jit(solution)/shard_map/ppermute | solution.py:288
  80.8 15.7 %collective-permute-start.14 = (bf16[152,8,128]{2,1,0:T(8,128)(2,1)}, bf16[152,8,128]{2,1,0:T(8,128)(2,1)}, u32[]{:S(2)}, u32[]{:S(2)}) collective-permute-start(bf16[152,8,128]{2,1,0:T(8,128)(2,1)} %collective-permute-done.13.far_k), channel_id=1, source_target_pairs={{0,7},{1,0},{2,1},{3,2},{4,3},{5,4},{6,5},{7,6},{8,15},{9,8},{10,9... | collective-permute-start | bytes 933896 | tf_op jit(solution)/shard_map/ppermute | solution.py:289
  87.5 16.5 %collective-permute-start.7 = (bf16[152,8,128]{2,1,0:T(8,128)(2,1)}, bf16[152,8,128]{2,1,0:T(8,128)(2,1)}, u32[]{:S(2)}, u32[]{:S(2)}) collective-permute-start(bf16[152,8,128]{2,1,0:T(8,128)(2,1)} %collective-permute-done.6.far_k), channel_id=1, source_target_pairs={{0,1},{1,2},{2,3},{3,4},{4,5},{5,6},{6,7},{7,0},{8,9},{9,10},{10,1... | collective-permute-start | bytes 933896 | tf_op jit(solution)/shard_map/ppermute | solution.py:283
  87.6 16.4 %collective-permute-start.11 = (bf16[152,8,128]{2,1,0:T(8,128)(2,1)}, bf16[152,8,128]{2,1,0:T(8,128)(2,1)}, u32[]{:S(2)}, u32[]{:S(2)}) collective-permute-start(bf16[152,8,128]{2,1,0:T(8,128)(2,1)} %collective-permute-done.10.far_v), channel_id=1, source_target_pairs={{0,7},{1,0},{2,1},{3,2},{4,3},{5,4},{6,5},{7,6},{8,15},{9,8},{10,9... | collective-permute-start | bytes 933896 | tf_op jit(solution)/shard_map/ppermute | solution.py:284
  94.2 26.5 %collective-permute-start.18 = (bf16[152,8,128]{2,1,0:T(8,128)(2,1)}, bf16[152,8,128]{2,1,0:T(8,128)(2,1)}, u32[]{:S(2)}, u32[]{:S(2)}) collective-permute-start(bf16[152,8,128]{2,1,0:T(8,128)(2,1)} %collective-permute-done.17.far_v), channel_id=1, source_target_pairs={{0,1},{1,2},{2,3},{3,4},{4,5},{5,6},{6,7},{7,0},{8,9},{9,10},{10,1... | collective-permute-start | bytes 933896 | tf_op jit(solution)/shard_map/ppermute | solution.py:288
  94.2 1.6 %copy-start = (bf16[128,64,128]{2,1,0:T(8,128)(2,1)S(1)}, bf16[128,64,128]{2,1,0:T(8,128)(2,1)}, u32[]{:S(2)}) copy-start(bf16[128,64,128]{2,1,0:T(8,128)(2,1)} %q.1) | copy-start | bytes 6291460
  96.5 28.0 %collective-permute-start.15 = (bf16[152,8,128]{2,1,0:T(8,128)(2,1)}, bf16[152,8,128]{2,1,0:T(8,128)(2,1)S(1)}, u32[]{:S(2)}, u32[]{:S(2)}) collective-permute-start(bf16[152,8,128]{2,1,0:T(8,128)(2,1)} %collective-permute-done.14.far_k), channel_id=1, source_target_pairs={{0,7},{1,0},{2,1},{3,2},{4,3},{5,4},{6,5},{7,6},{8,15},{9,8},{10,9... | collective-permute-start | bytes 933896 | tf_op jit(solution)/shard_map/ppermute | solution.py:289
  99.2 1.0 copy-start.2
  100.2 5.3 %copy-start.4 = (bf16[8,2,40,8,128]{4,3,2,1,0:T(8,128)(2,1)S(1)}, bf16[8,2,40,8,128]{4,3,2,1,0:T(8,128)(2,1)}, u32[]{:S(2)}) copy-start(bf16[8,2,40,8,128]{4,3,2,1,0:T(8,128)(2,1)} %get-tuple-element.17.rest) | copy-start | bytes 3932164
  104.0 24.3 %collective-permute-start.12 = (bf16[152,8,128]{2,1,0:T(8,128)(2,1)}, bf16[152,8,128]{2,1,0:T(8,128)(2,1)S(1)}, u32[]{:S(2)}, u32[]{:S(2)}) collective-permute-start(bf16[152,8,128]{2,1,0:T(8,128)(2,1)} %collective-permute-done.11.far_v), channel_id=1, source_target_pairs={{0,7},{1,0},{2,1},{3,2},{4,3},{5,4},{6,5},{7,6},{8,15},{9,8},{10,9... | collective-permute-start | bytes 933896 | tf_op jit(solution)/shard_map/ppermute | solution.py:284
  104.1 24.2 %collective-permute-start.8 = (bf16[152,8,128]{2,1,0:T(8,128)(2,1)}, bf16[152,8,128]{2,1,0:T(8,128)(2,1)S(1)}, u32[]{:S(2)}, u32[]{:S(2)}) collective-permute-start(bf16[152,8,128]{2,1,0:T(8,128)(2,1)} %collective-permute-done.7.far_k), channel_id=1, source_target_pairs={{0,1},{1,2},{2,3},{3,4},{4,5},{5,6},{6,7},{7,0},{8,9},{9,10},{10,1... | collective-permute-start | bytes 933896 | tf_op jit(solution)/shard_map/ppermute | solution.py:283

commit v5 on v4

--- a/solution.py
+++ b/solution.py
@@ -101,7 +101,7 @@
     over = meta[call, 18]
     lane = lax.broadcasted_iota(jnp.int32, (1, BS), 1)
     keys[0:BS, :] = own[0:16, g].reshape(BS, BS)
-    vals[0:BS, 0:BS] = own[16:32, g].reshape(BS, BS)
+    vals[0:BS, :] = own[16:32, g].reshape(BS, BS)
 
     def start(j, room):
         return jnp.minimum(meta[call, 1 + j], room - PIECES)
@@ -111,7 +111,7 @@
             at = slice((j + 1) * BS, (j + 2) * BS)
             pieces = pl.ds(start(j, room), PIECES)
             keys[at, :] = from_k[pieces].reshape(BS, BS)
-            vals[at, 0:BS] = from_v[pieces].reshape(BS, BS)
+            vals[at, :] = from_v[pieces].reshape(BS, BS)
 
     @pl.when(over == 0)
     def _():
@@ -134,7 +134,6 @@
     for j in range(far):
         low = (meta[call, 1 + j] - start(j, room)) * TILE
         bias.append(jnp.where((lane >= low) & (lane < low + meta[call, 9 + j]), 0.0, NEG))
-    vals[:, BS:] = jnp.ones((vals.shape[0], BS), jnp.bfloat16)
 
     tokens = 32
     rows = tokens * 8
@@ -161,8 +160,9 @@
 
     every = [scores(i) for i in range(parts)]
     every = [weights(s) for s in every]
+    wide = jnp.concatenate([vals[...], jnp.ones((9 * BS, BS), jnp.bfloat16)], axis=1)
     for i in range(parts):
-        o = jnp.dot(every[i], vals[...], preferred_element_type=jnp.float32)
+        o = jnp.dot(every[i], wide, preferred_element_type=jnp.float32)
         r = o[:, 0:BS] / o[:, BS:]
         held[i * tokens : (i + 1) * tokens] = r.reshape(tokens, 8, BS).astype(out.dtype)
         leave(i).start()
@@ -181,7 +181,7 @@
         out_specs=hbm,
         scratch_shapes=[
             pltpu.VMEM((9 * BS, BS), jnp.bfloat16),
-            pltpu.VMEM((9 * BS, 2 * BS), jnp.bfloat16),
+            pltpu.VMEM((9 * BS, BS), jnp.bfloat16),
             pltpu.VMEM((BS, 8, BS), jnp.bfloat16),
             pltpu.VMEM((ALL, TILE, BS), jnp.bfloat16),
             pltpu.VMEM((ALL, TILE, BS), jnp.bfloat16),

time: 133 us -> 132 us (level)
  no operation moved by 1% of the time
where the time goes in v5:
time: 132 us; the launch traced here: 131 us
  starting transfers between devices  46 us (35%)
  waiting for transfers between devices  41.5 us (31%)
  Pallas kernels  32.8 us (25%)
  local copies, waits for them, and re-layouts  7.11 us (5%)
  other arithmetic  2.65 us (2%)
    pallas_call x8, Pallas kernels, attend(): pl.pallas_call(functools.partial(attend_kernel, scale, call), out_shape=j...  29.2 us
    all_to_all x1, starting transfers between devices, attention(): lax.all_to_all(own.reshape(n_seq * n_head, TILE, BS), ('seq', 'head'), 0,...  15.6 us
    ppermute x5, waiting for transfers between devices, attention(): other = lax.ppermute(pools, 'seq', [(i, i ^ bit) for i in range(n_seq)])  12.5 us
    all_to_all x1, waiting for transfers between devices, attention(): far = lax.all_to_all(picked, 'seq', 0, 0, tiled=True)  10.7 us
    ppermute x4, starting transfers between devices, attention(): v_down = lax.ppermute(v_down, 'head', down)  8.36 us
    ppermute x4, waiting for transfers between devices, attention(): k_up = lax.ppermute(k_up, 'head', up)  8.26 us
    ppermute x3, starting transfers between devices, attention(): k_down = lax.ppermute(k_down, 'head', down)  8.23 us
    ppermute x3, waiting for transfers between devices, attention(): v_up = lax.ppermute(v_up, 'head', up)  6.94 us
  transfers between devices with their start and end apart: 21, of which 11 were waited for; matrix products, arithmetic and copies ran while one was open for 3% of the time, Pallas kernels for 20%

profile of v5, /device:TPU:1, one launch (start us, length us, event | category | flops | bytes accessed | tf_op | source)
XLA Modules:
  0.0 131.3 jit_solution(16840936206531644743)
XLA Ops:
  0.0 1.1 pad_maximum_fusion
  1.1 0.9 copy.22
  2.0 15.6 %all-to-all-start.1 = ((bf16[256,8,128]{2,1,0:T(8,128)(2,1)}), bf16[256,8,128]{2,1,0:T(8,128)(2,1)S(1)}, u32[]{:S(2)}, u32[]{:S(2)}) async-start(bf16[256,8,128]{2,1,0:T(8,128)(2,1)} %bitcast.12), calls=%async_computation.1 | async-start | bytes 1048576 | tf_op jit(solution)/shard_map/all_to_all | solution.py:263
  17.7 0.1 eq.45
  17.7 0.2 fusion.1
  17.9 0.2 convert_reduce_fusion
  18.1 0.1 select_reduce_fusion
  18.2 2.2 %collective-permute-start = (s32[1,128]{1,0:T(1,128)S(1)}, s32[1,128]{1,0:T(1,128)S(1)}, u32[]{:S(2)}, u32[]{:S(2)}) collective-permute-start(s32[1,128]{1,0:T(1,128)S(1)} %bitcast.25), channel_id=1, source_target_pairs={{0,8},{8,0},{16,24},{24,16},{32,40},{40,32},{48,56},{56,48},{64,72... | collective-permute-start | bytes 1544 | tf_op jit(solution)/shard_map/ppermute | solution.py:241
  20.5 0.8 collective-permute-done
  21.3 0.0 collective-permute-start.1
  21.3 2.7 %collective-permute-done.1 = s32[2,128]{1,0:T(2,128)S(1)} collective-permute-done((s32[2,128]{1,0:T(2,128)S(1)}, s32[2,128]{1,0:T(2,128)S(1)}, u32[]{:S(2)}, u32[]{:S(2)}) %collective-permute-start.1) | collective-permute-done | bytes 1056 | tf_op jit(solution)/shard_map/ppermute | solution.py:241
  24.0 1.2 collective-permute-start.2
  25.2 3.1 %collective-permute-done.2 = s32[4,128]{1,0:T(4,128)S(1)} collective-permute-done((s32[4,128]{1,0:T(4,128)S(1)}, s32[4,128]{1,0:T(4,128)S(1)}, u32[]{:S(2)}, u32[]{:S(2)}) %collective-permute-start.2) | collective-permute-done | bytes 2080 | tf_op jit(solution)/shard_map/ppermute | solution.py:241
  28.4 0.1 collective-permute-start.3
  28.5 2.7 %collective-permute-done.3 = s32[8,128]{1,0:T(8,128)S(1)} collective-permute-done((s32[8,128]{1,0:T(8,128)S(1)}, s32[8,128]{1,0:T(8,128)S(1)}, u32[]{:S(2)}, u32[]{:S(2)}) %collective-permute-start.3) | collective-permute-done | bytes 4128 | tf_op jit(solution)/shard_map/ppermute | solution.py:241
  31.2 1.3 %collective-permute-start.4 = (s32[16,128]{1,0:T(8,128)S(1)}, s32[16,128]{1,0:T(8,128)S(1)}, u32[]{:S(2)}, u32[]{:S(2)}) collective-permute-start(s32[16,128]{1,0:T(8,128)S(1)} %concatenate.34), channel_id=1, source_target_pairs={{0,128},{8,136},{16,144},{24,152},{32,160},{40,168},{48,176},{56,1... | collective-permute-start | bytes 24584 | tf_op jit(solution)/shard_map/ppermute | solution.py:241
  32.6 3.0 %collective-permute-done.4 = s32[16,128]{1,0:T(8,128)S(1)} collective-permute-done((s32[16,128]{1,0:T(8,128)S(1)}, s32[16,128]{1,0:T(8,128)S(1)}, u32[]{:S(2)}, u32[]{:S(2)}) %collective-permute-start.4) | collective-permute-done | bytes 8224 | tf_op jit(solution)/shard_map/ppermute | solution.py:241
  35.6 3.1 %all-to-all-done.1.held = bf16[256,8,128]{2,1,0:T(8,128)(2,1)S(1)} async-done(((bf16[256,8,128]{2,1,0:T(8,128)(2,1)}), bf16[256,8,128]{2,1,0:T(8,128)(2,1)S(1)}, u32[]{:S(2)}, u32[]{:S(2)}) %all-to-all-start.1) | async-done | bytes 524320 | tf_op jit(solution)/shard_map/all_to_all | solution.py:263
  38.8 2.2 %pick.1 = bf16[32,12,8,128]{3,2,1,0:T(8,128)(2,1)} custom-call(s32[32,128]{1,0:T(8,128)S(1)} %concatenate.35.pools, s32[1]{0:T(128)} %bitcast.11.me, bf16[256,8,128]{2,1,0:T(8,128)(2,1)S(1)} %all-to-all-done.1.held), custom_call_target="tpu_custom_call" | custom-call | tf_op jit(solution)/shard_map/pick/pallas_call | solution.py:57
  40.9 5.9 %all-to-all-start.2 = ((bf16[32,12,8,128]{3,2,1,0:T(8,128)(2,1)}), bf16[32,12,8,128]{3,2,1,0:T(8,128)(2,1)S(1)}, u32[]{:S(2)}, u32[]{:S(2)}) async-start(bf16[32,12,8,128]{3,2,1,0:T(8,128)(2,1)} %pick.1), calls=%async_computation.2 | async-start | bytes 1572864 | tf_op jit(solution)/shard_map/all_to_all | solution.py:265
  46.8 0.1 reshape.68
  46.9 0.7 gather_fusion
  47.6 0.1 select_reduce_fusion.1.offs
  47.8 0.7 slice.18
  49.1 0.6 gather_fusion.1
  49.8 0.6 dynamic_slice.11
  50.4 10.7 %all-to-all-done.2.far = bf16[32,12,8,128]{3,2,1,0:T(8,128)(2,1)S(1)} async-done(((bf16[32,12,8,128]{3,2,1,0:T(8,128)(2,1)}), bf16[32,12,8,128]{3,2,1,0:T(8,128)(2,1)S(1)}, u32[]{:S(2)}, u32[]{:S(2)}) %all-to-all-start.2) | async-done | bytes 786464 | tf_op jit(solution)/shard_map/all_to_all | solution.py:265
  61.1 0.8 pack.1
  61.9 1.5 %collective-permute-start.5 = (bf16[152,8,128]{2,1,0:T(8,128)(2,1)S(1)}, bf16[152,8,128]{2,1,0:T(8,128)(2,1)S(1)}, u32[]{:S(2)}, u32[]{:S(2)}) collective-permute-start(bf16[152,8,128]{2,1,0:T(8,128)(2,1)S(1)} %get-tuple-element.12.far_k), channel_id=1, source_target_pairs={{0,1},{1,2},{2,3},{3,4},{4,5},{5,6},{6,7},{7,0},{8,9},{9,10},{10,1... | collective-permute-start | bytes 933896 | tf_op jit(solution)/shard_map/ppermute | solution.py:283
  63.4 2.9 %collective-permute-start.9 = (bf16[152,8,128]{2,1,0:T(8,128)(2,1)S(1)}, bf16[152,8,128]{2,1,0:T(8,128)(2,1)S(1)}, u32[]{:S(2)}, u32[]{:S(2)}) collective-permute-start(bf16[152,8,128]{2,1,0:T(8,128)(2,1)S(1)} %get-tuple-element.13.far_v), channel_id=1, source_target_pairs={{0,7},{1,0},{2,1},{3,2},{4,3},{5,4},{6,5},{7,6},{8,15},{9,8},{10,9... | collective-permute-start | bytes 933896 | tf_op jit(solution)/shard_map/ppermute | solution.py:284
  66.4 0.0 collective-permute-start.16
  66.4 0.7 copy-done.1
  67.1 2.7 %collective-permute-start.13 = (bf16[152,8,128]{2,1,0:T(8,128)(2,1)S(1)}, bf16[152,8,128]{2,1,0:T(8,128)(2,1)}, u32[]{:S(2)}, u32[]{:S(2)}) collective-permute-start(bf16[152,8,128]{2,1,0:T(8,128)(2,1)S(1)} %get-tuple-element.12.far_k), channel_id=1, source_target_pairs={{0,7},{1,0},{2,1},{3,2},{4,3},{5,4},{6,5},{7,6},{8,15},{9,8},{10,9... | collective-permute-start | bytes 933896 | tf_op jit(solution)/shard_map/ppermute | solution.py:289
  69.8 4.3 %collective-permute-done.5.far_k = bf16[152,8,128]{2,1,0:T(8,128)(2,1)S(1)} collective-permute-done((bf16[152,8,128]{2,1,0:T(8,128)(2,1)S(1)}, bf16[152,8,128]{2,1,0:T(8,128)(2,1)S(1)}, u32[]{:S(2)}, u32[]{:S(2)}) %collective-permute-start.5) | collective-permute-done | bytes 311328 | tf_op jit(solution)/shard_map/ppermute | solution.py:283
  74.1 0.0 collective-permute-start.6
  74.1 2.7 %collective-permute-start.10 = (bf16[152,8,128]{2,1,0:T(8,128)(2,1)S(1)}, bf16[152,8,128]{2,1,0:T(8,128)(2,1)}, u32[]{:S(2)}, u32[]{:S(2)}) collective-permute-start(bf16[152,8,128]{2,1,0:T(8,128)(2,1)S(1)} %collective-permute-done.9.far_v), channel_id=1, source_target_pairs={{0,7},{1,0},{2,1},{3,2},{4,3},{5,4},{6,5},{7,6},{8,15},{9,8},{10,9... | collective-permute-start | bytes 933896 | tf_op jit(solution)/shard_map/ppermute | solution.py:284
  76.8 0.2 select_reduce_fusion.2
  77.0 3.8 %collective-permute-done.16.far_v = bf16[152,8,128]{2,1,0:T(8,128)(2,1)S(1)} collective-permute-done((bf16[152,8,128]{2,1,0:T(8,128)(2,1)S(1)}, bf16[152,8,128]{2,1,0:T(8,128)(2,1)S(1)}, u32[]{:S(2)}, u32[]{:S(2)}) %collective-permute-start.16) | collective-permute-done | bytes 311328 | tf_op jit(solution)/shard_map/ppermute | solution.py:288
  80.8 0.0 collective-permute-start.17
  80.8 0.0 collective-permute-done.13.far_k
  80.8 2.7 %collective-permute-start.14 = (bf16[152,8,128]{2,1,0:T(8,128)(2,1)}, bf16[152,8,128]{2,1,0:T(8,128)(2,1)}, u32[]{:S(2)}, u32[]{:S(2)}) collective-permute-start(bf16[152,8,128]{2,1,0:T(8,128)(2,1)} %collective-permute-done.13.far_k), channel_id=1, source_target_pairs={{0,7},{1,0},{2,1},{3,2},{4,3},{5,4},{6,5},{7,6},{8,15},{9,8},{10,9... | collective-permute-start | bytes 933896 | tf_op jit(solution)/shard_map/ppermute | solution.py:289
  83.5 4.0 %collective-permute-done.6.far_k = bf16[152,8,128]{2,1,0:T(8,128)(2,1)} collective-permute-done((bf16[152,8,128]{2,1,0:T(8,128)(2,1)S(1)}, bf16[152,8,128]{2,1,0:T(8,128)(2,1)}, u32[]{:S(2)}, u32[]{:S(2)}) %collective-permute-start.6) | collective-permute-done | bytes 311328 | tf_op jit(solution)/shard_map/ppermute | solution.py:283
  87.5 0.0 collective-permute-start.7
  87.5 0.0 collective-permute-done.10.far_v
  87.6 2.7 %collective-permute-start.11 = (bf16[152,8,128]{2,1,0:T(8,128)(2,1)}, bf16[152,8,128]{2,1,0:T(8,128)(2,1)}, u32[]{:S(2)}, u32[]{:S(2)}) collective-permute-start(bf16[152,8,128]{2,1,0:T(8,128)(2,1)} %collective-permute-done.10.far_v), channel_id=1, source_target_pairs={{0,7},{1,0},{2,1},{3,2},{4,3},{5,4},{6,5},{7,6},{8,15},{9,8},{10,9... | collective-permute-start | bytes 933896 | tf_op jit(solution)/shard_map/ppermute | solution.py:284
  90.2 0.7 add_bitcast_fusion
  90.9 0.1 pad.12.clone
  91.0 0.1 copy.18
  91.1 3.1 %collective-permute-done.17.far_v = bf16[152,8,128]{2,1,0:T(8,128)(2,1)} collective-permute-done((bf16[152,8,128]{2,1,0:T(8,128)(2,1)S(1)}, bf16[152,8,128]{2,1,0:T(8,128)(2,1)}, u32[]{:S(2)}, u32[]{:S(2)}) %collective-permute-start.17) | collective-permute-done | bytes 311328 | tf_op jit(solution)/shard_map/ppermute | solution.py:288
  94.2 0.0 copy-start
  94.2 1.6 %copy-done = bf16[128,64,128]{2,1,0:T(8,128)(2,1)S(1)} copy-done((bf16[128,64,128]{2,1,0:T(8,128)(2,1)S(1)}, bf16[128,64,128]{2,1,0:T(8,128)(2,1)}, u32[]{:S(2)}) %copy-start) | copy-done | bytes 2097176
  95.8 0.6 stage.1.q
  96.5 2.7 %collective-permute-start.15 = (bf16[152,8,128]{2,1,0:T(8,128)(2,1)}, bf16[152,8,128]{2,1,0:T(8,128)(2,1)S(1)}, u32[]{:S(2)}, u32[]{:S(2)}) collective-permute-start(bf16[152,8,128]{2,1,0:T(8,128)(2,1)} %collective-permute-done.14.far_k), channel_id=1, source_target_pairs={{0,7},{1,0},{2,1},{3,2},{4,3},{5,4},{6,5},{7,6},{8,15},{9,8},{10,9... | collective-permute-start | bytes 933896 | tf_op jit(solution)/shard_map/ppermute | solution.py:289
  99.2 1.0 copy-done.2
  100.2 3.6 %attend.8._ = bf16[128,64,128]{2,1,0:T(8,128)(2,1)} custom-call(s32[8,19]{1,0:T(8,128)S(1)} %pad_add_fusion.meta, bf16[8,128,8,128]{3,2,1,0:T(8,128)(2,1)S(1)} %stage.1.q, bf16[32,8,8,128]{3,2,1,0:T(8,128)(2,1)} %bitcast.20.clone.2.own, bf16[152,8,128]{2,1,0:T(8,128)(2,1)S(1)} %get-tuple-element.12.far_k, ...), custom_call_target="tpu_custom_call", output_to_operand_aliasing={{}: (6, {})} | custom-call | flops 603979776 | bytes 2097152 | tf_op jit(solution)/shard_map/attend/pallas_call | solution.py:177
  103.9 0.1 collective-permute-start.12
  104.0 1.4 %collective-permute-start.8 = (bf16[152,8,128]{2,1,0:T(8,128)(2,1)}, bf16[152,8,128]{2,1,0:T(8,128)(2,1)S(1)}, u32[]{:S(2)}, u32[]{:S(2)}) collective-permute-start(bf16[152,8,128]{2,1,0:T(8,128)(2,1)} %collective-permute-done.7.far_k), channel_id=1, source_target_pairs={{0,1},{1,2},{2,3},{3,4},{4,5},{5,6},{6,7},{7,0},{8,9},{9,10},{10,1... | collective-permute-start | bytes 933896 | tf_op jit(solution)/shard_map/ppermute | solution.py:283
  105.4 3.5 %attend.9._ = bf16[128,64,128]{2,1,0:T(8,128)(2,1)} custom-call(s32[8,19]{1,0:T(8,128)S(1)} %pad_add_fusion.meta, bf16[8,128,8,128]{3,2,1,0:T(8,128)(2,1)S(1)} %stage.1.q, bf16[32,8,8,128]{3,2,1,0:T(8,128)(2,1)} %bitcast.20.clone.2.own, bf16[152,8,128]{2,1,0:T(8,128)(2,1)S(1)} %collective-permute-done.5.far_k, ...), custom_call_target="tpu_custom_call", output_to_operand_aliasing={{}: (6, {})} | custom-call | flops 603979776 | bytes 2097152 | tf_op jit(solution)/shard_map/attend/pallas_call | solution.py:177
  108.9 3.6 %attend.10._ = bf16[128,64,128]{2,1,0:T(8,128)(2,1)} custom-call(s32[8,19]{1,0:T(8,128)S(1)} %pad_add_fusion.meta, bf16[8,128,8,128]{3,2,1,0:T(8,128)(2,1)S(1)} %stage.1.q, bf16[32,8,8,128]{3,2,1,0:T(8,128)(2,1)} %bitcast.20.clone.2.own, bf16[152,8,128]{2,1,0:T(8,128)(2,1)} %collective-permute-done.13.far_k, ...), custom_call_target="tpu_custom_call", output_to_operand_aliasing={{}: (6, {})} | custom-call | flops 603979776 | bytes 2097152 | tf_op jit(solution)/shard_map/attend/pallas_call | solution.py:177
  112.5 3.7 %attend.11._ = bf16[128,64,128]{2,1,0:T(8,128)(2,1)} custom-call(s32[8,19]{1,0:T(8,128)S(1)} %pad_add_fusion.meta, bf16[8,128,8,128]{3,2,1,0:T(8,128)(2,1)S(1)} %stage.1.q, bf16[32,8,8,128]{3,2,1,0:T(8,128)(2,1)} %bitcast.20.clone.2.own, bf16[152,8,128]{2,1,0:T(8,128)(2,1)} %collective-permute-done.6.far_k, ...), custom_call_target="tpu_custom_call", output_to_operand_aliasing={{}: (6, {})} | custom-call | flops 603979776 | bytes 2097152 | tf_op jit(solution)/shard_map/attend/pallas_call | solution.py:177
  116.2 3.9 %attend.12._ = bf16[128,64,128]{2,1,0:T(8,128)(2,1)} custom-call(s32[8,19]{1,0:T(8,128)S(1)} %pad_add_fusion.meta, bf16[8,128,8,128]{3,2,1,0:T(8,128)(2,1)S(1)} %stage.1.q, bf16[32,8,8,128]{3,2,1,0:T(8,128)(2,1)} %bitcast.20.clone.2.own, bf16[152,8,128]{2,1,0:T(8,128)(2,1)} %collective-permute-done.14.far_k, ...), custom_call_target="tpu_custom_call", output_to_operand_aliasing={{}: (6, {})} | custom-call | flops 603979776 | bytes 2097152 | tf_op jit(solution)/shard_map/attend/pallas_call | solution.py:177
  120.2 3.7 %attend.13._ = bf16[128,64,128]{2,1,0:T(8,128)(2,1)} custom-call(s32[8,19]{1,0:T(8,128)S(1)} %pad_add_fusion.meta, bf16[8,128,8,128]{3,2,1,0:T(8,128)(2,1)S(1)} %stage.1.q, bf16[32,8,8,128]{3,2,1,0:T(8,128)(2,1)} %bitcast.20.clone.2.own, bf16[152,8,128]{2,1,0:T(8,128)(2,1)} %collective-permute-done.7.far_k, ...), custom_call_target="tpu_custom_call", output_to_operand_aliasing={{}: (6, {})} | custom-call | flops 603979776 | bytes 2097152 | tf_op jit(solution)/shard_map/attend/pallas_call | solution.py:177
  123.9 3.6 %attend.14._ = bf16[128,64,128]{2,1,0:T(8,128)(2,1)} custom-call(s32[8,19]{1,0:T(8,128)S(1)} %pad_add_fusion.meta, bf16[8,128,8,128]{3,2,1,0:T(8,128)(2,1)S(1)} %stage.1.q, bf16[32,8,8,128]{3,2,1,0:T(8,128)(2,1)} %bitcast.20.clone.2.own, bf16[152,8,128]{2,1,0:T(8,128)(2,1)S(1)} %collective-permute-done.15.far_k, ...), custom_call_target="tpu_custom_call", output_to_operand_aliasing={{}: (6, {})} | custom-call | flops 603979776 | bytes 2097152 | tf_op jit(solution)/shard_map/attend/pallas_call | solution.py:177
  127.6 3.5 %attend.15 = bf16[128,64,128]{2,1,0:T(8,128)(2,1)} custom-call(s32[8,19]{1,0:T(8,128)S(1)} %pad_add_fusion.meta, bf16[8,128,8,128]{3,2,1,0:T(8,128)(2,1)S(1)} %stage.1.q, bf16[32,8,8,128]{3,2,1,0:T(8,128)(2,1)} %bitcast.20.clone.2.own, bf16[152,8,128]{2,1,0:T(8,128)(2,1)S(1)} %collective-permute-done.8.far_k, ...), custom_call_target="tpu_custom_call", output_to_operand_aliasing={{}: (6, {})} | custom-call | flops 603979776 | bytes 2097152 | tf_op jit(solution)/shard_map/attend/pallas_call | solution.py:177
  (38 shorter events, 0.2 us)
Async XLA Ops:
  0.0 17.7 %copy-start.5 = (s32[8,8]{1,0:T(8,128)S(1)}, s32[8,8]{1,0:T(8,128)}, u32[]{:S(2)}) copy-start(s32[8,8]{1,0:T(8,128)} %param.11) | copy-start | bytes 772
  2.0 44.9 %copy-start.3 = (s32[256]{0:T(256)S(1)}, s32[256]{0:T(256)}, u32[]{:S(2)}) copy-start(s32[256]{0:T(256)} %param.12) | copy-start | bytes 3076
  2.0 36.8 %all-to-all-start.1 = ((bf16[256,8,128]{2,1,0:T(8,128)(2,1)}), bf16[256,8,128]{2,1,0:T(8,128)(2,1)S(1)}, u32[]{:S(2)}, u32[]{:S(2)}) async-start(bf16[256,8,128]{2,1,0:T(8,128)(2,1)} %bitcast.12), calls=%async_computation.1 | async-start | bytes 1048576 | tf_op jit(solution)/shard_map/all_to_all | solution.py:263
  18.2 3.0 %collective-permute-start = (s32[1,128]{1,0:T(1,128)S(1)}, s32[1,128]{1,0:T(1,128)S(1)}, u32[]{:S(2)}, u32[]{:S(2)}) collective-permute-start(s32[1,128]{1,0:T(1,128)S(1)} %bitcast.25), channel_id=1, source_target_pairs={{0,8},{8,0},{16,24},{24,16},{32,40},{40,32},{48,56},{56,48},{64,72... | collective-permute-start | bytes 1544 | tf_op jit(solution)/shard_map/ppermute | solution.py:241
  21.3 2.7 %collective-permute-start.1 = (s32[2,128]{1,0:T(2,128)S(1)}, s32[2,128]{1,0:T(2,128)S(1)}, u32[]{:S(2)}, u32[]{:S(2)}) collective-permute-start(s32[2,128]{1,0:T(2,128)S(1)} %pad_add_fusion.3), channel_id=1, source_target_pairs={{0,16},{8,24},{16,0},{24,8},{32,48},{40,56},{48,32},{56,40},{64,80... | collective-permute-start | bytes 3080 | tf_op jit(solution)/shard_map/ppermute | solution.py:241
  24.0 4.3 %collective-permute-start.2 = (s32[4,128]{1,0:T(4,128)S(1)}, s32[4,128]{1,0:T(4,128)S(1)}, u32[]{:S(2)}, u32[]{:S(2)}) collective-permute-start(s32[4,128]{1,0:T(4,128)S(1)} %pad_add_fusion.2), channel_id=1, source_target_pairs={{0,32},{8,40},{16,48},{24,56},{32,0},{40,8},{48,16},{56,24},{64,96... | collective-permute-start | bytes 6152 | tf_op jit(solution)/shard_map/ppermute | solution.py:241
  28.4 2.8 %collective-permute-start.3 = (s32[8,128]{1,0:T(8,128)S(1)}, s32[8,128]{1,0:T(8,128)S(1)}, u32[]{:S(2)}, u32[]{:S(2)}) collective-permute-start(s32[8,128]{1,0:T(8,128)S(1)} %pad_add_fusion.1), channel_id=1, source_target_pairs={{0,64},{8,72},{16,80},{24,88},{32,96},{40,104},{48,112},{56,120},{... | collective-permute-start | bytes 12296 | tf_op jit(solution)/shard_map/ppermute | solution.py:241
  31.2 4.4 %collective-permute-start.4 = (s32[16,128]{1,0:T(8,128)S(1)}, s32[16,128]{1,0:T(8,128)S(1)}, u32[]{:S(2)}, u32[]{:S(2)}) collective-permute-start(s32[16,128]{1,0:T(8,128)S(1)} %concatenate.34), channel_id=1, source_target_pairs={{0,128},{8,136},{16,144},{24,152},{32,160},{40,168},{48,176},{56,1... | collective-permute-start | bytes 24584 | tf_op jit(solution)/shard_map/ppermute | solution.py:241
  38.8 42.0 %copy-start.6 = (s32[8]{0:T(128)S(1)}, s32[8]{0:T(128)}, u32[]{:S(2)}) copy-start(s32[8]{0:T(128)} %constant.77.clone) | copy-start | bytes 100
  40.9 20.1 %all-to-all-start.2 = ((bf16[32,12,8,128]{3,2,1,0:T(8,128)(2,1)}), bf16[32,12,8,128]{3,2,1,0:T(8,128)(2,1)S(1)}, u32[]{:S(2)}, u32[]{:S(2)}) async-start(bf16[32,12,8,128]{3,2,1,0:T(8,128)(2,1)} %pick.1), calls=%async_computation.2 | async-start | bytes 1572864 | tf_op jit(solution)/shard_map/all_to_all | solution.py:265
  61.9 12.2 %collective-permute-start.5 = (bf16[152,8,128]{2,1,0:T(8,128)(2,1)S(1)}, bf16[152,8,128]{2,1,0:T(8,128)(2,1)S(1)}, u32[]{:S(2)}, u32[]{:S(2)}) collective-permute-start(bf16[152,8,128]{2,1,0:T(8,128)(2,1)S(1)} %get-tuple-element.12.far_k), channel_id=1, source_target_pairs={{0,1},{1,2},{2,3},{3,4},{4,5},{5,6},{6,7},{7,0},{8,9},{9,10},{10,1... | collective-permute-start | bytes 933896 | tf_op jit(solution)/shard_map/ppermute | solution.py:283
  63.4 10.7 %collective-permute-start.9 = (bf16[152,8,128]{2,1,0:T(8,128)(2,1)S(1)}, bf16[152,8,128]{2,1,0:T(8,128)(2,1)S(1)}, u32[]{:S(2)}, u32[]{:S(2)}) collective-permute-start(bf16[152,8,128]{2,1,0:T(8,128)(2,1)S(1)} %get-tuple-element.13.far_v), channel_id=1, source_target_pairs={{0,7},{1,0},{2,1},{3,2},{4,3},{5,4},{6,5},{7,6},{8,15},{9,8},{10,9... | collective-permute-start | bytes 933896 | tf_op jit(solution)/shard_map/ppermute | solution.py:284
  66.4 14.4 %collective-permute-start.16 = (bf16[152,8,128]{2,1,0:T(8,128)(2,1)S(1)}, bf16[152,8,128]{2,1,0:T(8,128)(2,1)S(1)}, u32[]{:S(2)}, u32[]{:S(2)}) collective-permute-start(bf16[152,8,128]{2,1,0:T(8,128)(2,1)S(1)} %get-tuple-element.13.far_v), channel_id=1, source_target_pairs={{0,1},{1,2},{2,3},{3,4},{4,5},{5,6},{6,7},{7,0},{8,9},{9,10},{10,1... | collective-permute-start | bytes 933896 | tf_op jit(solution)/shard_map/ppermute | solution.py:288
  66.4 0.7 copy-start.1
  67.1 13.7 %collective-permute-start.13 = (bf16[152,8,128]{2,1,0:T(8,128)(2,1)S(1)}, bf16[152,8,128]{2,1,0:T(8,128)(2,1)}, u32[]{:S(2)}, u32[]{:S(2)}) collective-permute-start(bf16[152,8,128]{2,1,0:T(8,128)(2,1)S(1)} %get-tuple-element.12.far_k), channel_id=1, source_target_pairs={{0,7},{1,0},{2,1},{3,2},{4,3},{5,4},{6,5},{7,6},{8,15},{9,8},{10,9... | collective-permute-start | bytes 933896 | tf_op jit(solution)/shard_map/ppermute | solution.py:289
  74.1 13.4 %collective-permute-start.6 = (bf16[152,8,128]{2,1,0:T(8,128)(2,1)S(1)}, bf16[152,8,128]{2,1,0:T(8,128)(2,1)}, u32[]{:S(2)}, u32[]{:S(2)}) collective-permute-start(bf16[152,8,128]{2,1,0:T(8,128)(2,1)S(1)} %collective-permute-done.5.far_k), channel_id=1, source_target_pairs={{0,1},{1,2},{2,3},{3,4},{4,5},{5,6},{6,7},{7,0},{8,9},{9,10},{10,1... | collective-permute-start | bytes 933896 | tf_op jit(solution)/shard_map/ppermute | solution.py:283
  74.1 13.4 %collective-permute-start.10 = (bf16[152,8,128]{2,1,0:T(8,128)(2,1)S(1)}, bf16[152,8,128]{2,1,0:T(8,128)(2,1)}, u32[]{:S(2)}, u32[]{:S(2)}) collective-permute-start(bf16[152,8,128]{2,1,0:T(8,128)(2,1)S(1)} %collective-permute-done.9.far_v), channel_id=1, source_target_pairs={{0,7},{1,0},{2,1},{3,2},{4,3},{5,4},{6,5},{7,6},{8,15},{9,8},{10,9... | collective-permute-start | bytes 933896 | tf_op jit(solution)/shard_map/ppermute | solution.py:284
  80.8 13.4 %collective-permute-start.17 = (bf16[152,8,128]{2,1,0:T(8,128)(2,1)S(1)}, bf16[152,8,128]{2,1,0:T(8,128)(2,1)}, u32[]{:S(2)}, u32[]{:S(2)}) collective-permute-start(bf16[152,8,128]{2,1,0:T(8,128)(2,1)S(1)} %collective-permute-done.16.far_v), channel_id=1, source_target_pairs={{0,1},{1,2},{2,3},{3,4},{4,5},{5,6},{6,7},{7,0},{8,9},{9,10},{10,1... | collective-permute-start | bytes 933896 | tf_op jit(solution)/shard_map/ppermute | solution.py:288
  80.8 15.7 %collective-permute-start.14 = (bf16[152,8,128]{2,1,0:T(8,128)(2,1)}, bf16[152,8,128]{2,1,0:T(8,128)(2,1)}, u32[]{:S(2)}, u32[]{:S(2)}) collective-permute-start(bf16[152,8,128]{2,1,0:T(8,128)(2,1)} %collective-permute-done.13.far_k), channel_id=1, source_target_pairs={{0,7},{1,0},{2,1},{3,2},{4,3},{5,4},{6,5},{7,6},{8,15},{9,8},{10,9... | collective-permute-start | bytes 933896 | tf_op jit(solution)/shard_map/ppermute | solution.py:289
  87.5 16.4 %collective-permute-start.7 = (bf16[152,8,128]{2,1,0:T(8,128)(2,1)}, bf16[152,8,128]{2,1,0:T(8,128)(2,1)}, u32[]{:S(2)}, u32[]{:S(2)}) collective-permute-start(bf16[152,8,128]{2,1,0:T(8,128)(2,1)} %collective-permute-done.6.far_k), channel_id=1, source_target_pairs={{0,1},{1,2},{2,3},{3,4},{4,5},{5,6},{6,7},{7,0},{8,9},{9,10},{10,1... | collective-permute-start | bytes 933896 | tf_op jit(solution)/shard_map/ppermute | solution.py:283
  87.6 16.3 %collective-permute-start.11 = (bf16[152,8,128]{2,1,0:T(8,128)(2,1)}, bf16[152,8,128]{2,1,0:T(8,128)(2,1)}, u32[]{:S(2)}, u32[]{:S(2)}) collective-permute-start(bf16[152,8,128]{2,1,0:T(8,128)(2,1)} %collective-permute-done.10.far_v), channel_id=1, source_target_pairs={{0,7},{1,0},{2,1},{3,2},{4,3},{5,4},{6,5},{7,6},{8,15},{9,8},{10,9... | collective-permute-start | bytes 933896 | tf_op jit(solution)/shard_map/ppermute | solution.py:284
  94.2 26.0 %collective-permute-start.18 = (bf16[152,8,128]{2,1,0:T(8,128)(2,1)}, bf16[152,8,128]{2,1,0:T(8,128)(2,1)}, u32[]{:S(2)}, u32[]{:S(2)}) collective-permute-start(bf16[152,8,128]{2,1,0:T(8,128)(2,1)} %collective-permute-done.17.far_v), channel_id=1, source_target_pairs={{0,1},{1,2},{2,3},{3,4},{4,5},{5,6},{6,7},{7,0},{8,9},{9,10},{10,1... | collective-permute-start | bytes 933896 | tf_op jit(solution)/shard_map/ppermute | solution.py:288
  94.2 1.6 %copy-start = (bf16[128,64,128]{2,1,0:T(8,128)(2,1)S(1)}, bf16[128,64,128]{2,1,0:T(8,128)(2,1)}, u32[]{:S(2)}) copy-start(bf16[128,64,128]{2,1,0:T(8,128)(2,1)} %q.1) | copy-start | bytes 6291460
  96.5 27.4 %collective-permute-start.15 = (bf16[152,8,128]{2,1,0:T(8,128)(2,1)}, bf16[152,8,128]{2,1,0:T(8,128)(2,1)S(1)}, u32[]{:S(2)}, u32[]{:S(2)}) collective-permute-start(bf16[152,8,128]{2,1,0:T(8,128)(2,1)} %collective-permute-done.14.far_k), channel_id=1, source_target_pairs={{0,7},{1,0},{2,1},{3,2},{4,3},{5,4},{6,5},{7,6},{8,15},{9,8},{10,9... | collective-permute-start | bytes 933896 | tf_op jit(solution)/shard_map/ppermute | solution.py:289
  99.2 1.0 copy-start.2
  100.2 5.2 %copy-start.4 = (bf16[8,2,40,8,128]{4,3,2,1,0:T(8,128)(2,1)S(1)}, bf16[8,2,40,8,128]{4,3,2,1,0:T(8,128)(2,1)}, u32[]{:S(2)}) copy-start(bf16[8,2,40,8,128]{4,3,2,1,0:T(8,128)(2,1)} %get-tuple-element.17.rest) | copy-start | bytes 3932164
  103.9 23.7 %collective-permute-start.12 = (bf16[152,8,128]{2,1,0:T(8,128)(2,1)}, bf16[152,8,128]{2,1,0:T(8,128)(2,1)S(1)}, u32[]{:S(2)}, u32[]{:S(2)}) collective-permute-start(bf16[152,8,128]{2,1,0:T(8,128)(2,1)} %collective-permute-done.11.far_v), channel_id=1, source_target_pairs={{0,7},{1,0},{2,1},{3,2},{4,3},{5,4},{6,5},{7,6},{8,15},{9,8},{10,9... | collective-permute-start | bytes 933896 | tf_op jit(solution)/shard_map/ppermute | solution.py:284
  104.0 23.6 %collective-permute-start.8 = (bf16[152,8,128]{2,1,0:T(8,128)(2,1)}, bf16[152,8,128]{2,1,0:T(8,128)(2,1)S(1)}, u32[]{:S(2)}, u32[]{:S(2)}) collective-permute-start(bf16[152,8,128]{2,1,0:T(8,128)(2,1)} %collective-permute-done.7.far_k), channel_id=1, source_target_pairs={{0,1},{1,2},{2,3},{3,4},{4,5},{5,6},{6,7},{7,0},{8,9},{9,10},{10,1... | collective-permute-start | bytes 933896 | tf_op jit(solution)/shard_map/ppermute | solution.py:283

commit v6 on v5

--- a/solution.py
+++ b/solution.py
@@ -192,6 +192,31 @@
         cost_estimate=pl.CostEstimate(flops=flops, bytes_accessed=2 << 20, transcendentals=1024 * 1152),
         name="attend",
     )(meta, q, own, far_k, far_v, rest, prev)
+
+
+def cut_kernel(k_hbm, v_hbm, out, k, v, sems):
+    pairs = ((k_hbm, k), (v_hbm, v))
+    copies = [pltpu.make_async_copy(a, b, sems.at[i]) for i, (a, b) in enumerate(pairs)]
+    for copy in copies:
+        copy.start()
+    for i, (_, x) in enumerate(pairs):
+        copies[i].wait()
+        for p in range(PIECES):
+            rows = x[p * TILE : (p + 1) * TILE].astype(jnp.float32)
+            out[i * PIECES + p] = jnp.swapaxes(rows, 0, 1).astype(out.dtype)
+
+
+def cut(k, v):
+    hbm = pl.BlockSpec(memory_space=pl.ANY)
+    return pl.pallas_call(
+        cut_kernel,
+        out_shape=jax.ShapeDtypeStruct((2 * PIECES, 8, TILE, BS), k.dtype),
+        in_specs=[hbm, hbm],
+        out_specs=vmem(),
+        scratch_shapes=[pltpu.VMEM(k.shape, k.dtype), pltpu.VMEM(v.shape, v.dtype), pltpu.SemaphoreType.DMA((2,))],
+        compiler_params=pltpu.CompilerParams(vmem_limit_bytes=GRANT),
+        name="cut",
+    )(k, v)
 
 
 def stage_kernel(q, out, sems):
@@ -259,7 +284,7 @@
     heads = (level + jnp.array(shifts, jnp.int32)) % n_head
     meta = jnp.concatenate([heads[:, None], jnp.broadcast_to(row, (n_head, row.shape[1]))], axis=1)
 
-    own = jnp.concatenate([keys, values], axis=0).reshape(32, TILE, n_head, BS).transpose(0, 2, 1, 3)
+    own = cut(keys, values)
     held = lax.all_to_all(own.reshape(n_seq * n_head, TILE, BS), ("seq", "head"), 0, 0, tiled=True)
     picked = pick(pools, place.astype(jnp.int32)[None], held)
     far = lax.all_to_all(picked, "seq", 0, 0, tiled=True)

time: 132 us -> 133 us (level)
    unnamed x14 -> x18, local copies, waits for them, and re-layouts: 3.27 us -> 5.18 us
where the time goes in v6:
time: 133 us; the launch traced here: 132 us
  starting transfers between devices  46 us (35%)
  waiting for transfers between devices  41.6 us (31%)
  Pallas kernels  33.9 us (25%)
  local copies, waits for them, and re-layouts  8.1 us (6%)
  other arithmetic  1.58 us (1%)
    pallas_call x8, Pallas kernels, attend(): pl.pallas_call(functools.partial(attend_kernel, scale, call), out_shape=j...  29.2 us
    all_to_all x1, starting transfers between devices, attention(): lax.all_to_all(own.reshape(n_seq * n_head, TILE, BS), ('seq', 'head'), 0,...  15.7 us
    ppermute x5, waiting for transfers between devices, attention(): other = lax.ppermute(pools, 'seq', [(i, i ^ bit) for i in range(n_seq)])  12.5 us
    all_to_all x1, waiting for transfers between devices, attention(): far = lax.all_to_all(picked, 'seq', 0, 0, tiled=True)  10.8 us
    ppermute x4, starting transfers between devices, attention(): v_down = lax.ppermute(v_down, 'head', down)  8.37 us
    ppermute x4, waiting for transfers between devices, attention(): k_up = lax.ppermute(k_up, 'head', up)  8.25 us
    ppermute x3, starting transfers between devices, attention(): k_down = lax.ppermute(k_down, 'head', down)  8.23 us
    ppermute x3, waiting for transfers between devices, attention(): v_up = lax.ppermute(v_up, 'head', up)  6.93 us
  transfers between devices with their start and end apart: 21, of which 11 were waited for; matrix products, arithmetic and copies ran while one was open for 3% of the time, Pallas kernels for 20%

profile of v6, /device:TPU:1, one launch (start us, length us, event | category | flops | bytes accessed | tf_op | source)
XLA Modules:
  0.0 132.3 jit_solution(8836126410690193618)
XLA Ops:
  0.0 0.9 copy-done.3
  1.0 0.9 copy-done.4
  1.9 1.1 cut.1.own
  3.0 0.0 copy-start.5
  3.0 15.7 %all-to-all-start.1 = ((bf16[256,8,128]{2,1,0:T(8,128)(2,1)}), bf16[256,8,128]{2,1,0:T(8,128)(2,1)S(1)}, u32[]{:S(2)}, u32[]{:S(2)}) async-start(bf16[256,8,128]{2,1,0:T(8,128)(2,1)} %bitcast.10), calls=%async_computation.1 | async-start | bytes 1048576 | tf_op jit(solution)/shard_map/all_to_all | solution.py:288
  18.7 0.1 eq.45
  18.7 0.2 fusion.1
  18.9 0.2 convert_reduce_fusion
  19.1 0.1 select_reduce_fusion
  19.2 2.2 %collective-permute-start = (s32[1,128]{1,0:T(1,128)S(1)}, s32[1,128]{1,0:T(1,128)S(1)}, u32[]{:S(2)}, u32[]{:S(2)}) collective-permute-start(s32[1,128]{1,0:T(1,128)S(1)} %bitcast.20), channel_id=1, source_target_pairs={{0,8},{8,0},{16,24},{24,16},{32,40},{40,32},{48,56},{56,48},{64,72... | collective-permute-start | bytes 1544 | tf_op jit(solution)/shard_map/ppermute | solution.py:266
  21.5 0.8 collective-permute-done
  22.3 0.0 collective-permute-start.1
  22.3 2.7 %collective-permute-done.1 = s32[2,128]{1,0:T(2,128)S(1)} collective-permute-done((s32[2,128]{1,0:T(2,128)S(1)}, s32[2,128]{1,0:T(2,128)S(1)}, u32[]{:S(2)}, u32[]{:S(2)}) %collective-permute-start.1) | collective-permute-done | bytes 1056 | tf_op jit(solution)/shard_map/ppermute | solution.py:266
  25.0 1.2 collective-permute-start.2
  26.2 3.1 %collective-permute-done.2 = s32[4,128]{1,0:T(4,128)S(1)} collective-permute-done((s32[4,128]{1,0:T(4,128)S(1)}, s32[4,128]{1,0:T(4,128)S(1)}, u32[]{:S(2)}, u32[]{:S(2)}) %collective-permute-start.2) | collective-permute-done | bytes 2080 | tf_op jit(solution)/shard_map/ppermute | solution.py:266
  29.4 0.1 collective-permute-start.3
  29.5 2.7 %collective-permute-done.3 = s32[8,128]{1,0:T(8,128)S(1)} collective-permute-done((s32[8,128]{1,0:T(8,128)S(1)}, s32[8,128]{1,0:T(8,128)S(1)}, u32[]{:S(2)}, u32[]{:S(2)}) %collective-permute-start.3) | collective-permute-done | bytes 4128 | tf_op jit(solution)/shard_map/ppermute | solution.py:266
  32.2 1.3 %collective-permute-start.4 = (s32[16,128]{1,0:T(8,128)S(1)}, s32[16,128]{1,0:T(8,128)S(1)}, u32[]{:S(2)}, u32[]{:S(2)}) collective-permute-start(s32[16,128]{1,0:T(8,128)S(1)} %concatenate.30), channel_id=1, source_target_pairs={{0,128},{8,136},{16,144},{24,152},{32,160},{40,168},{48,176},{56,1... | collective-permute-start | bytes 24584 | tf_op jit(solution)/shard_map/ppermute | solution.py:266
  33.6 3.0 %collective-permute-done.4 = s32[16,128]{1,0:T(8,128)S(1)} collective-permute-done((s32[16,128]{1,0:T(8,128)S(1)}, s32[16,128]{1,0:T(8,128)S(1)}, u32[]{:S(2)}, u32[]{:S(2)}) %collective-permute-start.4) | collective-permute-done | bytes 8224 | tf_op jit(solution)/shard_map/ppermute | solution.py:266
  36.6 3.1 %all-to-all-done.1.held = bf16[256,8,128]{2,1,0:T(8,128)(2,1)S(1)} async-done(((bf16[256,8,128]{2,1,0:T(8,128)(2,1)}), bf16[256,8,128]{2,1,0:T(8,128)(2,1)S(1)}, u32[]{:S(2)}, u32[]{:S(2)}) %all-to-all-start.1) | async-done | bytes 524320 | tf_op jit(solution)/shard_map/all_to_all | solution.py:288
  39.8 2.2 %pick.1 = bf16[32,12,8,128]{3,2,1,0:T(8,128)(2,1)} custom-call(s32[32,128]{1,0:T(8,128)S(1)} %concatenate.31.pools, s32[1]{0:T(128)} %bitcast.9.me, bf16[256,8,128]{2,1,0:T(8,128)(2,1)S(1)} %all-to-all-done.1.held), custom_call_target="tpu_custom_call" | custom-call | tf_op jit(solution)/shard_map/pick/pallas_call | solution.py:57
  41.9 5.9 %all-to-all-start.2 = ((bf16[32,12,8,128]{3,2,1,0:T(8,128)(2,1)}), bf16[32,12,8,128]{3,2,1,0:T(8,128)(2,1)S(1)}, u32[]{:S(2)}, u32[]{:S(2)}) async-start(bf16[32,12,8,128]{3,2,1,0:T(8,128)(2,1)} %pick.1), calls=%async_computation.2 | async-start | bytes 1572864 | tf_op jit(solution)/shard_map/all_to_all | solution.py:290
  47.8 0.1 reshape.65
  47.9 0.7 gather_fusion
  48.6 0.1 select_reduce_fusion.1.offs
  48.7 0.6 slice.18
  49.9 0.6 gather_fusion.1
  50.6 0.7 dynamic_slice.11
  51.2 10.8 %all-to-all-done.2.far = bf16[32,12,8,128]{3,2,1,0:T(8,128)(2,1)S(1)} async-done(((bf16[32,12,8,128]{3,2,1,0:T(8,128)(2,1)}), bf16[32,12,8,128]{3,2,1,0:T(8,128)(2,1)S(1)}, u32[]{:S(2)}, u32[]{:S(2)}) %all-to-all-start.2) | async-done | bytes 786464 | tf_op jit(solution)/shard_map/all_to_all | solution.py:290
  62.1 0.8 pack.1
  62.9 1.5 %collective-permute-start.5 = (bf16[152,8,128]{2,1,0:T(8,128)(2,1)S(1)}, bf16[152,8,128]{2,1,0:T(8,128)(2,1)S(1)}, u32[]{:S(2)}, u32[]{:S(2)}) collective-permute-start(bf16[152,8,128]{2,1,0:T(8,128)(2,1)S(1)} %get-tuple-element.12.far_k), channel_id=1, source_target_pairs={{0,1},{1,2},{2,3},{3,4},{4,5},{5,6},{6,7},{7,0},{8,9},{9,10},{10,1... | collective-permute-start | bytes 933896 | tf_op jit(solution)/shard_map/ppermute | solution.py:308
  64.4 2.9 %collective-permute-start.9 = (bf16[152,8,128]{2,1,0:T(8,128)(2,1)S(1)}, bf16[152,8,128]{2,1,0:T(8,128)(2,1)S(1)}, u32[]{:S(2)}, u32[]{:S(2)}) collective-permute-start(bf16[152,8,128]{2,1,0:T(8,128)(2,1)S(1)} %get-tuple-element.13.far_v), channel_id=1, source_target_pairs={{0,7},{1,0},{2,1},{3,2},{4,3},{5,4},{6,5},{7,6},{8,15},{9,8},{10,9... | collective-permute-start | bytes 933896 | tf_op jit(solution)/shard_map/ppermute | solution.py:309
  67.4 0.7 copy-done.1
  68.1 2.7 %collective-permute-start.13 = (bf16[152,8,128]{2,1,0:T(8,128)(2,1)S(1)}, bf16[152,8,128]{2,1,0:T(8,128)(2,1)}, u32[]{:S(2)}, u32[]{:S(2)}) collective-permute-start(bf16[152,8,128]{2,1,0:T(8,128)(2,1)S(1)} %get-tuple-element.12.far_k), channel_id=1, source_target_pairs={{0,7},{1,0},{2,1},{3,2},{4,3},{5,4},{6,5},{7,6},{8,15},{9,8},{10,9... | collective-permute-start | bytes 933896 | tf_op jit(solution)/shard_map/ppermute | solution.py:314
  70.8 4.2 %collective-permute-done.5.far_k = bf16[152,8,128]{2,1,0:T(8,128)(2,1)S(1)} collective-permute-done((bf16[152,8,128]{2,1,0:T(8,128)(2,1)S(1)}, bf16[152,8,128]{2,1,0:T(8,128)(2,1)S(1)}, u32[]{:S(2)}, u32[]{:S(2)}) %collective-permute-start.5) | collective-permute-done | bytes 311328 | tf_op jit(solution)/shard_map/ppermute | solution.py:308
  75.1 2.7 %collective-permute-start.10 = (bf16[152,8,128]{2,1,0:T(8,128)(2,1)S(1)}, bf16[152,8,128]{2,1,0:T(8,128)(2,1)}, u32[]{:S(2)}, u32[]{:S(2)}) collective-permute-start(bf16[152,8,128]{2,1,0:T(8,128)(2,1)S(1)} %collective-permute-done.9.far_v), channel_id=1, source_target_pairs={{0,7},{1,0},{2,1},{3,2},{4,3},{5,4},{6,5},{7,6},{8,15},{9,8},{10,9... | collective-permute-start | bytes 933896 | tf_op jit(solution)/shard_map/ppermute | solution.py:309
  77.8 0.2 select_reduce_fusion.2
  78.0 3.8 %collective-permute-done.16.far_v = bf16[152,8,128]{2,1,0:T(8,128)(2,1)S(1)} collective-permute-done((bf16[152,8,128]{2,1,0:T(8,128)(2,1)S(1)}, bf16[152,8,128]{2,1,0:T(8,128)(2,1)S(1)}, u32[]{:S(2)}, u32[]{:S(2)}) %collective-permute-start.16) | collective-permute-done | bytes 311328 | tf_op jit(solution)/shard_map/ppermute | solution.py:313
  81.8 0.0 collective-permute-done.13.far_k
  81.8 2.7 %collective-permute-start.14 = (bf16[152,8,128]{2,1,0:T(8,128)(2,1)}, bf16[152,8,128]{2,1,0:T(8,128)(2,1)}, u32[]{:S(2)}, u32[]{:S(2)}) collective-permute-start(bf16[152,8,128]{2,1,0:T(8,128)(2,1)} %collective-permute-done.13.far_k), channel_id=1, source_target_pairs={{0,7},{1,0},{2,1},{3,2},{4,3},{5,4},{6,5},{7,6},{8,15},{9,8},{10,9... | collective-permute-start | bytes 933896 | tf_op jit(solution)/shard_map/ppermute | solution.py:314
  84.5 4.0 %collective-permute-done.6.far_k = bf16[152,8,128]{2,1,0:T(8,128)(2,1)} collective-permute-done((bf16[152,8,128]{2,1,0:T(8,128)(2,1)S(1)}, bf16[152,8,128]{2,1,0:T(8,128)(2,1)}, u32[]{:S(2)}, u32[]{:S(2)}) %collective-permute-start.6) | collective-permute-done | bytes 311328 | tf_op jit(solution)/shard_map/ppermute | solution.py:308
  88.5 0.0 collective-permute-start.7
  88.5 2.7 %collective-permute-start.11 = (bf16[152,8,128]{2,1,0:T(8,128)(2,1)}, bf16[152,8,128]{2,1,0:T(8,128)(2,1)}, u32[]{:S(2)}, u32[]{:S(2)}) collective-permute-start(bf16[152,8,128]{2,1,0:T(8,128)(2,1)} %collective-permute-done.10.far_v), channel_id=1, source_target_pairs={{0,7},{1,0},{2,1},{3,2},{4,3},{5,4},{6,5},{7,6},{8,15},{9,8},{10,9... | collective-permute-start | bytes 933896 | tf_op jit(solution)/shard_map/ppermute | solution.py:309
  91.2 0.7 add_bitcast_fusion
  91.9 0.1 pad.10.clone
  92.0 0.1 copy.17
  92.1 3.1 %collective-permute-done.17.far_v = bf16[152,8,128]{2,1,0:T(8,128)(2,1)} collective-permute-done((bf16[152,8,128]{2,1,0:T(8,128)(2,1)S(1)}, bf16[152,8,128]{2,1,0:T(8,128)(2,1)}, u32[]{:S(2)}, u32[]{:S(2)}) %collective-permute-start.17) | collective-permute-done | bytes 311328 | tf_op jit(solution)/shard_map/ppermute | solution.py:313
  95.2 0.0 collective-permute-start.18
  95.2 0.0 copy-start
  95.2 1.6 %copy-done = bf16[128,64,128]{2,1,0:T(8,128)(2,1)S(1)} copy-done((bf16[128,64,128]{2,1,0:T(8,128)(2,1)S(1)}, bf16[128,64,128]{2,1,0:T(8,128)(2,1)}, u32[]{:S(2)}) %copy-start) | copy-done | bytes 2097176
  96.8 0.6 stage.1.q
  97.5 2.7 %collective-permute-start.15 = (bf16[152,8,128]{2,1,0:T(8,128)(2,1)}, bf16[152,8,128]{2,1,0:T(8,128)(2,1)S(1)}, u32[]{:S(2)}, u32[]{:S(2)}) collective-permute-start(bf16[152,8,128]{2,1,0:T(8,128)(2,1)} %collective-permute-done.14.far_k), channel_id=1, source_target_pairs={{0,7},{1,0},{2,1},{3,2},{4,3},{5,4},{6,5},{7,6},{8,15},{9,8},{10,9... | collective-permute-start | bytes 933896 | tf_op jit(solution)/shard_map/ppermute | solution.py:314
  100.2 1.0 copy-done.2
  101.2 3.6 %attend.8._ = bf16[128,64,128]{2,1,0:T(8,128)(2,1)} custom-call(s32[8,19]{1,0:T(8,128)S(1)} %pad_add_fusion.meta, bf16[8,128,8,128]{3,2,1,0:T(8,128)(2,1)S(1)} %stage.1.q, bf16[32,8,8,128]{3,2,1,0:T(8,128)(2,1)} %cut.1.own, bf16[152,8,128]{2,1,0:T(8,128)(2,1)S(1)} %get-tuple-element.12.far_k, ...), custom_call_target="tpu_custom_call", output_to_operand_aliasing={{}: (6, {})} | custom-call | flops 603979776 | bytes 2097152 | tf_op jit(solution)/shard_map/attend/pallas_call | solution.py:177
  104.8 0.0 collective-permute-done.11.far_v
  104.8 0.1 collective-permute-start.12
  104.9 1.4 %collective-permute-start.8 = (bf16[152,8,128]{2,1,0:T(8,128)(2,1)}, bf16[152,8,128]{2,1,0:T(8,128)(2,1)S(1)}, u32[]{:S(2)}, u32[]{:S(2)}) collective-permute-start(bf16[152,8,128]{2,1,0:T(8,128)(2,1)} %collective-permute-done.7.far_k), channel_id=1, source_target_pairs={{0,1},{1,2},{2,3},{3,4},{4,5},{5,6},{6,7},{7,0},{8,9},{9,10},{10,1... | collective-permute-start | bytes 933896 | tf_op jit(solution)/shard_map/ppermute | solution.py:308
  106.4 3.5 %attend.9._ = bf16[128,64,128]{2,1,0:T(8,128)(2,1)} custom-call(s32[8,19]{1,0:T(8,128)S(1)} %pad_add_fusion.meta, bf16[8,128,8,128]{3,2,1,0:T(8,128)(2,1)S(1)} %stage.1.q, bf16[32,8,8,128]{3,2,1,0:T(8,128)(2,1)} %cut.1.own, bf16[152,8,128]{2,1,0:T(8,128)(2,1)S(1)} %collective-permute-done.5.far_k, ...), custom_call_target="tpu_custom_call", output_to_operand_aliasing={{}: (6, {})} | custom-call | flops 603979776 | bytes 2097152 | tf_op jit(solution)/shard_map/attend/pallas_call | solution.py:177
  109.9 3.6 %attend.10._ = bf16[128,64,128]{2,1,0:T(8,128)(2,1)} custom-call(s32[8,19]{1,0:T(8,128)S(1)} %pad_add_fusion.meta, bf16[8,128,8,128]{3,2,1,0:T(8,128)(2,1)S(1)} %stage.1.q, bf16[32,8,8,128]{3,2,1,0:T(8,128)(2,1)} %cut.1.own, bf16[152,8,128]{2,1,0:T(8,128)(2,1)} %collective-permute-done.13.far_k, ...), custom_call_target="tpu_custom_call", output_to_operand_aliasing={{}: (6, {})} | custom-call | flops 603979776 | bytes 2097152 | tf_op jit(solution)/shard_map/attend/pallas_call | solution.py:177
  113.5 3.9 %attend.11._ = bf16[128,64,128]{2,1,0:T(8,128)(2,1)} custom-call(s32[8,19]{1,0:T(8,128)S(1)} %pad_add_fusion.meta, bf16[8,128,8,128]{3,2,1,0:T(8,128)(2,1)S(1)} %stage.1.q, bf16[32,8,8,128]{3,2,1,0:T(8,128)(2,1)} %cut.1.own, bf16[152,8,128]{2,1,0:T(8,128)(2,1)} %collective-permute-done.6.far_k, ...), custom_call_target="tpu_custom_call", output_to_operand_aliasing={{}: (6, {})} | custom-call | flops 603979776 | bytes 2097152 | tf_op jit(solution)/shard_map/attend/pallas_call | solution.py:177
  117.5 3.7 %attend.12._ = bf16[128,64,128]{2,1,0:T(8,128)(2,1)} custom-call(s32[8,19]{1,0:T(8,128)S(1)} %pad_add_fusion.meta, bf16[8,128,8,128]{3,2,1,0:T(8,128)(2,1)S(1)} %stage.1.q, bf16[32,8,8,128]{3,2,1,0:T(8,128)(2,1)} %cut.1.own, bf16[152,8,128]{2,1,0:T(8,128)(2,1)} %collective-permute-done.14.far_k, ...), custom_call_target="tpu_custom_call", output_to_operand_aliasing={{}: (6, {})} | custom-call | flops 603979776 | bytes 2097152 | tf_op jit(solution)/shard_map/attend/pallas_call | solution.py:177
  121.2 3.7 %attend.13._ = bf16[128,64,128]{2,1,0:T(8,128)(2,1)} custom-call(s32[8,19]{1,0:T(8,128)S(1)} %pad_add_fusion.meta, bf16[8,128,8,128]{3,2,1,0:T(8,128)(2,1)S(1)} %stage.1.q, bf16[32,8,8,128]{3,2,1,0:T(8,128)(2,1)} %cut.1.own, bf16[152,8,128]{2,1,0:T(8,128)(2,1)} %collective-permute-done.7.far_k, ...), custom_call_target="tpu_custom_call", output_to_operand_aliasing={{}: (6, {})} | custom-call | flops 603979776 | bytes 2097152 | tf_op jit(solution)/shard_map/attend/pallas_call | solution.py:177
  124.9 3.6 %attend.14._ = bf16[128,64,128]{2,1,0:T(8,128)(2,1)} custom-call(s32[8,19]{1,0:T(8,128)S(1)} %pad_add_fusion.meta, bf16[8,128,8,128]{3,2,1,0:T(8,128)(2,1)S(1)} %stage.1.q, bf16[32,8,8,128]{3,2,1,0:T(8,128)(2,1)} %cut.1.own, bf16[152,8,128]{2,1,0:T(8,128)(2,1)S(1)} %collective-permute-done.15.far_k, ...), custom_call_target="tpu_custom_call", output_to_operand_aliasing={{}: (6, {})} | custom-call | flops 603979776 | bytes 2097152 | tf_op jit(solution)/shard_map/attend/pallas_call | solution.py:177
  128.6 3.5 %attend.15 = bf16[128,64,128]{2,1,0:T(8,128)(2,1)} custom-call(s32[8,19]{1,0:T(8,128)S(1)} %pad_add_fusion.meta, bf16[8,128,8,128]{3,2,1,0:T(8,128)(2,1)S(1)} %stage.1.q, bf16[32,8,8,128]{3,2,1,0:T(8,128)(2,1)} %cut.1.own, bf16[152,8,128]{2,1,0:T(8,128)(2,1)S(1)} %collective-permute-done.8.far_k, ...), custom_call_target="tpu_custom_call", output_to_operand_aliasing={{}: (6, {})} | custom-call | flops 603979776 | bytes 2097152 | tf_op jit(solution)/shard_map/attend/pallas_call | solution.py:177
  (41 shorter events, 0.2 us)
Async XLA Ops:
  0.0 0.9 copy-start.3
  1.0 0.9 copy-start.4
  1.9 16.8 %copy-start.7 = (s32[8,8]{1,0:T(8,128)S(1)}, s32[8,8]{1,0:T(8,128)}, u32[]{:S(2)}) copy-start(s32[8,8]{1,0:T(8,128)} %param.11) | copy-start | bytes 772
  3.0 45.0 %copy-start.5 = (s32[256]{0:T(256)S(1)}, s32[256]{0:T(256)}, u32[]{:S(2)}) copy-start(s32[256]{0:T(256)} %param.12) | copy-start | bytes 3076
  3.0 36.8 %all-to-all-start.1 = ((bf16[256,8,128]{2,1,0:T(8,128)(2,1)}), bf16[256,8,128]{2,1,0:T(8,128)(2,1)S(1)}, u32[]{:S(2)}, u32[]{:S(2)}) async-start(bf16[256,8,128]{2,1,0:T(8,128)(2,1)} %bitcast.10), calls=%async_computation.1 | async-start | bytes 1048576 | tf_op jit(solution)/shard_map/all_to_all | solution.py:288
  19.2 3.0 %collective-permute-start = (s32[1,128]{1,0:T(1,128)S(1)}, s32[1,128]{1,0:T(1,128)S(1)}, u32[]{:S(2)}, u32[]{:S(2)}) collective-permute-start(s32[1,128]{1,0:T(1,128)S(1)} %bitcast.20), channel_id=1, source_target_pairs={{0,8},{8,0},{16,24},{24,16},{32,40},{40,32},{48,56},{56,48},{64,72... | collective-permute-start | bytes 1544 | tf_op jit(solution)/shard_map/ppermute | solution.py:266
  22.3 2.7 %collective-permute-start.1 = (s32[2,128]{1,0:T(2,128)S(1)}, s32[2,128]{1,0:T(2,128)S(1)}, u32[]{:S(2)}, u32[]{:S(2)}) collective-permute-start(s32[2,128]{1,0:T(2,128)S(1)} %pad_add_fusion.3), channel_id=1, source_target_pairs={{0,16},{8,24},{16,0},{24,8},{32,48},{40,56},{48,32},{56,40},{64,80... | collective-permute-start | bytes 3080 | tf_op jit(solution)/shard_map/ppermute | solution.py:266
  25.0 4.3 %collective-permute-start.2 = (s32[4,128]{1,0:T(4,128)S(1)}, s32[4,128]{1,0:T(4,128)S(1)}, u32[]{:S(2)}, u32[]{:S(2)}) collective-permute-start(s32[4,128]{1,0:T(4,128)S(1)} %pad_add_fusion.2), channel_id=1, source_target_pairs={{0,32},{8,40},{16,48},{24,56},{32,0},{40,8},{48,16},{56,24},{64,96... | collective-permute-start | bytes 6152 | tf_op jit(solution)/shard_map/ppermute | solution.py:266
  29.4 2.8 %collective-permute-start.3 = (s32[8,128]{1,0:T(8,128)S(1)}, s32[8,128]{1,0:T(8,128)S(1)}, u32[]{:S(2)}, u32[]{:S(2)}) collective-permute-start(s32[8,128]{1,0:T(8,128)S(1)} %pad_add_fusion.1), channel_id=1, source_target_pairs={{0,64},{8,72},{16,80},{24,88},{32,96},{40,104},{48,112},{56,120},{... | collective-permute-start | bytes 12296 | tf_op jit(solution)/shard_map/ppermute | solution.py:266
  32.2 4.4 %collective-permute-start.4 = (s32[16,128]{1,0:T(8,128)S(1)}, s32[16,128]{1,0:T(8,128)S(1)}, u32[]{:S(2)}, u32[]{:S(2)}) collective-permute-start(s32[16,128]{1,0:T(8,128)S(1)} %concatenate.30), channel_id=1, source_target_pairs={{0,128},{8,136},{16,144},{24,152},{32,160},{40,168},{48,176},{56,1... | collective-permute-start | bytes 24584 | tf_op jit(solution)/shard_map/ppermute | solution.py:266
  39.8 42.0 %copy-start.8 = (s32[8]{0:T(128)S(1)}, s32[8]{0:T(128)}, u32[]{:S(2)}) copy-start(s32[8]{0:T(128)} %constant.77.clone) | copy-start | bytes 100
  41.9 20.1 %all-to-all-start.2 = ((bf16[32,12,8,128]{3,2,1,0:T(8,128)(2,1)}), bf16[32,12,8,128]{3,2,1,0:T(8,128)(2,1)S(1)}, u32[]{:S(2)}, u32[]{:S(2)}) async-start(bf16[32,12,8,128]{3,2,1,0:T(8,128)(2,1)} %pick.1), calls=%async_computation.2 | async-start | bytes 1572864 | tf_op jit(solution)/shard_map/all_to_all | solution.py:290
  62.9 12.2 %collective-permute-start.5 = (bf16[152,8,128]{2,1,0:T(8,128)(2,1)S(1)}, bf16[152,8,128]{2,1,0:T(8,128)(2,1)S(1)}, u32[]{:S(2)}, u32[]{:S(2)}) collective-permute-start(bf16[152,8,128]{2,1,0:T(8,128)(2,1)S(1)} %get-tuple-element.12.far_k), channel_id=1, source_target_pairs={{0,1},{1,2},{2,3},{3,4},{4,5},{5,6},{6,7},{7,0},{8,9},{9,10},{10,1... | collective-permute-start | bytes 933896 | tf_op jit(solution)/shard_map/ppermute | solution.py:308
  64.4 10.7 %collective-permute-start.9 = (bf16[152,8,128]{2,1,0:T(8,128)(2,1)S(1)}, bf16[152,8,128]{2,1,0:T(8,128)(2,1)S(1)}, u32[]{:S(2)}, u32[]{:S(2)}) collective-permute-start(bf16[152,8,128]{2,1,0:T(8,128)(2,1)S(1)} %get-tuple-element.13.far_v), channel_id=1, source_target_pairs={{0,7},{1,0},{2,1},{3,2},{4,3},{5,4},{6,5},{7,6},{8,15},{9,8},{10,9... | collective-permute-start | bytes 933896 | tf_op jit(solution)/shard_map/ppermute | solution.py:309
  67.4 14.4 %collective-permute-start.16 = (bf16[152,8,128]{2,1,0:T(8,128)(2,1)S(1)}, bf16[152,8,128]{2,1,0:T(8,128)(2,1)S(1)}, u32[]{:S(2)}, u32[]{:S(2)}) collective-permute-start(bf16[152,8,128]{2,1,0:T(8,128)(2,1)S(1)} %get-tuple-element.13.far_v), channel_id=1, source_target_pairs={{0,1},{1,2},{2,3},{3,4},{4,5},{5,6},{6,7},{7,0},{8,9},{9,10},{10,1... | collective-permute-start | bytes 933896 | tf_op jit(solution)/shard_map/ppermute | solution.py:313
  67.4 0.7 copy-start.1
  68.1 13.7 %collective-permute-start.13 = (bf16[152,8,128]{2,1,0:T(8,128)(2,1)S(1)}, bf16[152,8,128]{2,1,0:T(8,128)(2,1)}, u32[]{:S(2)}, u32[]{:S(2)}) collective-permute-start(bf16[152,8,128]{2,1,0:T(8,128)(2,1)S(1)} %get-tuple-element.12.far_k), channel_id=1, source_target_pairs={{0,7},{1,0},{2,1},{3,2},{4,3},{5,4},{6,5},{7,6},{8,15},{9,8},{10,9... | collective-permute-start | bytes 933896 | tf_op jit(solution)/shard_map/ppermute | solution.py:314
  75.1 13.4 %collective-permute-start.6 = (bf16[152,8,128]{2,1,0:T(8,128)(2,1)S(1)}, bf16[152,8,128]{2,1,0:T(8,128)(2,1)}, u32[]{:S(2)}, u32[]{:S(2)}) collective-permute-start(bf16[152,8,128]{2,1,0:T(8,128)(2,1)S(1)} %collective-permute-done.5.far_k), channel_id=1, source_target_pairs={{0,1},{1,2},{2,3},{3,4},{4,5},{5,6},{6,7},{7,0},{8,9},{9,10},{10,1... | collective-permute-start | bytes 933896 | tf_op jit(solution)/shard_map/ppermute | solution.py:308
  75.1 13.4 %collective-permute-start.10 = (bf16[152,8,128]{2,1,0:T(8,128)(2,1)S(1)}, bf16[152,8,128]{2,1,0:T(8,128)(2,1)}, u32[]{:S(2)}, u32[]{:S(2)}) collective-permute-start(bf16[152,8,128]{2,1,0:T(8,128)(2,1)S(1)} %collective-permute-done.9.far_v), channel_id=1, source_target_pairs={{0,7},{1,0},{2,1},{3,2},{4,3},{5,4},{6,5},{7,6},{8,15},{9,8},{10,9... | collective-permute-start | bytes 933896 | tf_op jit(solution)/shard_map/ppermute | solution.py:309
  81.8 13.4 %collective-permute-start.17 = (bf16[152,8,128]{2,1,0:T(8,128)(2,1)S(1)}, bf16[152,8,128]{2,1,0:T(8,128)(2,1)}, u32[]{:S(2)}, u32[]{:S(2)}) collective-permute-start(bf16[152,8,128]{2,1,0:T(8,128)(2,1)S(1)} %collective-permute-done.16.far_v), channel_id=1, source_target_pairs={{0,1},{1,2},{2,3},{3,4},{4,5},{5,6},{6,7},{7,0},{8,9},{9,10},{10,1... | collective-permute-start | bytes 933896 | tf_op jit(solution)/shard_map/ppermute | solution.py:313
  81.8 15.7 %collective-permute-start.14 = (bf16[152,8,128]{2,1,0:T(8,128)(2,1)}, bf16[152,8,128]{2,1,0:T(8,128)(2,1)}, u32[]{:S(2)}, u32[]{:S(2)}) collective-permute-start(bf16[152,8,128]{2,1,0:T(8,128)(2,1)} %collective-permute-done.13.far_k), channel_id=1, source_target_pairs={{0,7},{1,0},{2,1},{3,2},{4,3},{5,4},{6,5},{7,6},{8,15},{9,8},{10,9... | collective-permute-start | bytes 933896 | tf_op jit(solution)/shard_map/ppermute | solution.py:314
  88.5 16.4 %collective-permute-start.7 = (bf16[152,8,128]{2,1,0:T(8,128)(2,1)}, bf16[152,8,128]{2,1,0:T(8,128)(2,1)}, u32[]{:S(2)}, u32[]{:S(2)}) collective-permute-start(bf16[152,8,128]{2,1,0:T(8,128)(2,1)} %collective-permute-done.6.far_k), channel_id=1, source_target_pairs={{0,1},{1,2},{2,3},{3,4},{4,5},{5,6},{6,7},{7,0},{8,9},{9,10},{10,1... | collective-permute-start | bytes 933896 | tf_op jit(solution)/shard_map/ppermute | solution.py:308
  88.5 16.3 %collective-permute-start.11 = (bf16[152,8,128]{2,1,0:T(8,128)(2,1)}, bf16[152,8,128]{2,1,0:T(8,128)(2,1)}, u32[]{:S(2)}, u32[]{:S(2)}) collective-permute-start(bf16[152,8,128]{2,1,0:T(8,128)(2,1)} %collective-permute-done.10.far_v), channel_id=1, source_target_pairs={{0,7},{1,0},{2,1},{3,2},{4,3},{5,4},{6,5},{7,6},{8,15},{9,8},{10,9... | collective-permute-start | bytes 933896 | tf_op jit(solution)/shard_map/ppermute | solution.py:309
  95.2 26.0 %collective-permute-start.18 = (bf16[152,8,128]{2,1,0:T(8,128)(2,1)}, bf16[152,8,128]{2,1,0:T(8,128)(2,1)}, u32[]{:S(2)}, u32[]{:S(2)}) collective-permute-start(bf16[152,8,128]{2,1,0:T(8,128)(2,1)} %collective-permute-done.17.far_v), channel_id=1, source_target_pairs={{0,1},{1,2},{2,3},{3,4},{4,5},{5,6},{6,7},{7,0},{8,9},{9,10},{10,1... | collective-permute-start | bytes 933896 | tf_op jit(solution)/shard_map/ppermute | solution.py:313
  95.2 1.6 %copy-start = (bf16[128,64,128]{2,1,0:T(8,128)(2,1)S(1)}, bf16[128,64,128]{2,1,0:T(8,128)(2,1)}, u32[]{:S(2)}) copy-start(bf16[128,64,128]{2,1,0:T(8,128)(2,1)} %q.1) | copy-start | bytes 6291460
  97.5 27.4 %collective-permute-start.15 = (bf16[152,8,128]{2,1,0:T(8,128)(2,1)}, bf16[152,8,128]{2,1,0:T(8,128)(2,1)S(1)}, u32[]{:S(2)}, u32[]{:S(2)}) collective-permute-start(bf16[152,8,128]{2,1,0:T(8,128)(2,1)} %collective-permute-done.14.far_k), channel_id=1, source_target_pairs={{0,7},{1,0},{2,1},{3,2},{4,3},{5,4},{6,5},{7,6},{8,15},{9,8},{10,9... | collective-permute-start | bytes 933896 | tf_op jit(solution)/shard_map/ppermute | solution.py:314
  100.2 1.0 copy-start.2
  101.2 5.2 %copy-start.6 = (bf16[8,2,40,8,128]{4,3,2,1,0:T(8,128)(2,1)S(1)}, bf16[8,2,40,8,128]{4,3,2,1,0:T(8,128)(2,1)}, u32[]{:S(2)}) copy-start(bf16[8,2,40,8,128]{4,3,2,1,0:T(8,128)(2,1)} %get-tuple-element.15.rest) | copy-start | bytes 3932164
  104.8 23.7 %collective-permute-start.12 = (bf16[152,8,128]{2,1,0:T(8,128)(2,1)}, bf16[152,8,128]{2,1,0:T(8,128)(2,1)S(1)}, u32[]{:S(2)}, u32[]{:S(2)}) collective-permute-start(bf16[152,8,128]{2,1,0:T(8,128)(2,1)} %collective-permute-done.11.far_v), channel_id=1, source_target_pairs={{0,7},{1,0},{2,1},{3,2},{4,3},{5,4},{6,5},{7,6},{8,15},{9,8},{10,9... | collective-permute-start | bytes 933896 | tf_op jit(solution)/shard_map/ppermute | solution.py:309
  104.9 23.6 %collective-permute-start.8 = (bf16[152,8,128]{2,1,0:T(8,128)(2,1)}, bf16[152,8,128]{2,1,0:T(8,128)(2,1)S(1)}, u32[]{:S(2)}, u32[]{:S(2)}) collective-permute-start(bf16[152,8,128]{2,1,0:T(8,128)(2,1)} %collective-permute-done.7.far_k), channel_id=1, source_target_pairs={{0,1},{1,2},{2,3},{3,4},{4,5},{5,6},{6,7},{7,0},{8,9},{9,10},{10,1... | collective-permute-start | bytes 933896 | tf_op jit(solution)/shard_map/ppermute | solution.py:308
